TPU v7x, 512 devices: a whole 4x8x8 slice. The times are simulated.
512 devices in a mesh: len: 64 (over y, z), wid: 8 (over x, core).
Axes of the slice: x: 4, y: 8, z: 8, core: 2. Of those that a mesh axis runs over, the one named last changes fastest.
Arguments:
- density: float32 [16, 4096, 4096], P(None, 'len', 'wid'), may hold values from 0.05 to 1.5
- len_band: int32 [2, 16], replicated, may hold values from 0 to 21, as said below
- wid_band: int32 [2, 16], replicated, may hold values from 0 to 127, as said below
- len_taps: float32 [16, 8], replicated, may hold values from 0.25 to 4
- wid_taps: float32 [16, 8], replicated, may hold values from 0.25 to 4
- tile_pairs: int32 [64, 3], replicated, may hold values from -1 to 3, as said below
- agg_kern: float32 [4, 64, 64], replicated, as said below
Outputs:
- updated: float32 [16, 4096, 4096], P(None, 'len', 'wid')
Inputs may be any that keep to these rules, and one draw needn't show every extreme that they name: `len_band`: offset plus count minus one is at most 21 for every batch; counts run from 1 to 8. `wid_band`: offset plus count minus one is at most 127 for every batch; counts run from 1 to 8. `tile_pairs`: -1 marks an absent pair. `agg_kern`: entries are nonnegative.
All inputs are finite; a program needn't handle non-finite values.
Results may differ from a plain program's by a relative error of at most 0.0003.
Values sent between devices are 32-bit elements; how exact they have to be, the bound alone decides.
No kernel may reach another device: no remote copies, remote signals or barrier semaphores. Data moves between devices by JAX's collectives and lax.ppermute only.
A program may use at most 128 MiB of HBM per device.

v0:
```python
import jax
import jax.numpy as jnp
from jax import lax
from jax.sharding import PartitionSpec as P

WBLK = 128


BETA = 0.5
HIGHEST = lax.Precision.HIGHEST


def shifted(value, axis, steps):
    count = lax.axis_size(axis)
    first, last = (max(0, -steps), min(count, count - steps))
    return lax.ppermute(value, axis, [(source, source + steps) for source in range(first, last)])


def band_matrix(band, taps, lead_rows, out_span):
    offsets = band[0]
    counts = band[1]
    tap_range = jnp.arange(taps.shape[1], dtype=jnp.int32)
    weights = jnp.where(tap_range[None, :] < counts[:, None], taps, 0.0)
    scaled = weights / jnp.sum(weights, axis=1, keepdims=True)
    source = jnp.arange(lead_rows + out_span, dtype=jnp.int32)[:, None]
    target = jnp.arange(out_span, dtype=jnp.int32)[None, :]
    distance = (lead_rows + target - source)[None, :, :] - offsets[:, None, None]
    matrix = jnp.zeros(distance.shape, jnp.float32)
    for tap_index in range(taps.shape[1]):
        matrix = matrix + jnp.where(distance == tap_index, scaled[:, tap_index][:, None, None], 0.0)
    return matrix


def width_sweep(extended, matrix):
    batches, rows, columns = extended.shape
    groups = columns // WBLK - 1
    blocked = extended.reshape(batches, rows, groups + 1, WBLK)
    paired = jnp.concatenate([blocked[:, :, :-1], blocked[:, :, 1:]], axis=3)
    moved = jnp.einsum("brni,bij->brnj", paired, matrix, precision=HIGHEST)
    return moved.reshape(batches, rows, groups * WBLK)


def shards(density, len_band, wid_band, len_taps, wid_taps, tile_pairs, agg_kern):
    tile_len = density.shape[1]
    group_width = density.shape[2]
    reach = tile_len // 3
    wid_matrix = band_matrix(wid_band, wid_taps, WBLK, WBLK)
    rim = density[:, tile_len - reach :, :]
    lower_rim = shifted(rim, "len", 1)
    len_matrix = band_matrix(len_band, len_taps, reach, tile_len)
    grown = jnp.einsum(
        "biw,bij->bjw", jnp.concatenate([lower_rim, density], axis=1), len_matrix, precision=HIGHEST
    )
    grown_edge = grown[:, :, group_width - WBLK :]
    lower_grown = shifted(grown_edge, "wid", 1)
    spread = width_sweep(jnp.concatenate([lower_grown, grown], axis=2), wid_matrix)
    lower_one = shifted(spread, "len", 1)
    lower_two = shifted(spread, "len", 2)
    pair_row = lax.dynamic_slice_in_dim(tile_pairs, lax.axis_index("len"), 1, 0)[0]
    kernels = []
    for offset_index in range(3):
        kernel_id = pair_row[offset_index]
        kernels.append(agg_kern[jnp.maximum(kernel_id, 0)] * (kernel_id >= 0).astype(jnp.float32))
    stacked = jnp.concatenate([spread, lower_one, lower_two], axis=1)
    rate = jnp.einsum("blw,lm->bmw", stacked, jnp.concatenate(kernels, axis=0), precision=HIGHEST)
    return spread + BETA * (rate * rate / (1.0 + rate) - spread * rate)


def solution(mesh):
    in_specs = (P(None, "len", "wid"), P(), P(), P(), P(), P(), P())
    out_specs = P(None, "len", "wid")
    return jax.shard_map(shards, mesh=mesh, in_specs=in_specs, out_specs=out_specs, check_vma=False)
```

profile of v0, /device:TPU:98, one launch (start us, length us, event | category | flops | bytes accessed | tf_op | source)
XLA Modules:
  0.0 204.2 jit_solution(13422404167392282019)
XLA Ops:
  0.0 1.4 slice.94
  1.4 0.4 copy.28
  1.9 4.3 %collective-permute-start = (f32[16,21,512]{2,0,1:T(8,128)S(1)}, f32[16,21,512]{2,0,1:T(8,128)S(1)}, u32[]{:S(2)}, u32[]{:S(2)}) collective-permute-start(f32[16,21,512]{2,0,1:T(8,128)S(1)} %copy.28), channel_id=1, source_target_pairs={{0,8},{8,16},{16,24},{24,32},{32,40},{40,48},{48,56},{56,64},{64,7... | collective-permute-start | bytes 2064392 | tf_op jit(solution)/shard_map/ppermute | solution.py:16
  6.4 14.6 %collective-permute-done = f32[16,21,512]{2,0,1:T(8,128)S(1)} collective-permute-done((f32[16,21,512]{2,0,1:T(8,128)S(1)}, f32[16,21,512]{2,0,1:T(8,128)S(1)}, u32[]{:S(2)}, u32[]{:S(2)}) %collective-permute-start) | collective-permute-done | bytes 688160 | tf_op jit(solution)/shard_map/ppermute | solution.py:16
  20.9 0.4 copy.20
  21.3 2.6 %fusion.10 = f32[16,64,512]{2,1,0:T(8,128)S(1)} fusion(f32[16,64,512]{2,1,0:T(8,128)S(1)} %copy-done.1, f32[16,21,512]{2,1,0:T(8,128)S(1)} %copy.20, f32[16]{0:T(128)S(1)} %get-tuple-element.19, f32[16]{0:T(128)S(1)} %get-tuple-element.20, f32[16]{0:T(128)S(1)} %get-tuple-element.21, f32[16]{0:T(128)S(1)} %get-tuple-element.22, ...), kind=kOutput, calls=%fused_computation.18 | convolution fusion | flops 537559040 | bytes 4904768 | tf_op jit(solution)/shard_map/biw,bij->bjw/dot_general | solution.py:51
  24.0 1.9 collective-permute-start.1
  26.0 8.5 %collective-permute-done.1 = f32[16,64,128]{2,1,0:T(8,128)S(1)} collective-permute-done((f32[16,64,128]{2,1,0:T(8,128)S(1)}, f32[16,64,128]{2,1,0:T(8,128)S(1)}, u32[]{:S(2)}, u32[]{:S(2)}) %collective-permute-start.1) | collective-permute-done | bytes 524320 | tf_op jit(solution)/shard_map/ppermute | solution.py:16
  34.5 0.2 pad_maximum_fusion
  34.7 2.2 %reshape.108 = f32[16,64,5,128]{3,2,1,0:T(8,128)} reshape(f32[16,64,640]{2,1,0:T(8,128)S(1)} %pad_maximum_fusion) | data formatting | bytes 5242880 | tf_op jit(solution)/shard_map/reshape | solution.py:37
  36.9 4.6 %fusion.125 = (f32[16,64,4,128]{3,2,1,0:T(4,128)S(1)}, f32[16,64,4,128]{3,2,1,0:T(4,128)S(1)}) fusion(f32[16,64,5,128]{3,2,1,0:T(8,128)} %reshape.108), kind=kLoop, calls=%fused_computation.174 | loop fusion | bytes 8388608 | tf_op jit(solution)/shard_map/slice | solution.py:38
  41.5 0.3 copy.29
  41.8 0.3 copy.30
  42.1 5.8 %fusion.34 = f32[16,4,8,8,128]{4,3,2,1,0:T(8,128)S(1)} fusion(f32[16,64,4,128]{3,1,2,0:T(8,128)S(1)} %copy.30, f32[16,64,4,128]{3,1,2,0:T(8,128)S(1)} %copy.29, f32[16]{0:T(128)S(1)} %get-tuple-element.11, f32[16]{0:T(128)S(1)} %get-tuple-element.12, f32[16]{0:T(128)S(1)} %get-tuple-element.13, f32[16]{0:T(128)S(1)} %get-tuple-element.14, ...), kind=kOutput, calls=%fused_computation.55 | convolution fusion | flops 1624244224 | bytes 6423104 | tf_op jit(solution)/shard_map/brni,bij->brnj/dot_general | solution.py:39
  47.9 0.3 copy.36
  48.2 4.3 %collective-permute-start.2 = (f32[16,64,512]{2,1,0:T(8,128)S(1)}, f32[16,64,512]{2,1,0:T(8,128)}, u32[]{:S(2)}, u32[]{:S(2)}) collective-permute-start(f32[16,64,512]{2,1,0:T(8,128)S(1)} %bitcast.83), channel_id=1, source_target_pairs={{0,8},{8,16},{16,24},{24,32},{32,40},{40,48},{48,56},{56,64},{64,7... | collective-permute-start | bytes 6291464 | tf_op jit(solution)/shard_map/ppermute | solution.py:16
  52.5 8.7 %collective-permute-start.3 = (f32[16,64,512]{2,1,0:T(8,128)S(1)}, f32[16,64,512]{2,1,0:T(8,128)}, u32[]{:S(2)}, u32[]{:S(2)}) collective-permute-start(f32[16,64,512]{2,1,0:T(8,128)S(1)} %bitcast.84), channel_id=1, source_target_pairs={{0,16},{8,24},{16,32},{24,40},{32,48},{40,56},{48,64},{56,72},{64,... | collective-permute-start | bytes 6291464 | tf_op jit(solution)/shard_map/ppermute | solution.py:16
  61.2 0.1 constant_dynamic-slice_fusion.3
  61.3 0.5 fusion.126
  65.4 0.1 copy.33
  65.5 0.1 copy.31
  65.6 37.9 %collective-permute-done.2 = f32[16,64,512]{2,1,0:T(8,128)} collective-permute-done((f32[16,64,512]{2,1,0:T(8,128)S(1)}, f32[16,64,512]{2,1,0:T(8,128)}, u32[]{:S(2)}, u32[]{:S(2)}) %collective-permute-start.2) | collective-permute-done | bytes 2097184 | tf_op jit(solution)/shard_map/ppermute | solution.py:16
  103.6 92.7 %collective-permute-done.3 = f32[16,64,512]{2,1,0:T(8,128)} collective-permute-done((f32[16,64,512]{2,1,0:T(8,128)S(1)}, f32[16,64,512]{2,1,0:T(8,128)}, u32[]{:S(2)}, u32[]{:S(2)}) %collective-permute-start.3) | collective-permute-done | bytes 2097184 | tf_op jit(solution)/shard_map/ppermute | solution.py:16
  196.3 7.9 %fusion.18 = f32[16,64,512]{2,1,0:T(8,128)} fusion(f32[16,64,512]{2,1,0:T(8,128)S(1)} %bitcast.85, f32[16,64,512]{2,1,0:T(8,128)} %collective-permute-done.3, f32[16,64,512]{2,1,0:T(8,128)} %collective-permute-done.2, f32[64,64]{0,1:T(8,128)S(1)} %get-tuple-element.33, f32[64,64]{0,1:T(8,128)S(1)} %get-tuple-element.34, f32[64,64]{0,1:T(8,128)S(1)} %multiply_bitcast_fusion.2), kind=kOutput, calls=%fused_computation.39 | convolution fusion | flops 1214799872 | bytes 8437760 | tf_op jit(solution)/shard_map/blw,lm->bmw/dot_general | solution.py:65
  (31 shorter events, 0.4 us)
Async XLA Ops:
  0.0 61.2 %copy-start = (s32[64,3]{0,1:T(4,128)S(1)}, s32[64,3]{0,1:T(4,128)}, u32[]{:S(2)}) copy-start(s32[64,3]{0,1:T(4,128)} %param.12) | copy-start | bytes 2308
  0.0 21.3 %copy-start.1 = (f32[16,64,512]{2,1,0:T(8,128)S(1)}, f32[16,64,512]{2,1,0:T(8,128)}, u32[]{:S(2)}) copy-start(f32[16,64,512]{2,1,0:T(8,128)} %param.7) | copy-start | bytes 6291460
  0.0 6.1 %copy-start.5 = (s32[2,16]{1,0:T(2,128)S(1)}, s32[2,16]{1,0:T(2,128)}, u32[]{:S(2)}) copy-start(s32[2,16]{1,0:T(2,128)} %param.8) | copy-start | bytes 388
  0.0 6.2 %copy-start.3 = (f32[16,8]{0,1:T(8,128)S(1)}, f32[16,8]{0,1:T(8,128)}, u32[]{:S(2)}) copy-start(f32[16,8]{0,1:T(8,128)} %param.10) | copy-start | bytes 1540
  0.0 6.2 %copy-start.6 = (s32[2,16]{1,0:T(2,128)S(1)}, s32[2,16]{1,0:T(2,128)}, u32[]{:S(2)}) copy-start(s32[2,16]{1,0:T(2,128)} %param.9) | copy-start | bytes 388
  0.0 6.2 %copy-start.4 = (f32[16,8]{0,1:T(8,128)S(1)}, f32[16,8]{0,1:T(8,128)}, u32[]{:S(2)}) copy-start(f32[16,8]{0,1:T(8,128)} %param.11) | copy-start | bytes 1540
  1.9 19.1 %collective-permute-start = (f32[16,21,512]{2,0,1:T(8,128)S(1)}, f32[16,21,512]{2,0,1:T(8,128)S(1)}, u32[]{:S(2)}, u32[]{:S(2)}) collective-permute-start(f32[16,21,512]{2,0,1:T(8,128)S(1)} %copy.28), channel_id=1, source_target_pairs={{0,8},{8,16},{16,24},{24,32},{32,40},{40,48},{48,56},{56,64},{64,7... | collective-permute-start | bytes 2064392 | tf_op jit(solution)/shard_map/ppermute | solution.py:16
  24.0 10.5 %collective-permute-start.1 = (f32[16,64,128]{2,1,0:T(8,128)S(1)}, f32[16,64,128]{2,1,0:T(8,128)S(1)}, u32[]{:S(2)}, u32[]{:S(2)}) collective-permute-start(f32[16,64,128]{2,1,0:T(8,128)S(1)} %slice.111), channel_id=1, source_target_pairs={{0,1},{1,2},{2,3},{3,4},{4,5},{5,6},{6,7},{8,9},{9,10},{10,11},{11... | collective-permute-start | bytes 1572872 | tf_op jit(solution)/shard_map/ppermute | solution.py:16
  47.9 17.4 %copy-start.2 = (f32[4,64,64]{2,1,0:T(8,128)S(1)}, f32[4,64,64]{2,1,0:T(8,128)}, u32[]{:S(2)}) copy-start(f32[4,64,64]{2,1,0:T(8,128)} %param.13) | copy-start | bytes 196612
  48.2 55.4 %collective-permute-start.2 = (f32[16,64,512]{2,1,0:T(8,128)S(1)}, f32[16,64,512]{2,1,0:T(8,128)}, u32[]{:S(2)}, u32[]{:S(2)}) collective-permute-start(f32[16,64,512]{2,1,0:T(8,128)S(1)} %bitcast.83), channel_id=1, source_target_pairs={{0,8},{8,16},{16,24},{24,32},{32,40},{40,48},{48,56},{56,64},{64,7... | collective-permute-start | bytes 6291464 | tf_op jit(solution)/shard_map/ppermute | solution.py:16
  52.5 143.9 %collective-permute-start.3 = (f32[16,64,512]{2,1,0:T(8,128)S(1)}, f32[16,64,512]{2,1,0:T(8,128)}, u32[]{:S(2)}, u32[]{:S(2)}) collective-permute-start(f32[16,64,512]{2,1,0:T(8,128)S(1)} %bitcast.84), channel_id=1, source_target_pairs={{0,16},{8,24},{16,32},{24,40},{32,48},{40,56},{48,64},{56,72},{64,... | collective-permute-start | bytes 6291464 | tf_op jit(solution)/shard_map/ppermute | solution.py:16
where the time goes:
time: 204 us
  waiting for transfers between devices  154 us (75%)
  starting transfers between devices  19.2 us (9%)
  matrix products  16.2 us (8%)
  local copies, waits for them, and re-layouts  10.8 us (5%)
  between operations  3.84 us (2%)
    ppermute x4, waiting for transfers between devices, shifted(): lax.ppermute(value, axis, [(source, source + steps) for source in range(f...  154 us
    ppermute x4, starting transfers between devices, shifted(): lax.ppermute(value, axis, [(source, source + steps) for source in range(f...  19.2 us
    dot_general x1, matrix products, shards(): jnp.einsum('blw,lm->bmw', stacked, jnp.concatenate(kernels, axis=0), prec...  7.87 us
    dot_general x1, matrix products, width_sweep(): moved = jnp.einsum('brni,bij->brnj', paired, matrix, precision=HIGHEST)  5.78 us
    slice x1, local copies, waits for them, and re-layouts, width_sweep(): paired = jnp.concatenate([blocked[:, :, :-1], blocked[:, :, 1:]], axis=3)  4.59 us
  transfers between devices with their start and end apart: 4, of which 4 were waited for; matrix products, arithmetic and copies ran while one was open for 1% of the time, Pallas kernels for 0%

commit v1 on v0

v1 whole, which is shorter than its diff:
```python
import jax
import jax.numpy as jnp
from jax import lax
from jax.sharding import PartitionSpec as P

WBLK = 128
BETA = 0.5
RING = 8
RIM = 24
HIGHEST = lax.Precision.HIGHEST

FORWARD = ((0, 6), (6, 12))
BACKWARD = ((12, 14), (14, 16))


def tap_scale(band, taps):
    tap_range = jnp.arange(taps.shape[1], dtype=jnp.int32)
    weights = jnp.where(tap_range[None, :] < band[1][:, None], taps, 0.0)
    return weights / jnp.sum(weights, axis=1, keepdims=True)


def band_matrix(band, taps, lead_rows, out_span):
    scaled = tap_scale(band, taps)
    source = jnp.arange(lead_rows + out_span, dtype=jnp.int32)[:, None]
    target = jnp.arange(out_span, dtype=jnp.int32)[None, :]
    distance = (lead_rows + target - source)[None, :, :] - band[0][:, None, None]
    matrix = jnp.zeros(distance.shape, jnp.float32)
    for tap_index in range(taps.shape[1]):
        matrix = matrix + jnp.where(distance == tap_index, scaled[:, tap_index][:, None, None], 0.0)
    return matrix


def width_sweep(extended, matrix):
    batches, rows, columns = extended.shape
    groups = columns // WBLK - 1
    blocked = extended.reshape(batches, rows, groups + 1, WBLK)
    paired = jnp.concatenate([blocked[:, :, :-1], blocked[:, :, 1:]], axis=3)
    moved = jnp.einsum("brni,bij->brnj", paired, matrix, precision=HIGHEST)
    return moved.reshape(batches, rows, groups * WBLK)


def shards(density, len_band, wid_band, len_taps, wid_taps, tile_pairs, agg_kern):
    batches, tile_len, group_width = density.shape
    tiles = lax.axis_size("len")
    groups = lax.axis_size("wid")
    me = lax.axis_index("len")

    def spot(tile, step):
        return tile // RING * RING + (tile + step) % RING

    hop = [(t, (t + 1) % tiles) for t in range(tiles)]
    unhop = [(t, (t - 1) % tiles) for t in range(tiles)]
    back_three = [(t, spot(t, -3)) for t in range(tiles)]
    back_five = [(spot(t, -3), (t + 3) % tiles) for t in range(tiles)]

    edge = lax.ppermute(density[:, :, group_width - WBLK :], "wid", [(s, s + 1) for s in range(groups - 1)])
    wid_matrix = band_matrix(wid_band, wid_taps, WBLK, WBLK)
    band = jnp.swapaxes(band_matrix(len_band, len_taps, RIM, tile_len), 1, 2)
    pair_row = lax.dynamic_slice_in_dim(tile_pairs, me, 1, 0)[0]

    def lay(matrix, below):
        left = (2 - below) * tile_len
        return jnp.pad(matrix, ((0, 0), (0, 0), (left, below * tile_len)))

    rate_op = jnp.zeros((batches, tile_len, RIM + 3 * tile_len), jnp.float32)
    for below in range(3):
        kernel_id = pair_row[below]
        kernel = agg_kern[jnp.maximum(kernel_id, 0)] * (kernel_id >= 0).astype(jnp.float32)
        rate_op = rate_op + lay(jnp.einsum("ml,bmi->bli", kernel, band, precision=HIGHEST), below)
    operator = jnp.concatenate([rate_op, lay(band, 0)], axis=1)
    column = jnp.arange(RIM + 3 * tile_len, dtype=jnp.int32)
    tile_of = me - 2 + (column - RIM) // tile_len
    operator = jnp.where((tile_of >= 0)[None, None, :], operator, 0.0)

    swept = []
    stacks = {}
    for part in FORWARD + BACKWARD:
        lo, hi = part
        extended = jnp.concatenate([edge[lo:hi], density[lo:hi]], axis=2)
        stacks[part] = [width_sweep(extended, wid_matrix[lo:hi])]

    for part in FORWARD:
        own = stacks[part][0]
        one = lax.ppermute(own, "len", hop)
        two = lax.ppermute(one, "len", hop)
        rim = lax.ppermute(two[:, tile_len - RIM :], "len", hop)
        stacks[part] = [rim, two, one, own]
    for part in BACKWARD:
        own = stacks[part][0]
        away = lax.ppermute(own, "len", back_three)
        three = lax.ppermute(away, "len", back_five)
        two = lax.ppermute(three, "len", unhop)
        one = lax.ppermute(two, "len", unhop)
        stacks[part] = [three[:, tile_len - RIM :], two, one, own]

    outs = []
    for part in FORWARD + BACKWARD:
        lo, hi = part
        stack = jnp.concatenate(stacks[part], axis=1)
        both = jnp.einsum("bli,biw->blw", operator[lo:hi], stack, precision=HIGHEST)
        rate, spread = both[:, :tile_len], both[:, tile_len:]
        outs.append(spread + BETA * (rate * rate / (1.0 + rate) - spread * rate))
    return jnp.concatenate(outs, axis=0)


def solution(mesh):
    in_specs = (P(None, "len", "wid"), P(), P(), P(), P(), P(), P())
    out_specs = P(None, "len", "wid")
    return jax.shard_map(shards, mesh=mesh, in_specs=in_specs, out_specs=out_specs, check_vma=False)
```

time: 204 us -> 175 us (0.86)
  the two profiles are of different devices: /device:TPU:98 before, /device:TPU:2 now
where the time goes in v1:
time: 175 us; the launch traced here: 174 us
  starting transfers between devices  72.2 us (41%)
  waiting for transfers between devices  51.7 us (30%)
  local copies, waits for them, and re-layouts  19.4 us (11%)
  matrix products  17.7 us (10%)
  other arithmetic  8.36 us (5%)
  between operations  4.35 us (2%)
    ppermute x2, waiting for transfers between devices, shards(): two = lax.ppermute(one, 'len', hop)  20.9 us
    ppermute x2, starting transfers between devices, shards(): two = lax.ppermute(three, 'len', unhop)  18.7 us
    ppermute x2, waiting for transfers between devices, shards(): away = lax.ppermute(own, 'len', back_three)  18.6 us
    ppermute x2, starting transfers between devices, shards(): away = lax.ppermute(own, 'len', back_three)  12.8 us
    ppermute x2, starting transfers between devices, shards(): three = lax.ppermute(away, 'len', back_five)  11.8 us
    ppermute x2, starting transfers between devices, shards(): one = lax.ppermute(two, 'len', unhop)  10.7 us
    dot_general x4, matrix products, shards(): both = jnp.einsum('bli,biw->blw', operator[lo:hi], stack, precision=HIGHEST)  9.36 us
    ppermute x2, starting transfers between devices, shards(): one = lax.ppermute(own, 'len', hop)  8.17 us
  transfers between devices with their start and end apart: 15, of which 8 were waited for; matrix products, arithmetic and copies ran while one was open for 15% of the time, Pallas kernels for 0%

profile of v1, /device:TPU:2, one launch (start us, length us, event | category | flops | bytes accessed | tf_op | source)
XLA Modules:
  0.0 173.8 jit_solution(8138228715649618370)
XLA Ops:
  0.0 2.0 %slice.197 = f32[16,64,128]{2,1,0:T(8,128)} slice(f32[16,64,512]{2,1,0:T(8,128)} %param.7), slice={[0:16], [0:64], [384:512]} | slice | bytes 1048576 | tf_op jit(solution)/shard_map/slice | solution.py:56
  17.8 2.5 %pad_maximum_fusion.1 = (f32[6,64,640]{2,1,0:T(8,128)}, f32[6,64,640]{2,1,0:T(8,128)S(1)}) fusion(f32[6,64,512]{2,1,0:T(8,128)} %get-tuple-element.5, f32[6,64,128]{2,1,0:T(8,128)S(1)} %get-tuple-element.13, f32[6,64,512]{2,1,0:T(8,128)} %get-tuple-element.6, f32[6,64,128]{2,1,0:T(8,128)S(1)} %get-tuple-element.14), kind=kLoop, calls=%fused_computation.53 | loop fusion | flops 491520 | bytes 3932160 | tf_op jit(solution)/shard_map/concatenate | solution.py:79
  20.3 2.5 %reshape.147 = f32[6,64,5,128]{3,2,1,0:T(8,128)} reshape(f32[6,64,640]{2,1,0:T(8,128)} %get-tuple-element.47) | data formatting | bytes 1966080 | tf_op jit(solution)/shard_map/reshape | solution.py:36
  24.0 2.3 %fusion.91 = (f32[6,64,4,128]{3,2,1,0:T(4,128)S(1)}, f32[6,64,4,128]{3,2,1,0:T(4,128)S(1)}) fusion(f32[6,64,5,128]{3,2,1,0:T(8,128)} %reshape.149), kind=kLoop, calls=%fused_computation.161 | loop fusion | bytes 3145728 | tf_op jit(solution)/shard_map/slice | solution.py:37
  28.0 10.9 %collective-permute-start.11 = (f32[2,64,512]{2,1,0:T(8,128)S(1)}, f32[2,64,512]{2,1,0:T(8,128)S(1)}, u32[]{:S(2)}, u32[]{:S(2)}) collective-permute-start(f32[2,64,512]{2,1,0:T(8,128)S(1)} %bitcast.108), channel_id=1, source_target_pairs={{0,40},{8,48},{16,56},{24,0},{32,8},{40,16},{48,24},{56,32},{64,10... | collective-permute-start | bytes 786440 | tf_op jit(solution)/shard_map/ppermute | solution.py:90
  41.3 1.9 %collective-permute-start.7 = (f32[2,64,512]{2,1,0:T(8,128)S(1)}, f32[2,64,512]{2,1,0:T(8,128)}, u32[]{:S(2)}, u32[]{:S(2)}) collective-permute-start(f32[2,64,512]{2,1,0:T(8,128)S(1)} %bitcast.110), channel_id=1, source_target_pairs={{0,40},{8,48},{16,56},{24,0},{32,8},{40,16},{48,24},{56,32},{64,10... | collective-permute-start | bytes 786440 | tf_op jit(solution)/shard_map/ppermute | solution.py:90
  43.2 3.4 %collective-permute-start.4 = (f32[6,64,512]{2,1,0:T(8,128)S(1)}, f32[6,64,512]{2,1,0:T(8,128)}, u32[]{:S(2)}, u32[]{:S(2)}) collective-permute-start(f32[6,64,512]{2,1,0:T(8,128)S(1)} %bitcast.104), channel_id=1, source_target_pairs={{0,8},{8,16},{16,24},{24,32},{32,40},{40,48},{48,56},{56,64},{64,7... | collective-permute-start | bytes 2359304 | tf_op jit(solution)/shard_map/ppermute | solution.py:84
  46.6 3.8 %collective-permute-done.11 = f32[2,64,512]{2,1,0:T(8,128)S(1)} collective-permute-done((f32[2,64,512]{2,1,0:T(8,128)S(1)}, f32[2,64,512]{2,1,0:T(8,128)S(1)}, u32[]{:S(2)}, u32[]{:S(2)}) %collective-permute-start.11) | collective-permute-done | bytes 262176 | tf_op jit(solution)/shard_map/ppermute | solution.py:90
  50.4 9.9 %collective-permute-start.12 = (f32[2,64,512]{2,1,0:T(8,128)S(1)}, f32[2,64,512]{2,1,0:T(8,128)}, u32[]{:S(2)}, u32[]{:S(2)}) collective-permute-start(f32[2,64,512]{2,1,0:T(8,128)S(1)} %collective-permute-done.11), channel_id=1, source_target_pairs={{40,24},{48,32},{56,40},{0,48},{8,56},{16,64},{24,72},{32,80},{104... | collective-permute-start | bytes 786440 | tf_op jit(solution)/shard_map/ppermute | solution.py:91
  62.5 4.8 %collective-permute-start.1 = (f32[6,64,512]{2,1,0:T(8,128)S(1)}, f32[6,64,512]{2,1,0:T(8,128)}, u32[]{:S(2)}, u32[]{:S(2)}) collective-permute-start(f32[6,64,512]{2,1,0:T(8,128)S(1)} %bitcast.106), channel_id=1, source_target_pairs={{0,8},{8,16},{16,24},{24,32},{32,40},{40,48},{48,56},{56,64},{64,7... | collective-permute-start | bytes 2359304 | tf_op jit(solution)/shard_map/ppermute | solution.py:84
  67.3 14.8 %collective-permute-done.7 = f32[2,64,512]{2,1,0:T(8,128)} collective-permute-done((f32[2,64,512]{2,1,0:T(8,128)S(1)}, f32[2,64,512]{2,1,0:T(8,128)}, u32[]{:S(2)}, u32[]{:S(2)}) %collective-permute-start.7) | collective-permute-done | bytes 262176 | tf_op jit(solution)/shard_map/ppermute | solution.py:90
  84.9 9.6 %collective-permute-start.13 = (f32[2,64,512]{2,1,0:T(8,128)}, f32[2,64,512]{2,1,0:T(8,128)}, u32[]{:S(2)}, u32[]{:S(2)}) collective-permute-start(f32[2,64,512]{2,1,0:T(8,128)} %collective-permute-done.12), channel_id=1, source_target_pairs={{0,504},{8,0},{16,8},{24,16},{32,24},{40,32},{48,40},{56,48},{64,5... | collective-permute-start | bytes 786440 | tf_op jit(solution)/shard_map/ppermute | solution.py:92
  97.5 4.6 %collective-permute-done.8 = f32[2,64,512]{2,1,0:T(8,128)} collective-permute-done((f32[2,64,512]{2,1,0:T(8,128)}, f32[2,64,512]{2,1,0:T(8,128)}, u32[]{:S(2)}, u32[]{:S(2)}) %collective-permute-start.8) | collective-permute-done | bytes 262176 | tf_op jit(solution)/shard_map/ppermute | solution.py:91
  102.1 9.0 %collective-permute-start.9 = (f32[2,64,512]{2,1,0:T(8,128)}, f32[2,64,512]{2,1,0:T(8,128)}, u32[]{:S(2)}, u32[]{:S(2)}) collective-permute-start(f32[2,64,512]{2,1,0:T(8,128)} %collective-permute-done.8), channel_id=1, source_target_pairs={{0,504},{8,0},{16,8},{24,16},{32,24},{40,32},{48,40},{56,48},{64,5... | collective-permute-start | bytes 786440 | tf_op jit(solution)/shard_map/ppermute | solution.py:92
  111.2 3.5 %collective-permute-start.14 = (f32[2,64,512]{2,1,0:T(8,128)}, f32[2,64,512]{2,1,0:T(8,128)}, u32[]{:S(2)}, u32[]{:S(2)}) collective-permute-start(f32[2,64,512]{2,1,0:T(8,128)} %collective-permute-done.13), channel_id=1, source_target_pairs={{0,504},{8,0},{16,8},{24,16},{32,24},{40,32},{48,40},{56,48},{64,5... | collective-permute-start | bytes 786440 | tf_op jit(solution)/shard_map/ppermute | solution.py:93
  114.7 2.4 %collective-permute-start.5 = (f32[6,64,512]{2,1,0:T(8,128)}, f32[6,64,512]{2,1,0:T(8,128)}, u32[]{:S(2)}, u32[]{:S(2)}) collective-permute-start(f32[6,64,512]{2,1,0:T(8,128)} %collective-permute-done.4), channel_id=1, source_target_pairs={{0,8},{8,16},{16,24},{24,32},{32,40},{40,48},{48,56},{56,64},{64,7... | collective-permute-start | bytes 2359304 | tf_op jit(solution)/shard_map/ppermute | solution.py:85
  118.7 7.2 %collective-permute-start.10 = (f32[2,64,512]{2,1,0:T(8,128)}, f32[2,64,512]{2,1,0:T(8,128)S(1)}, u32[]{:S(2)}, u32[]{:S(2)}) collective-permute-start(f32[2,64,512]{2,1,0:T(8,128)} %collective-permute-done.9), channel_id=1, source_target_pairs={{0,504},{8,0},{16,8},{24,16},{32,24},{40,32},{48,40},{56,48},{64,5... | collective-permute-start | bytes 786440 | tf_op jit(solution)/shard_map/ppermute | solution.py:93
  133.1 7.5 %collective-permute-done.5 = f32[6,64,512]{2,1,0:T(8,128)} collective-permute-done((f32[6,64,512]{2,1,0:T(8,128)}, f32[6,64,512]{2,1,0:T(8,128)}, u32[]{:S(2)}, u32[]{:S(2)}) %collective-permute-start.5) | collective-permute-done | bytes 786464 | tf_op jit(solution)/shard_map/ppermute | solution.py:85
  143.8 13.3 %collective-permute-done.2 = f32[6,64,512]{2,1,0:T(8,128)S(1)} collective-permute-done((f32[6,64,512]{2,1,0:T(8,128)}, f32[6,64,512]{2,1,0:T(8,128)S(1)}, u32[]{:S(2)}, u32[]{:S(2)}) %collective-permute-start.2) | collective-permute-done | bytes 786464 | tf_op jit(solution)/shard_map/ppermute | solution.py:85
  157.1 1.9 %collective-permute-start.3 = (f32[6,24,512]{2,1,0:T(8,128)S(1)}, f32[6,24,512]{2,1,0:T(8,128)S(1)}, u32[]{:S(2)}, u32[]{:S(2)}) collective-permute-start(f32[6,24,512]{2,1,0:T(8,128)S(1)} %slice.247), channel_id=1, source_target_pairs={{0,8},{8,16},{16,24},{24,32},{32,40},{40,48},{48,56},{56,64},{64,7... | collective-permute-start | bytes 884744 | tf_op jit(solution)/shard_map/ppermute | solution.py:86
  159.1 3.0 %collective-permute-done.6 = f32[6,24,512]{2,1,0:T(8,128)S(1)} collective-permute-done((f32[6,24,512]{2,1,0:T(8,128)S(1)}, f32[6,24,512]{2,1,0:T(8,128)S(1)}, u32[]{:S(2)}, u32[]{:S(2)}) %collective-permute-start.6) | collective-permute-done | bytes 294944 | tf_op jit(solution)/shard_map/ppermute | solution.py:86
  162.1 3.1 %fusion.8 = f32[6,128,512]{2,1,0:T(8,128)S(1)} fusion(f32[6,64,512]{2,1,0:T(8,128)S(1)} %bitcast.105, f32[6,64,512]{2,1,0:T(8,128)} %collective-permute-done.4, f32[6,64,512]{2,1,0:T(8,128)} %collective-permute-done.5, f32[6,24,512]{2,1,0:T(8,128)S(1)} %collective-permute-done.6, f32[16,64,88]{2,1,0:T(8,128)S(1)} %copy-done.7, ...), kind=kOutput, calls=%fused_computation.16 | convolution fusion | flops 1022976000 | bytes 5472472 | tf_op jit(solution)/shard_map/bli,biw->blw/dot_general | solution.py:100
  165.4 3.7 %collective-permute-done.3 = f32[6,24,512]{2,1,0:T(8,128)S(1)} collective-permute-done((f32[6,24,512]{2,1,0:T(8,128)S(1)}, f32[6,24,512]{2,1,0:T(8,128)S(1)}, u32[]{:S(2)}, u32[]{:S(2)}) %collective-permute-start.3) | collective-permute-done | bytes 294944 | tf_op jit(solution)/shard_map/ppermute | solution.py:86
  169.1 2.9 %fusion = f32[6,128,512]{2,1,0:T(8,128)S(1)} fusion(f32[6,64,512]{2,1,0:T(8,128)S(1)} %bitcast.107, f32[6,64,512]{2,1,0:T(8,128)} %collective-permute-done.1, f32[6,64,512]{2,1,0:T(8,128)S(1)} %collective-permute-done.2, f32[6,24,512]{2,1,0:T(8,128)S(1)} %collective-permute-done.3, f32[16,64,88]{2,1,0:T(8,128)S(1)} %copy-done.7, ...), kind=kOutput, calls=%fused_computation.8 | convolution fusion | flops 1022976000 | bytes 5472472 | tf_op jit(solution)/shard_map/bli,biw->blw/dot_general | solution.py:100
  (113 shorter events, 38.9 us)
Async XLA Ops:
  0.0 4.0 %copy-start = (s32[64,3]{0,1:T(4,128)S(1)}, s32[64,3]{0,1:T(4,128)}, u32[]{:S(2)}) copy-start(s32[64,3]{0,1:T(4,128)} %param.12) | copy-start | bytes 2308
  0.0 7.1 %copy-start.2 = (f32[16,64,512]{2,1,0:T(8,128)S(1)}, f32[16,64,512]{2,1,0:T(8,128)}, u32[]{:S(2)}) copy-start(f32[16,64,512]{2,1,0:T(8,128)} %param.7) | copy-start | bytes 6291460
  2.0 12.4 %collective-permute-start = (f32[16,64,128]{2,1,0:T(8,128)}, f32[16,64,128]{2,1,0:T(8,128)S(1)}, u32[]{:S(2)}, u32[]{:S(2)}) collective-permute-start(f32[16,64,128]{2,1,0:T(8,128)} %slice.197), channel_id=1, source_target_pairs={{0,1},{1,2},{2,3},{3,4},{4,5},{5,6},{6,7},{8,9},{9,10},{10,11},{11... | collective-permute-start | bytes 1572872 | tf_op jit(solution)/shard_map/ppermute | solution.py:56
  26.4 12.6 %copy-start.3 = (f32[2,64,4,128]{3,1,2,0:T(8,128)S(1)}, f32[2,64,4,128]{3,1,2,0:T(8,128)}, u32[]{:S(2)}) copy-start(f32[2,64,4,128]{3,1,2,0:T(8,128)} %copy.50) | copy-start | bytes 786436
  28.0 13.2 %copy-start.10 = (f32[2,4,8,8,128]{4,3,1,2,0:T(8,128)}, f32[2,4,8,8,128]{4,3,1,2,0:T(8,128)S(1)}, u32[]{:S(2)}) copy-start(f32[2,4,8,8,128]{4,3,1,2,0:T(8,128)S(1)} %copy.63) | copy-start | bytes 786436
  28.0 22.4 %collective-permute-start.11 = (f32[2,64,512]{2,1,0:T(8,128)S(1)}, f32[2,64,512]{2,1,0:T(8,128)S(1)}, u32[]{:S(2)}, u32[]{:S(2)}) collective-permute-start(f32[2,64,512]{2,1,0:T(8,128)S(1)} %bitcast.108), channel_id=1, source_target_pairs={{0,40},{8,48},{16,56},{24,0},{32,8},{40,16},{48,24},{56,32},{64,10... | collective-permute-start | bytes 786440 | tf_op jit(solution)/shard_map/ppermute | solution.py:90
  39.6 20.7 %copy-start.1 = (f32[6,64,5,128]{3,2,1,0:T(8,128)S(1)}, f32[6,64,5,128]{3,2,1,0:T(8,128)}, u32[]{:S(2)}) copy-start(f32[6,64,5,128]{3,2,1,0:T(8,128)} %reshape.147) | copy-start | bytes 2949124
  41.3 40.7 %collective-permute-start.7 = (f32[2,64,512]{2,1,0:T(8,128)S(1)}, f32[2,64,512]{2,1,0:T(8,128)}, u32[]{:S(2)}, u32[]{:S(2)}) collective-permute-start(f32[2,64,512]{2,1,0:T(8,128)S(1)} %bitcast.110), channel_id=1, source_target_pairs={{0,40},{8,48},{16,56},{24,0},{32,8},{40,16},{48,24},{56,32},{64,10... | collective-permute-start | bytes 786440 | tf_op jit(solution)/shard_map/ppermute | solution.py:90
  43.2 71.4 %collective-permute-start.4 = (f32[6,64,512]{2,1,0:T(8,128)S(1)}, f32[6,64,512]{2,1,0:T(8,128)}, u32[]{:S(2)}, u32[]{:S(2)}) collective-permute-start(f32[6,64,512]{2,1,0:T(8,128)S(1)} %bitcast.104), channel_id=1, source_target_pairs={{0,8},{8,16},{16,24},{24,32},{32,40},{40,48},{48,56},{56,64},{64,7... | collective-permute-start | bytes 2359304 | tf_op jit(solution)/shard_map/ppermute | solution.py:84
  50.4 34.5 %collective-permute-start.12 = (f32[2,64,512]{2,1,0:T(8,128)S(1)}, f32[2,64,512]{2,1,0:T(8,128)}, u32[]{:S(2)}, u32[]{:S(2)}) collective-permute-start(f32[2,64,512]{2,1,0:T(8,128)S(1)} %collective-permute-done.11), channel_id=1, source_target_pairs={{40,24},{48,32},{56,40},{0,48},{8,56},{16,64},{24,72},{32,80},{104... | collective-permute-start | bytes 786440 | tf_op jit(solution)/shard_map/ppermute | solution.py:91
  62.5 65.3 %collective-permute-start.1 = (f32[6,64,512]{2,1,0:T(8,128)S(1)}, f32[6,64,512]{2,1,0:T(8,128)}, u32[]{:S(2)}, u32[]{:S(2)}) collective-permute-start(f32[6,64,512]{2,1,0:T(8,128)S(1)} %bitcast.106), channel_id=1, source_target_pairs={{0,8},{8,16},{16,24},{24,32},{32,40},{40,48},{48,56},{56,64},{64,7... | collective-permute-start | bytes 2359304 | tf_op jit(solution)/shard_map/ppermute | solution.py:84
  82.0 20.1 %collective-permute-start.8 = (f32[2,64,512]{2,1,0:T(8,128)}, f32[2,64,512]{2,1,0:T(8,128)}, u32[]{:S(2)}, u32[]{:S(2)}) collective-permute-start(f32[2,64,512]{2,1,0:T(8,128)} %collective-permute-done.7), channel_id=1, source_target_pairs={{40,24},{48,32},{56,40},{0,48},{8,56},{16,64},{24,72},{32,80},{104... | collective-permute-start | bytes 786440 | tf_op jit(solution)/shard_map/ppermute | solution.py:91
  84.9 26.3 %collective-permute-start.13 = (f32[2,64,512]{2,1,0:T(8,128)}, f32[2,64,512]{2,1,0:T(8,128)}, u32[]{:S(2)}, u32[]{:S(2)}) collective-permute-start(f32[2,64,512]{2,1,0:T(8,128)} %collective-permute-done.12), channel_id=1, source_target_pairs={{0,504},{8,0},{16,8},{24,16},{32,24},{40,32},{48,40},{56,48},{64,5... | collective-permute-start | bytes 786440 | tf_op jit(solution)/shard_map/ppermute | solution.py:92
  96.4 22.0 %copy-start.6 = (f32[16,64,88]{2,1,0:T(8,128)S(1)}, f32[16,64,88]{2,1,0:T(8,128)}, u32[]{:S(2)}) copy-start(f32[16,64,88]{2,1,0:T(8,128)} %convolution_bitcast_fusion) | copy-start | bytes 1081348
  97.5 32.2 %copy-start.11 = (f32[2,4,8,8,128]{4,3,1,2,0:T(8,128)S(1)}, f32[2,4,8,8,128]{4,3,1,2,0:T(8,128)}, u32[]{:S(2)}) copy-start(f32[2,4,8,8,128]{4,3,1,2,0:T(8,128)} %copy-done.10) | copy-start | bytes 786436
  102.1 16.6 %collective-permute-start.9 = (f32[2,64,512]{2,1,0:T(8,128)}, f32[2,64,512]{2,1,0:T(8,128)}, u32[]{:S(2)}, u32[]{:S(2)}) collective-permute-start(f32[2,64,512]{2,1,0:T(8,128)} %collective-permute-done.8), channel_id=1, source_target_pairs={{0,504},{8,0},{16,8},{24,16},{32,24},{40,32},{48,40},{56,48},{64,5... | collective-permute-start | bytes 786440 | tf_op jit(solution)/shard_map/ppermute | solution.py:92
  111.2 18.5 %collective-permute-start.14 = (f32[2,64,512]{2,1,0:T(8,128)}, f32[2,64,512]{2,1,0:T(8,128)}, u32[]{:S(2)}, u32[]{:S(2)}) collective-permute-start(f32[2,64,512]{2,1,0:T(8,128)} %collective-permute-done.13), channel_id=1, source_target_pairs={{0,504},{8,0},{16,8},{24,16},{32,24},{40,32},{48,40},{56,48},{64,5... | collective-permute-start | bytes 786440 | tf_op jit(solution)/shard_map/ppermute | solution.py:93
  114.7 26.0 %collective-permute-start.5 = (f32[6,64,512]{2,1,0:T(8,128)}, f32[6,64,512]{2,1,0:T(8,128)}, u32[]{:S(2)}, u32[]{:S(2)}) collective-permute-start(f32[6,64,512]{2,1,0:T(8,128)} %collective-permute-done.4), channel_id=1, source_target_pairs={{0,8},{8,16},{16,24},{24,32},{32,40},{40,48},{48,56},{56,64},{64,7... | collective-permute-start | bytes 2359304 | tf_op jit(solution)/shard_map/ppermute | solution.py:85
  118.4 11.4 %copy-start.7 = (f32[16,64,88]{2,1,0:T(8,128)S(1)}, f32[16,64,88]{2,1,0:T(8,128)}, u32[]{:S(2)}) copy-start(f32[16,64,88]{2,1,0:T(8,128)} %select_add_fusion.1) | copy-start | bytes 1081348
  118.7 12.8 %copy-start.13 = (f32[2,4,8,8,128]{4,3,1,2,0:T(8,128)S(1)}, f32[2,4,8,8,128]{4,3,1,2,0:T(8,128)}, u32[]{:S(2)}) copy-start(f32[2,4,8,8,128]{4,3,1,2,0:T(8,128)} %copy-done.12) | copy-start | bytes 786436
  118.7 12.7 %collective-permute-start.10 = (f32[2,64,512]{2,1,0:T(8,128)}, f32[2,64,512]{2,1,0:T(8,128)S(1)}, u32[]{:S(2)}, u32[]{:S(2)}) collective-permute-start(f32[2,64,512]{2,1,0:T(8,128)} %collective-permute-done.9), channel_id=1, source_target_pairs={{0,504},{8,0},{16,8},{24,16},{32,24},{40,32},{48,40},{56,48},{64,5... | collective-permute-start | bytes 786440 | tf_op jit(solution)/shard_map/ppermute | solution.py:93
  127.8 29.3 %collective-permute-start.2 = (f32[6,64,512]{2,1,0:T(8,128)}, f32[6,64,512]{2,1,0:T(8,128)S(1)}, u32[]{:S(2)}, u32[]{:S(2)}) collective-permute-start(f32[6,64,512]{2,1,0:T(8,128)} %collective-permute-done.1), channel_id=1, source_target_pairs={{0,8},{8,16},{16,24},{24,32},{32,40},{40,48},{48,56},{56,64},{64,7... | collective-permute-start | bytes 2359304 | tf_op jit(solution)/shard_map/ppermute | solution.py:85
  141.7 20.4 %collective-permute-start.6 = (f32[6,24,512]{2,1,0:T(8,128)S(1)}, f32[6,24,512]{2,1,0:T(8,128)S(1)}, u32[]{:S(2)}, u32[]{:S(2)}) collective-permute-start(f32[6,24,512]{2,1,0:T(8,128)S(1)} %slice.254), channel_id=1, source_target_pairs={{0,8},{8,16},{16,24},{24,32},{32,40},{40,48},{48,56},{56,64},{64,7... | collective-permute-start | bytes 884744 | tf_op jit(solution)/shard_map/ppermute | solution.py:86
  157.1 11.9 %collective-permute-start.3 = (f32[6,24,512]{2,1,0:T(8,128)S(1)}, f32[6,24,512]{2,1,0:T(8,128)S(1)}, u32[]{:S(2)}, u32[]{:S(2)}) collective-permute-start(f32[6,24,512]{2,1,0:T(8,128)S(1)} %slice.247), channel_id=1, source_target_pairs={{0,8},{8,16},{16,24},{24,32},{32,40},{40,48},{48,56},{56,64},{64,7... | collective-permute-start | bytes 884744 | tf_op jit(solution)/shard_map/ppermute | solution.py:86
  (10 other events, 22.6 us)

commit v2 on v1

v2 whole, which is shorter than its diff:
```python
import functools

import jax
import jax.numpy as jnp
from jax import lax
from jax.experimental import pallas as pl
from jax.experimental.pallas import tpu as pltpu
from jax.sharding import PartitionSpec as P

WBLK = 128
BETA = 0.5
RING = 8
RIM = 24
HIGHEST = lax.Precision.HIGHEST

EARLY = (0, 7)
LATE = (7, 13)
BACK = (13, 16)


def tap_scale(band, taps):
    tap_range = jnp.arange(taps.shape[1], dtype=jnp.int32)
    weights = jnp.where(tap_range[None, :] < band[1][:, None], taps, 0.0)
    return weights / jnp.sum(weights, axis=1, keepdims=True)


def band_matrix(band, taps, lead_rows, out_span):
    scaled = tap_scale(band, taps)
    source = jnp.arange(lead_rows + out_span, dtype=jnp.int32)[:, None]
    target = jnp.arange(out_span, dtype=jnp.int32)[None, :]
    distance = (lead_rows + target - source)[None, :, :] - band[0][:, None, None]
    matrix = jnp.zeros(distance.shape, jnp.float32)
    for tap_index in range(taps.shape[1]):
        matrix = matrix + jnp.where(distance == tap_index, scaled[:, tap_index][:, None, None], 0.0)
    return matrix


def sweep_kernel(first, taps, offset_ref, scale_ref, field_ref, edge_ref, out_ref):
    batch = pl.program_id(0) + first
    offset = offset_ref[batch]
    rows = field_ref.shape[1]
    groups = field_ref.shape[2] // WBLK
    lane = lax.broadcasted_iota(jnp.int32, (rows, WBLK), 1)
    turned = [pltpu.roll(edge_ref[0], offset, 1)]
    for group in range(groups):
        turned.append(pltpu.roll(field_ref[0, :, group * WBLK : (group + 1) * WBLK], offset, 1))
    sums = [None] * groups
    for tap in range(taps):
        if tap:
            turned = [pltpu.roll(piece, 1, 1) for piece in turned]
        scale = scale_ref[batch, tap]
        inside = lane >= offset + tap
        for group in range(groups):
            term = scale * jnp.where(inside, turned[group + 1], turned[group])
            sums[group] = term if tap == 0 else sums[group] + term
    for group in range(groups):
        out_ref[0, :, group * WBLK : (group + 1) * WBLK] = sums[group]


def sweep(field, edge, offsets, scales, part, field_first, edge_first):
    lo, hi = part
    _, rows, width = field.shape
    count = hi - lo
    taps = scales.shape[1]
    return pl.pallas_call(
        functools.partial(sweep_kernel, lo, taps),
        grid_spec=pltpu.PrefetchScalarGridSpec(
            num_scalar_prefetch=2,
            grid=(count,),
            in_specs=[
                pl.BlockSpec((1, rows, width), lambda i, o, s: (i + field_first, 0, 0)),
                pl.BlockSpec((1, rows, WBLK), lambda i, o, s: (i + edge_first, 0, 0)),
            ],
            out_specs=pl.BlockSpec((1, rows, width), lambda i, o, s: (i, 0, 0)),
        ),
        out_shape=jax.ShapeDtypeStruct((count, rows, width), jnp.float32),
        cost_estimate=pl.CostEstimate(
            flops=3 * taps * count * rows * width, bytes_accessed=9 * count * rows * width, transcendentals=0
        ),
        name="sweep",
    )(offsets, scales, field, edge)


def split(value):
    high = value.astype(jnp.bfloat16)
    return high, (value - high.astype(jnp.float32)).astype(jnp.bfloat16)


def finish_kernel(op_ref, own_ref, one_ref, two_ref, rim_ref, *rest):
    out_ref, high_ref, low_ref = rest[-3:]
    rows = own_ref.shape[1]
    at = 0
    for ref in (own_ref, one_ref, two_ref, rim_ref):
        high, low = split(ref[0])
        high_ref[at : at + ref.shape[1]] = high
        low_ref[at : at + ref.shape[1]] = low
        at += ref.shape[1]
    op_high, op_low = split(op_ref[0])
    dot = functools.partial(jnp.dot, preferred_element_type=jnp.float32)
    both = dot(op_high, low_ref[...]) + dot(op_low, high_ref[...]) + dot(op_high, high_ref[...])
    rate, spread = both[:rows], both[rows:]
    out_ref[0] = spread + BETA * (rate * rate / (1.0 + rate) - spread * rate)


def finish(operator, own, one, two, rim, part, total, before):
    lo, hi = part
    count, rows, width = own.shape
    depth = operator.shape[2]
    here = lambda i: (i, 0, 0)
    in_specs = [
        pl.BlockSpec((1, operator.shape[1], depth), lambda i: (i + lo, 0, 0)),
        pl.BlockSpec((1, rows, width), here),
        pl.BlockSpec((1, rows, width), here),
        pl.BlockSpec((1, rows, width), here),
        pl.BlockSpec((1, RIM, width), here),
    ]
    operands = [operator, own, one, two, rim]
    aliases = {}
    if before is not None:
        in_specs.append(pl.BlockSpec(memory_space=pl.ANY))
        operands.append(before)
        aliases = {5: 0}
    return pl.pallas_call(
        finish_kernel,
        grid=(count,),
        in_specs=in_specs,
        out_specs=pl.BlockSpec((1, rows, width), lambda i: (i + lo, 0, 0)),
        out_shape=jax.ShapeDtypeStruct((total, rows, width), jnp.float32),
        scratch_shapes=[pltpu.VMEM((depth, width), jnp.bfloat16)] * 2,
        input_output_aliases=aliases,
        cost_estimate=pl.CostEstimate(
            flops=6 * count * 2 * rows * depth * width, bytes_accessed=20 * count * rows * width, transcendentals=0
        ),
        name="finish",
    )(*operands)


def after(value, *earlier):
    return lax.optimization_barrier((value,) + earlier)[0]


def shards(density, len_band, wid_band, len_taps, wid_taps, tile_pairs, agg_kern):
    batches, tile_len, group_width = density.shape
    tiles = lax.axis_size("len")
    groups = lax.axis_size("wid")
    me = lax.axis_index("len")

    def spot(tile, step):
        return tile // RING * RING + (tile + step) % RING

    hop = functools.partial(lax.ppermute, axis_name="len", perm=[(t, (t + 1) % tiles) for t in range(tiles)])
    unhop = functools.partial(lax.ppermute, axis_name="len", perm=[(t, (t - 1) % tiles) for t in range(tiles)])
    back_three = functools.partial(lax.ppermute, axis_name="len", perm=[(t, spot(t, -3)) for t in range(tiles)])
    back_five = functools.partial(
        lax.ppermute, axis_name="len", perm=[(spot(t, -3), (t + 3) % tiles) for t in range(tiles)]
    )
    side = functools.partial(lax.ppermute, axis_name="wid", perm=[(s, s + 1) for s in range(groups - 1)])

    early_one_raw = hop(density[EARLY[0] : EARLY[1]])
    edge = side(density[:, :, group_width - WBLK :])

    offsets = wid_band[0]
    scales = tap_scale(wid_band, wid_taps)

    back_own = sweep(density, edge, offsets, scales, BACK, BACK[0], BACK[0])
    back_away = back_three(back_own)
    late_own = sweep(density, after(edge, back_own), offsets, scales, LATE, LATE[0], LATE[0])
    late_one = hop(late_own)
    early_one_raw = after(early_one_raw, late_own)

    band = jnp.swapaxes(band_matrix(len_band, len_taps, RIM, tile_len), 1, 2)
    pair_row = lax.dynamic_slice_in_dim(tile_pairs, me, 1, 0)[0]

    def lay(matrix, below):
        low, body = matrix[:, :, :RIM], matrix[:, :, RIM:]
        zero = jnp.zeros_like(body)
        columns = [zero, zero, zero, jnp.zeros_like(low)]
        columns[below] = body
        if below < 2:
            columns[below + 1] = jnp.pad(low, ((0, 0), (0, 0), (tile_len - RIM, 0)))
        else:
            columns[3] = low
        return jnp.concatenate(columns, axis=2)

    rate_op = 0.0
    for below in range(3):
        kernel_id = pair_row[below]
        kernel = agg_kern[jnp.maximum(kernel_id, 0)] * (kernel_id >= 0).astype(jnp.float32)
        rate_op = rate_op + lay(jnp.einsum("ml,bmi->bli", kernel, band, precision=HIGHEST), below)
    operator = jnp.concatenate([rate_op, lay(band, 0)], axis=1)
    column = jnp.arange(RIM + 3 * tile_len, dtype=jnp.int32)
    operator = jnp.where((me >= column // tile_len)[None, None, :], operator, 0.0)

    early_edge = side(early_one_raw[:, :, group_width - WBLK :])
    early_own = sweep(density, edge, offsets, scales, EARLY, EARLY[0], EARLY[0])
    early_one = sweep(early_one_raw, early_edge, offsets, scales, EARLY, 0, 0)
    early_two = hop(early_one)
    late_two = hop(late_one)
    back_three_below = back_five(after(back_away, late_one))
    early_rim = hop(after(early_two[:, tile_len - RIM :], back_away))
    back_two = unhop(after(back_three_below, early_two))
    late_rim = hop(after(late_two[:, tile_len - RIM :], back_three_below))
    back_one = unhop(after(back_two, early_two))

    out = finish(operator, early_own, early_one, early_two, early_rim, EARLY, batches, None)
    out = finish(
        operator, back_own, back_one, back_two, back_three_below[:, tile_len - RIM :], BACK, batches, out
    )
    return finish(operator, late_own, late_one, late_two, late_rim, LATE, batches, out)


def solution(mesh):
    in_specs = (P(None, "len", "wid"), P(), P(), P(), P(), P(), P())
    out_specs = P(None, "len", "wid")
    return jax.shard_map(shards, mesh=mesh, in_specs=in_specs, out_specs=out_specs, check_vma=False)
```

time: 175 us -> 149 us (0.85)
  Pallas kernels: 0 us -> 42.1 us
  starting transfers between devices: 72.2 us -> 41.4 us
  matrix products: 17.7 us -> 3.31 us
  waiting for transfers between devices: 51.7 us -> 41.2 us
  local copies, waits for them, and re-layouts: 19.4 us -> 11.4 us
  other arithmetic: 8.36 us -> 4.35 us
    pallas_call x0 -> x7, Pallas kernels: none -> 42.1 us  [the longest x4 26.6 us: sweep(): pl.pallas_call(functools.partial(sweep_kernel, lo, taps), grid_spec=pltpu...]
    ppermute x15 -> x12, starting transfers between devices: 72.2 us -> 41.4 us  [the longest x1 7.7 us: shards(): back_one = unhop(after(back_two, early_two))]
    dot_general x8 -> x0, matrix products: 13.6 us -> none  [the longest x4 9.36 us: shards(): both = jnp.einsum('bli,biw->blw', operator[lo:hi], stack, precision=HIGHEST)]
    ppermute x15 -> x12, waiting for transfers between devices: 51.7 us -> 41.2 us  [the longest x1 15 us: shards(): back_away = back_three(back_own)]
    slice x13 -> x11, local copies, waits for them, and re-layouts: 10.2 us -> 5.15 us  [the longest x1 1.57 us: shards(): back_three_below[:, tile_len - RIM:]]
    concatenate x3 -> x0, other arithmetic: 4.09 us -> none  [the longest x2 2.5 us: shards(): extended = jnp.concatenate([edge[lo:hi], density[lo:hi]], axis=2)]
    reshape x8 -> x0, local copies, waits for them, and re-layouts: 4.05 us -> none  [the longest x4 3.84 us: width_sweep(): blocked = extended.reshape(batches, rows, groups + 1, WBLK)]
    add x2 -> x1, other arithmetic: 3.15 us -> 0.49 us  [band_matrix(): matrix + jnp.where(distance == tap_index, scaled[:, tap_index][:, None, N...]
  transfers between devices with their start and end apart: 15 -> 12, of which waited for: 8 -> 5; matrix products, arithmetic and copies ran while one was open for 15% -> 9% of each run, Pallas kernels for 0% -> 25%
where the time goes in v2:
time: 149 us; the launch traced here: 148 us
  Pallas kernels  42.1 us (28%)
  starting transfers between devices  41.4 us (28%)
  waiting for transfers between devices  41.2 us (28%)
  local copies, waits for them, and re-layouts  11.4 us (8%)
  other arithmetic  4.35 us (3%)
  between operations  4.09 us (3%)
  matrix products  3.31 us (2%)
    pallas_call x4, Pallas kernels, sweep(): pl.pallas_call(functools.partial(sweep_kernel, lo, taps), grid_spec=pltpu...  26.6 us
    pallas_call x3, Pallas kernels, finish(): pl.pallas_call(finish_kernel, grid=(count,), in_specs=in_specs, out_specs...  15.5 us
    ppermute x1, waiting for transfers between devices, shards(): back_away = back_three(back_own)  15 us
    ppermute x1, waiting for transfers between devices, shards(): back_three_below = back_five(after(back_away, late_one))  13.5 us
    ppermute x1, waiting for transfers between devices, shards(): early_one_raw = hop(density[EARLY[0]:EARLY[1]])  8.71 us
    ppermute x1, starting transfers between devices, shards(): back_one = unhop(after(back_two, early_two))  7.7 us
    ppermute x1, starting transfers between devices, shards(): back_two = unhop(after(back_three_below, early_two))  7.15 us
    unnamed x39, local copies, waits for them, and re-layouts  5 us
  transfers between devices with their start and end apart: 12, of which 5 were waited for; matrix products, arithmetic and copies ran while one was open for 9% of the time, Pallas kernels for 25%

profile of v2, /device:TPU:2, one launch (start us, length us, event | category | flops | bytes accessed | tf_op | source)
XLA Modules:
  0.0 147.9 jit_solution(4991305805555803281)
XLA Ops:
  1.2 1.9 %collective-permute-start = (f32[16,64,128]{2,1,0:T(8,128)S(1)}, f32[16,64,128]{2,1,0:T(8,128)S(1)}, u32[]{:S(2)}, u32[]{:S(2)}) collective-permute-start(f32[16,64,128]{2,1,0:T(8,128)S(1)} %slice.113), channel_id=1, source_target_pairs={{0,1},{1,2},{2,3},{3,4},{4,5},{5,6},{6,7},{8,9},{9,10},{10,11},{11... | collective-permute-start | bytes 1572872 | tf_op jit(solution)/shard_map/ppermute | solution.py:160
  4.4 4.3 %collective-permute-start.6 = (f32[7,64,512]{2,1,0:T(8,128)S(1)}, f32[7,64,512]{2,1,0:T(8,128)S(1)}, u32[]{:S(2)}, u32[]{:S(2)}) collective-permute-start(f32[7,64,512]{2,1,0:T(8,128)S(1)} %slice.115), channel_id=1, source_target_pairs={{0,8},{8,16},{16,24},{24,32},{32,40},{40,48},{48,56},{56,64},{64,7... | collective-permute-start | bytes 2752520 | tf_op jit(solution)/shard_map/ppermute | solution.py:159
  14.2 4.5 %sweep.4.own_ref = f32[3,64,512]{2,1,0:T(8,128)} custom-call(s32[16]{0:T(128)} %get-tuple-element.34.offset_ref, f32[16,8]{1,0:T(8,128)} %fusion.22.scale_ref, f32[16,64,512]{2,1,0:T(8,128)} %field_ref.5, f32[16,64,128]{2,1,0:T(8,128)} %copy-done.1), custom_call_target="tpu_custom_call" | custom-call | flops 2359296 | bytes 884736 | tf_op jit(solution)/shard_map/sweep/pallas_call | solution.py:65
  18.7 6.9 %sweep.5.own_ref = f32[6,64,512]{2,1,0:T(8,128)} custom-call(s32[16]{0:T(128)} %get-tuple-element.34.offset_ref, f32[16,8]{1,0:T(8,128)} %fusion.22.scale_ref, f32[16,64,512]{2,1,0:T(8,128)} %field_ref.5, f32[16,64,128]{2,1,0:T(8,128)} %copy-done.1), custom_call_target="tpu_custom_call" | custom-call | flops 4718592 | bytes 1769472 | tf_op jit(solution)/shard_map/sweep/pallas_call | solution.py:65
  25.6 4.3 %collective-permute-start.1 = (f32[6,64,512]{2,1,0:T(8,128)}, f32[6,64,512]{2,1,0:T(8,128)}, u32[]{:S(2)}, u32[]{:S(2)}) collective-permute-start(f32[6,64,512]{2,1,0:T(8,128)} %sweep.5.own_ref), channel_id=1, source_target_pairs={{0,8},{8,16},{16,24},{24,32},{32,40},{40,48},{48,56},{56,64},{64,7... | collective-permute-start | bytes 2359304 | tf_op jit(solution)/shard_map/ppermute | solution.py:168
  29.8 8.7 %collective-permute-done.6.field_ref = f32[7,64,512]{2,1,0:T(8,128)S(1)} collective-permute-done((f32[7,64,512]{2,1,0:T(8,128)S(1)}, f32[7,64,512]{2,1,0:T(8,128)S(1)}, u32[]{:S(2)}, u32[]{:S(2)}) %collective-permute-start.6) | collective-permute-done | bytes 917536 | tf_op jit(solution)/shard_map/ppermute | solution.py:159
  38.6 2.6 %collective-permute-start.7 = (f32[7,64,128]{2,1,0:T(8,128)S(1)}, f32[7,64,128]{2,1,0:T(8,128)S(1)}, u32[]{:S(2)}, u32[]{:S(2)}) collective-permute-start(f32[7,64,128]{2,1,0:T(8,128)S(1)} %slice.116), channel_id=1, source_target_pairs={{0,1},{1,2},{2,3},{3,4},{4,5},{5,6},{6,7},{8,9},{9,10},{10,11},{11... | collective-permute-start | bytes 688136 | tf_op jit(solution)/shard_map/ppermute | solution.py:194
  43.2 1.9 %collective-permute-start.3 = (f32[3,64,512]{2,1,0:T(8,128)S(1)}, f32[3,64,512]{2,1,0:T(8,128)}, u32[]{:S(2)}, u32[]{:S(2)}) collective-permute-start(f32[3,64,512]{2,1,0:T(8,128)S(1)} %copy-done.3), channel_id=1, source_target_pairs={{0,40},{8,48},{16,56},{24,0},{32,8},{40,16},{48,24},{56,32},{64,10... | collective-permute-start | bytes 1179656 | tf_op jit(solution)/shard_map/ppermute | solution.py:166
  46.6 7.6 %sweep.6.one_ref = f32[7,64,512]{2,1,0:T(8,128)} custom-call(s32[16]{0:T(128)} %get-tuple-element.34.offset_ref, f32[16,8]{1,0:T(8,128)} %fusion.22.scale_ref, f32[7,64,512]{2,1,0:T(8,128)} %copy-done.5, f32[7,64,128]{2,1,0:T(8,128)} %copy-done.10), custom_call_target="tpu_custom_call" | custom-call | flops 5505024 | bytes 2064384 | tf_op jit(solution)/shard_map/sweep/pallas_call | solution.py:65
  54.2 1.9 %collective-permute-start.8 = (f32[7,64,512]{2,1,0:T(8,128)}, f32[7,64,512]{2,1,0:T(8,128)S(1)}, u32[]{:S(2)}, u32[]{:S(2)}) collective-permute-start(f32[7,64,512]{2,1,0:T(8,128)} %sweep.6.one_ref), channel_id=1, source_target_pairs={{0,8},{8,16},{16,24},{24,32},{32,40},{40,48},{48,56},{56,64},{64,7... | collective-permute-start | bytes 2752520 | tf_op jit(solution)/shard_map/ppermute | solution.py:197
  58.9 15.0 %collective-permute-done.3 = f32[3,64,512]{2,1,0:T(8,128)} collective-permute-done((f32[3,64,512]{2,1,0:T(8,128)S(1)}, f32[3,64,512]{2,1,0:T(8,128)}, u32[]{:S(2)}, u32[]{:S(2)}) %collective-permute-start.3) | collective-permute-done | bytes 393248 | tf_op jit(solution)/shard_map/ppermute | solution.py:166
  73.9 1.9 %collective-permute-start.4 = (f32[3,64,512]{2,1,0:T(8,128)}, f32[3,64,512]{2,1,0:T(8,128)S(1)}, u32[]{:S(2)}, u32[]{:S(2)}) collective-permute-start(f32[3,64,512]{2,1,0:T(8,128)} %collective-permute-done.3), channel_id=1, source_target_pairs={{40,24},{48,32},{56,40},{0,48},{8,56},{16,64},{24,72},{32,80},{104... | collective-permute-start | bytes 1179656 | tf_op jit(solution)/shard_map/ppermute | solution.py:199
  75.8 3.9 %collective-permute-start.2 = (f32[6,64,512]{2,1,0:T(8,128)}, f32[6,64,512]{2,1,0:T(8,128)S(1)}, u32[]{:S(2)}, u32[]{:S(2)}) collective-permute-start(f32[6,64,512]{2,1,0:T(8,128)} %collective-permute-done.1.one_ref), channel_id=1, source_target_pairs={{0,8},{8,16},{16,24},{24,32},{32,40},{40,48},{48,56},{56,64},{64,7... | collective-permute-start | bytes 2359304 | tf_op jit(solution)/shard_map/ppermute | solution.py:198
  81.7 13.5 %collective-permute-done.4 = f32[3,64,512]{2,1,0:T(8,128)S(1)} collective-permute-done((f32[3,64,512]{2,1,0:T(8,128)}, f32[3,64,512]{2,1,0:T(8,128)S(1)}, u32[]{:S(2)}, u32[]{:S(2)}) %collective-permute-start.4) | collective-permute-done | bytes 393248 | tf_op jit(solution)/shard_map/ppermute | solution.py:199
  95.2 7.2 %collective-permute-start.9 = (f32[3,64,512]{2,1,0:T(8,128)S(1)}, f32[3,64,512]{2,1,0:T(8,128)S(1)}, u32[]{:S(2)}, u32[]{:S(2)}) collective-permute-start(f32[3,64,512]{2,1,0:T(8,128)S(1)} %collective-permute-done.4), channel_id=1, source_target_pairs={{0,504},{8,0},{16,8},{24,16},{32,24},{40,32},{48,40},{56,48},{64,5... | collective-permute-start | bytes 1179656 | tf_op jit(solution)/shard_map/ppermute | solution.py:201
  103.5 1.9 %collective-permute-start.11 = (f32[7,24,512]{2,1,0:T(8,128)S(1)}, f32[7,24,512]{2,1,0:T(8,128)S(1)}, u32[]{:S(2)}, u32[]{:S(2)}) collective-permute-start(f32[7,24,512]{2,1,0:T(8,128)S(1)} %slice.137), channel_id=1, source_target_pairs={{0,8},{8,16},{16,24},{24,32},{32,40},{40,48},{48,56},{56,64},{64,7... | collective-permute-start | bytes 1032200 | tf_op jit(solution)/shard_map/ppermute | solution.py:200
  106.3 1.9 %collective-permute-start.5 = (f32[6,24,512]{2,1,0:T(8,128)S(1)}, f32[6,24,512]{2,1,0:T(8,128)S(1)}, u32[]{:S(2)}, u32[]{:S(2)}) collective-permute-start(f32[6,24,512]{2,1,0:T(8,128)S(1)} %slice.135), channel_id=1, source_target_pairs={{0,8},{8,16},{16,24},{24,32},{32,40},{40,48},{48,56},{56,64},{64,7... | collective-permute-start | bytes 884744 | tf_op jit(solution)/shard_map/ppermute | solution.py:202
  108.3 3.3 %collective-permute-done.9.two_ref = f32[3,64,512]{2,1,0:T(8,128)S(1)} collective-permute-done((f32[3,64,512]{2,1,0:T(8,128)S(1)}, f32[3,64,512]{2,1,0:T(8,128)S(1)}, u32[]{:S(2)}, u32[]{:S(2)}) %collective-permute-start.9) | collective-permute-done | bytes 393248 | tf_op jit(solution)/shard_map/ppermute | solution.py:201
  111.5 7.7 %collective-permute-start.10 = (f32[3,64,512]{2,1,0:T(8,128)S(1)}, f32[3,64,512]{2,1,0:T(8,128)S(1)}, u32[]{:S(2)}, u32[]{:S(2)}) collective-permute-start(f32[3,64,512]{2,1,0:T(8,128)S(1)} %collective-permute-done.9.two_ref), channel_id=1, source_target_pairs={{0,504},{8,0},{16,8},{24,16},{32,24},{40,32},{48,40},{56,48},{64,5... | collective-permute-start | bytes 1179656 | tf_op jit(solution)/shard_map/ppermute | solution.py:203
  119.2 1.8 %fusion.3.op_ref = f32[16,128,216]{2,1,0:T(8,128)} fusion(f32[16,64,24]{2,1,0:T(8,128)S(1)} %bitcast.36, f32[16,64,24]{2,1,0:T(8,128)S(1)} %broadcast.95, f32[16,64,64]{2,1,0:T(8,128)S(1)} %broadcast.94, f32[16,64,64]{2,1,0:T(8,128)S(1)} %slice.133, f32[16,64,216]{2,1,0:T(8,128)S(1)} %fusion.7, pred[216]{0:T(512)(128)(4,1)S(1)} %fusion.26), kind=kLoop, calls=%fused_computation.14 | loop fusion | flops 5308416 | bytes 3375320 | tf_op jit(solution)/shard_map/jit(_where)/select_n | solution.py:192
  121.0 7.6 %sweep.7.own_ref = f32[7,64,512]{2,1,0:T(8,128)} custom-call(s32[16]{0:T(128)} %get-tuple-element.34.offset_ref, f32[16,8]{1,0:T(8,128)} %fusion.22.scale_ref, f32[16,64,512]{2,1,0:T(8,128)} %field_ref.5, f32[16,64,128]{2,1,0:T(8,128)} %copy-done.1), custom_call_target="tpu_custom_call" | custom-call | flops 5505024 | bytes 2064384 | tf_op jit(solution)/shard_map/sweep/pallas_call | solution.py:65
  130.9 6.4 %finish.3.rest_0_ = f32[16,64,512]{2,1,0:T(8,128)} custom-call(f32[16,128,216]{2,1,0:T(8,128)} %fusion.3.op_ref, f32[7,64,512]{2,1,0:T(8,128)} %sweep.7.own_ref, f32[7,64,512]{2,1,0:T(8,128)} %sweep.6.one_ref, f32[7,64,512]{2,1,0:T(8,128)} %copy-done.2, f32[7,24,512]{2,1,0:T(8,128)} %copy-done.8), custom_call_target="tpu_custom_call" | custom-call | flops 594542592 | bytes 4587520 | tf_op jit(solution)/shard_map/finish/pallas_call | solution.py:123
  138.1 3.5 %finish.4.rest_0_ = f32[16,64,512]{2,1,0:T(8,128)} custom-call(f32[16,128,216]{2,1,0:T(8,128)} %fusion.3.op_ref, f32[3,64,512]{2,1,0:T(8,128)} %sweep.4.own_ref, f32[3,64,512]{2,1,0:T(8,128)} %copy-done.7, f32[3,64,512]{2,1,0:T(8,128)} %copy-done.6, f32[3,24,512]{2,1,0:T(8,128)} %slice.136.rim_ref, ...), custom_call_target="tpu_custom_call", output_to_operand_aliasing={{}: (5, {})} | custom-call | flops 254803968 | bytes 1966080 | tf_op jit(solution)/shard_map/finish/pallas_call | solution.py:123
  142.3 5.5 %finish.5 = f32[16,64,512]{2,1,0:T(8,128)} custom-call(f32[16,128,216]{2,1,0:T(8,128)} %fusion.3.op_ref, f32[6,64,512]{2,1,0:T(8,128)} %sweep.5.own_ref, f32[6,64,512]{2,1,0:T(8,128)} %collective-permute-done.1.one_ref, f32[6,64,512]{2,1,0:T(8,128)} %copy-done.4, f32[6,24,512]{2,1,0:T(8,128)} %copy-done.9, ...), custom_call_target="tpu_custom_call", output_to_operand_aliasing={{}: (5, {})} | custom-call | flops 509607936 | bytes 3932160 | tf_op jit(solution)/shard_map/finish/pallas_call | solution.py:123
  (79 shorter events, 18.1 us)
Async XLA Ops:
  0.0 9.2 %copy-start = (s32[64,3]{0,1:T(4,128)S(1)}, s32[64,3]{0,1:T(4,128)}, u32[]{:S(2)}) copy-start(s32[64,3]{0,1:T(4,128)} %param.12) | copy-start | bytes 2308
  0.0 8.7 %copy-start.15 = (s32[2,16]{1,0:T(2,128)S(1)}, s32[2,16]{1,0:T(2,128)}, u32[]{:S(2)}) copy-start(s32[2,16]{1,0:T(2,128)} %param.8) | copy-start | bytes 388
  0.0 8.7 %copy-start.16 = (s32[2,16]{1,0:T(2,128)S(1)}, s32[2,16]{1,0:T(2,128)}, u32[]{:S(2)}) copy-start(s32[2,16]{1,0:T(2,128)} %param.9) | copy-start | bytes 388
  0.0 11.7 %copy-start.13 = (f32[16,8]{0,1:T(8,128)S(1)}, f32[16,8]{0,1:T(8,128)}, u32[]{:S(2)}) copy-start(f32[16,8]{0,1:T(8,128)} %param.10) | copy-start | bytes 1540
  0.0 11.8 %copy-start.14 = (f32[16,8]{0,1:T(8,128)S(1)}, f32[16,8]{0,1:T(8,128)}, u32[]{:S(2)}) copy-start(f32[16,8]{0,1:T(8,128)} %param.11) | copy-start | bytes 1540
  0.0 12.6 %copy-start.11 = (f32[4,64,64]{2,1,0:T(8,128)S(1)}, f32[4,64,64]{2,1,0:T(8,128)}, u32[]{:S(2)}) copy-start(f32[4,64,64]{2,1,0:T(8,128)} %param.13) | copy-start | bytes 196612
  1.2 12.2 %collective-permute-start = (f32[16,64,128]{2,1,0:T(8,128)S(1)}, f32[16,64,128]{2,1,0:T(8,128)S(1)}, u32[]{:S(2)}, u32[]{:S(2)}) collective-permute-start(f32[16,64,128]{2,1,0:T(8,128)S(1)} %slice.113), channel_id=1, source_target_pairs={{0,1},{1,2},{2,3},{3,4},{4,5},{5,6},{6,7},{8,9},{9,10},{10,11},{11... | collective-permute-start | bytes 1572872 | tf_op jit(solution)/shard_map/ppermute | solution.py:160
  4.4 34.2 %collective-permute-start.6 = (f32[7,64,512]{2,1,0:T(8,128)S(1)}, f32[7,64,512]{2,1,0:T(8,128)S(1)}, u32[]{:S(2)}, u32[]{:S(2)}) collective-permute-start(f32[7,64,512]{2,1,0:T(8,128)S(1)} %slice.115), channel_id=1, source_target_pairs={{0,8},{8,16},{16,24},{24,32},{32,40},{40,48},{48,56},{56,64},{64,7... | collective-permute-start | bytes 2752520 | tf_op jit(solution)/shard_map/ppermute | solution.py:159
  18.7 24.5 %copy-start.3 = (f32[3,64,512]{2,1,0:T(8,128)S(1)}, f32[3,64,512]{2,1,0:T(8,128)}, u32[]{:S(2)}) copy-start(f32[3,64,512]{2,1,0:T(8,128)} %sweep.4.own_ref) | copy-start | bytes 1179652
  25.6 48.3 %collective-permute-start.1 = (f32[6,64,512]{2,1,0:T(8,128)}, f32[6,64,512]{2,1,0:T(8,128)}, u32[]{:S(2)}, u32[]{:S(2)}) collective-permute-start(f32[6,64,512]{2,1,0:T(8,128)} %sweep.5.own_ref), channel_id=1, source_target_pairs={{0,8},{8,16},{16,24},{24,32},{32,40},{40,48},{48,56},{56,64},{64,7... | collective-permute-start | bytes 2359304 | tf_op jit(solution)/shard_map/ppermute | solution.py:168
  38.5 7.4 %copy-start.5 = (f32[7,64,512]{2,1,0:T(8,128)}, f32[7,64,512]{2,1,0:T(8,128)S(1)}, u32[]{:S(2)}) copy-start(f32[7,64,512]{2,1,0:T(8,128)S(1)} %collective-permute-done.6.field_ref) | copy-start | bytes 2752516
  38.6 7.3 %collective-permute-start.7 = (f32[7,64,128]{2,1,0:T(8,128)S(1)}, f32[7,64,128]{2,1,0:T(8,128)S(1)}, u32[]{:S(2)}, u32[]{:S(2)}) collective-permute-start(f32[7,64,128]{2,1,0:T(8,128)S(1)} %slice.116), channel_id=1, source_target_pairs={{0,1},{1,2},{2,3},{3,4},{4,5},{5,6},{6,7},{8,9},{9,10},{10,11},{11... | collective-permute-start | bytes 688136 | tf_op jit(solution)/shard_map/ppermute | solution.py:194
  43.2 30.6 %collective-permute-start.3 = (f32[3,64,512]{2,1,0:T(8,128)S(1)}, f32[3,64,512]{2,1,0:T(8,128)}, u32[]{:S(2)}, u32[]{:S(2)}) collective-permute-start(f32[3,64,512]{2,1,0:T(8,128)S(1)} %copy-done.3), channel_id=1, source_target_pairs={{0,40},{8,48},{16,56},{24,0},{32,8},{40,16},{48,24},{56,32},{64,10... | collective-permute-start | bytes 1179656 | tf_op jit(solution)/shard_map/ppermute | solution.py:166
  54.2 41.0 %collective-permute-start.8 = (f32[7,64,512]{2,1,0:T(8,128)}, f32[7,64,512]{2,1,0:T(8,128)S(1)}, u32[]{:S(2)}, u32[]{:S(2)}) collective-permute-start(f32[7,64,512]{2,1,0:T(8,128)} %sweep.6.one_ref), channel_id=1, source_target_pairs={{0,8},{8,16},{16,24},{24,32},{32,40},{40,48},{48,56},{56,64},{64,7... | collective-permute-start | bytes 2752520 | tf_op jit(solution)/shard_map/ppermute | solution.py:197
  73.9 21.4 %collective-permute-start.4 = (f32[3,64,512]{2,1,0:T(8,128)}, f32[3,64,512]{2,1,0:T(8,128)S(1)}, u32[]{:S(2)}, u32[]{:S(2)}) collective-permute-start(f32[3,64,512]{2,1,0:T(8,128)} %collective-permute-done.3), channel_id=1, source_target_pairs={{40,24},{48,32},{56,40},{0,48},{8,56},{16,64},{24,72},{32,80},{104... | collective-permute-start | bytes 1179656 | tf_op jit(solution)/shard_map/ppermute | solution.py:199
  75.8 29.6 %collective-permute-start.2 = (f32[6,64,512]{2,1,0:T(8,128)}, f32[6,64,512]{2,1,0:T(8,128)S(1)}, u32[]{:S(2)}, u32[]{:S(2)}) collective-permute-start(f32[6,64,512]{2,1,0:T(8,128)} %collective-permute-done.1.one_ref), channel_id=1, source_target_pairs={{0,8},{8,16},{16,24},{24,32},{32,40},{40,48},{48,56},{56,64},{64,7... | collective-permute-start | bytes 2359304 | tf_op jit(solution)/shard_map/ppermute | solution.py:198
  95.2 8.2 %copy-start.12 = (f32[3,64,512]{2,1,0:T(8,128)}, f32[3,64,512]{2,1,0:T(8,128)S(1)}, u32[]{:S(2)}) copy-start(f32[3,64,512]{2,1,0:T(8,128)S(1)} %collective-permute-done.4) | copy-start | bytes 1179652
  95.2 8.2 %copy-start.2 = (f32[7,64,512]{2,1,0:T(8,128)}, f32[7,64,512]{2,1,0:T(8,128)S(1)}, u32[]{:S(2)}) copy-start(f32[7,64,512]{2,1,0:T(8,128)S(1)} %collective-permute-done.8.two_ref) | copy-start | bytes 2752516
  95.2 16.3 %collective-permute-start.9 = (f32[3,64,512]{2,1,0:T(8,128)S(1)}, f32[3,64,512]{2,1,0:T(8,128)S(1)}, u32[]{:S(2)}, u32[]{:S(2)}) collective-permute-start(f32[3,64,512]{2,1,0:T(8,128)S(1)} %collective-permute-done.4), channel_id=1, source_target_pairs={{0,504},{8,0},{16,8},{24,16},{32,24},{40,32},{48,40},{56,48},{64,5... | collective-permute-start | bytes 1179656 | tf_op jit(solution)/shard_map/ppermute | solution.py:201
  103.5 26.7 %collective-permute-start.11 = (f32[7,24,512]{2,1,0:T(8,128)S(1)}, f32[7,24,512]{2,1,0:T(8,128)S(1)}, u32[]{:S(2)}, u32[]{:S(2)}) collective-permute-start(f32[7,24,512]{2,1,0:T(8,128)S(1)} %slice.137), channel_id=1, source_target_pairs={{0,8},{8,16},{16,24},{24,32},{32,40},{40,48},{48,56},{56,64},{64,7... | collective-permute-start | bytes 1032200 | tf_op jit(solution)/shard_map/ppermute | solution.py:200
  105.4 0.9 copy-start.4
  106.3 35.3 %collective-permute-start.5 = (f32[6,24,512]{2,1,0:T(8,128)S(1)}, f32[6,24,512]{2,1,0:T(8,128)S(1)}, u32[]{:S(2)}, u32[]{:S(2)}) collective-permute-start(f32[6,24,512]{2,1,0:T(8,128)S(1)} %slice.135), channel_id=1, source_target_pairs={{0,8},{8,16},{16,24},{24,32},{32,40},{40,48},{48,56},{56,64},{64,7... | collective-permute-start | bytes 884744 | tf_op jit(solution)/shard_map/ppermute | solution.py:202
  111.5 9.5 %copy-start.6 = (f32[3,64,512]{2,1,0:T(8,128)}, f32[3,64,512]{2,1,0:T(8,128)S(1)}, u32[]{:S(2)}) copy-start(f32[3,64,512]{2,1,0:T(8,128)S(1)} %collective-permute-done.9.two_ref) | copy-start | bytes 1179652
  111.5 25.8 %collective-permute-start.10 = (f32[3,64,512]{2,1,0:T(8,128)S(1)}, f32[3,64,512]{2,1,0:T(8,128)S(1)}, u32[]{:S(2)}, u32[]{:S(2)}) collective-permute-start(f32[3,64,512]{2,1,0:T(8,128)S(1)} %collective-permute-done.9.two_ref), channel_id=1, source_target_pairs={{0,504},{8,0},{16,8},{24,16},{32,24},{40,32},{48,40},{56,48},{64,5... | collective-permute-start | bytes 1179656 | tf_op jit(solution)/shard_map/ppermute | solution.py:203
  (5 other events, 3.7 us)

commit v3 on v2

v3 whole, which is shorter than its diff:
```python
import functools
import jax
import jax.numpy as jnp
from jax import lax
from jax.experimental import pallas as pl
from jax.experimental.pallas import tpu as pltpu
from jax.sharding import PartitionSpec as P

WBLK = 128
BETA = 0.5
RIM = 24
VMEM = 16 << 20
FINCOST = 10000000000
NOCOST = pl.CostEstimate(flops=1, bytes_accessed=1, transcendentals=0)


def sweep_kernel(first, taps, step_rows, offset_ref, scale_ref, field_ref, edge_ref, out_ref):
    batch = pl.program_id(0) + first
    offset = offset_ref[batch]
    rows = field_ref.shape[1]
    groups = field_ref.shape[2] // WBLK
    lane = lax.broadcasted_iota(jnp.int32, (step_rows, WBLK), 1) - offset
    scale = [scale_ref[batch, tap] for tap in range(taps)]
    for row in range(0, rows, step_rows):
        here = slice(row, row + step_rows)
        turned = [pltpu.roll(edge_ref[0, here], offset, 1)]
        for group in range(groups):
            turned.append(pltpu.roll(field_ref[0, here, group * WBLK : (group + 1) * WBLK], offset, 1))
        sums = [None] * groups
        for tap in range(taps):
            if tap:
                turned = [pltpu.roll(piece, 1, 1) for piece in turned]
            inside = lane >= tap
            for group in range(groups):
                term = scale[tap] * jnp.where(inside, turned[group + 1], turned[group])
                sums[group] = term if tap == 0 else sums[group] + term
        for group in range(groups):
            out_ref[0, here, group * WBLK : (group + 1) * WBLK] = sums[group]


def split(value):
    high = value.astype(jnp.bfloat16)
    return high, (value - high.astype(jnp.float32)).astype(jnp.bfloat16)


def sweep_mxu_kernel(first, taps, step_rows, offset_ref, scale_ref, field_ref, edge_ref, out_ref):
    batch = pl.program_id(0) + first
    offset = offset_ref[batch]
    rows = field_ref.shape[1]
    groups = field_ref.shape[2] // WBLK
    source = lax.broadcasted_iota(jnp.int32, (2 * WBLK, WBLK), 0)
    target = lax.broadcasted_iota(jnp.int32, (2 * WBLK, WBLK), 1)
    distance = WBLK + target - source - offset
    matrix = jnp.zeros((2 * WBLK, WBLK), jnp.float32)
    for tap in range(taps):
        matrix = jnp.where(distance == tap, scale_ref[batch, tap], matrix)
    mh, ml = split(matrix)
    pieces = [edge_ref[0]] + [field_ref[0, :, g * WBLK : (g + 1) * WBLK] for g in range(groups)]
    parts = [split(p) for p in pieces]
    hi = jnp.concatenate([jnp.concatenate([parts[g][0], parts[g + 1][0]], axis=1) for g in range(groups)], axis=0)
    lo = jnp.concatenate([jnp.concatenate([parts[g][1], parts[g + 1][1]], axis=1) for g in range(groups)], axis=0)
    dot = functools.partial(jnp.dot, preferred_element_type=jnp.float32)
    both = dot(hi, jnp.concatenate([mh, ml], axis=1))
    res = both[:, :WBLK] + both[:, WBLK:] + dot(lo, mh)
    for group in range(groups):
        out_ref[0, :, group * WBLK : (group + 1) * WBLK] = res[group * rows : (group + 1) * rows]


def sweep(field, edge, offsets, scales, part, field_first, edge_first, kern=sweep_kernel, step_rows=8):
    lo, hi = part
    _, rows, width = field.shape
    count = hi - lo
    taps = scales.shape[1]
    return pl.pallas_call(
        functools.partial(kern, lo, taps, step_rows),
        grid_spec=pltpu.PrefetchScalarGridSpec(
            num_scalar_prefetch=2,
            grid=(count,),
            in_specs=[
                pl.BlockSpec((1, rows, width), lambda i, o, s: (i + field_first, 0, 0)),
                pl.BlockSpec((1, rows, WBLK), lambda i, o, s: (i + edge_first, 0, 0)),
            ],
            out_specs=pl.BlockSpec((1, rows, width), lambda i, o, s: (i, 0, 0)),
        ),
        out_shape=jax.ShapeDtypeStruct((count, rows, width), jnp.float32),
        compiler_params=pltpu.CompilerParams(vmem_limit_bytes=VMEM),
        cost_estimate=NOCOST,
        name="sweep",
    )(offsets, scales, field, edge)


def operator_kernel(taps, spot_ref, offset_ref, scale_ref, own_ref, one_ref, two_ref, out_ref, turn_ref):
    tile_len = own_ref.shape[1]
    batch = pl.program_id(0)
    depth = out_ref.shape[2]

    @pl.when(batch == 0)
    def _():
        for below, ref in enumerate((own_ref, one_ref, two_ref)):
            present = (spot_ref[1 + below] >= 0).astype(jnp.float32)
            turn_ref[:, below * tile_len : (below + 1) * tile_len] = ref[0].T * present

    column = lax.broadcasted_iota(jnp.int32, (3 * tile_len, depth), 1)
    row = lax.broadcasted_iota(jnp.int32, (3 * tile_len, depth), 0)
    tile_row, tile_col = row // tile_len, column // tile_len
    place_row = row % tile_len - tile_len * tile_row
    place_col = column % tile_len - tile_len * tile_col + jnp.where(tile_col == 3, tile_len - RIM, 0)
    distance = jnp.where(spot_ref[0] >= tile_col, place_row - place_col - offset_ref[batch], -1)
    band = jnp.zeros((3 * tile_len, depth), jnp.float32)
    for tap in range(taps):
        band = jnp.where(distance == tap, scale_ref[batch, tap], band)
    band_high, band_low = split(band)
    turn_high, turn_low = split(turn_ref[...])
    dot = functools.partial(jnp.dot, preferred_element_type=jnp.float32)
    rate = dot(turn_high, band_low) + dot(turn_low, band_high) + dot(turn_high, band_high)
    high, low = split(rate)
    out_ref[0, :tile_len] = high
    out_ref[0, tile_len : 2 * tile_len] = band_high[:tile_len]
    out_ref[0, 2 * tile_len : 3 * tile_len] = low
    out_ref[0, 3 * tile_len :] = band_low[:tile_len]


def length_operator(spot, offsets, scales, agg_kern):
    batches, taps = scales.shape
    tile_len = agg_kern.shape[1]
    depth = 3 * tile_len + RIM

    def pick(below):
        return pl.BlockSpec((1, tile_len, tile_len), lambda i, s, o, q: (jnp.maximum(s[1 + below], 0), 0, 0))

    return pl.pallas_call(
        functools.partial(operator_kernel, taps),
        grid_spec=pltpu.PrefetchScalarGridSpec(
            num_scalar_prefetch=3,
            grid=(batches,),
            in_specs=[pick(0), pick(1), pick(2)],
            out_specs=pl.BlockSpec((1, 4 * tile_len, depth), lambda i, s, o, q: (i, 0, 0)),
            scratch_shapes=[pltpu.VMEM((tile_len, 3 * tile_len), jnp.float32)],
        ),
        out_shape=jax.ShapeDtypeStruct((batches, 4 * tile_len, depth), jnp.bfloat16),
        compiler_params=pltpu.CompilerParams(vmem_limit_bytes=VMEM),
        cost_estimate=NOCOST,
        name="operator",
    )(spot, offsets, scales, agg_kern, agg_kern, agg_kern)


def finish_kernel(op_ref, own_ref, one_ref, two_ref, rim_ref, *rest):
    out_ref, high_ref, low_ref = rest[-3:]
    rows = own_ref.shape[1]
    at = 0
    for ref in (own_ref, one_ref, two_ref, rim_ref):
        high, low = split(ref[0])
        high_ref[at : at + ref.shape[1]] = high
        low_ref[at : at + ref.shape[1]] = low
        at += ref.shape[1]
    dot = functools.partial(jnp.dot, preferred_element_type=jnp.float32)
    four = dot(op_ref[0], high_ref[...])
    both = four[: 2 * rows] + four[2 * rows :] + dot(op_ref[0, : 2 * rows], low_ref[...])
    rate, spread = both[:rows], both[rows:]
    out_ref[0] = spread + BETA * (rate * rate / (1.0 + rate) - spread * rate)


def finish(operator, own, one, two, rim, part, total, before, own_first):
    lo, hi = part
    count, rows, width = one.shape
    depth = operator.shape[2]
    here = lambda i: (i, 0, 0)
    in_specs = [
        pl.BlockSpec((1, operator.shape[1], depth), lambda i: (i + lo, 0, 0)),
        pl.BlockSpec((1, rows, width), lambda i: (i + own_first, 0, 0)),
        pl.BlockSpec((1, rows, width), here),
        pl.BlockSpec((1, rows, width), here),
        pl.BlockSpec((1, RIM, width), here),
    ]
    operands = [operator, own, one, two, rim]
    aliases = {}
    if before is not None:
        in_specs.append(pl.BlockSpec(memory_space=pl.ANY))
        operands.append(before)
        aliases = {5: 0}
    return pl.pallas_call(
        finish_kernel,
        grid=(count,),
        in_specs=in_specs,
        out_specs=pl.BlockSpec((1, rows, width), lambda i: (i + lo, 0, 0)),
        out_shape=jax.ShapeDtypeStruct((total, rows, width), jnp.float32),
        scratch_shapes=[pltpu.VMEM((depth, width), jnp.bfloat16)] * 2,
        input_output_aliases=aliases,
        compiler_params=pltpu.CompilerParams(vmem_limit_bytes=VMEM),
        cost_estimate=pl.CostEstimate(flops=FINCOST, bytes_accessed=1, transcendentals=0),
        name="finish",
    )(*operands)


RING = 8
EARLY = (0, 6)
BACK = (6, 9)
LATE = (9, 16)
FIRST = (0, 9)


def tap_scale(band, taps):
    tap_range = jnp.arange(taps.shape[1], dtype=jnp.int32)
    weights = jnp.where(tap_range[None, :] < band[1][:, None], taps, 0.0)
    return weights / jnp.sum(weights, axis=1, keepdims=True)


def after(value, *earlier):
    return lax.optimization_barrier((value,) + earlier)[0]


def shards(density, len_band, wid_band, len_taps, wid_taps, tile_pairs, agg_kern):
    batches, tile_len, group_width = density.shape
    tiles = lax.axis_size("len")
    groups = lax.axis_size("wid")
    me = lax.axis_index("len")
    margin = group_width - WBLK

    def spot(tile, step):
        return tile // RING * RING + (tile + step) % RING

    def move(pairs):
        return functools.partial(lax.ppermute, axis_name="len", perm=pairs)

    hop = move([(t, (t + 1) % tiles) for t in range(tiles)])
    unhop = move([(t, (t - 1) % tiles) for t in range(tiles)])
    back_three = move([(t, spot(t, -3)) for t in range(tiles)])
    back_five = move([(spot(t, -3), (t + 3) % tiles) for t in range(tiles)])
    side = functools.partial(lax.ppermute, axis_name="wid", perm=[(s, s + 1) for s in range(groups - 1)])

    early_one_raw = hop(density[EARLY[0] : EARLY[1]])
    back_away_raw = back_three(density[BACK[0] : BACK[1]])
    edge = side(density[:, :, margin:])

    offsets = wid_band[0]
    scales = tap_scale(wid_band, wid_taps)
    length_scales = tap_scale(len_band, len_taps)
    place = jnp.concatenate([me[None].astype(jnp.int32), lax.dynamic_slice_in_dim(tile_pairs, me, 1, 0)[0]])
    edge = after(edge, scales, length_scales, place)

    late_own = sweep(density, edge, offsets, scales, LATE, LATE[0], LATE[0])
    late_one = hop(late_own)
    operator = length_operator(after(place, late_own), len_band[0], length_scales, agg_kern)
    first_own = sweep(density, after(edge, operator), offsets, scales, FIRST, FIRST[0], FIRST[0])
    early_one_raw, back_away_raw, first_own = lax.optimization_barrier((early_one_raw, back_away_raw, first_own))

    first_edge = side(jnp.concatenate([early_one_raw[:, :, margin:], back_away_raw[:, :, margin:]], axis=0))
    early_one = sweep(early_one_raw, first_edge, offsets, scales, EARLY, 0, 0)
    early_two = hop(early_one)
    back_away = sweep(back_away_raw, after(first_edge, early_one), offsets, scales, BACK, 0, EARLY[1])
    back_three_below = back_five(back_away)
    late_one = after(late_one, back_away)
    late_two = hop(late_one)
    early_two = after(early_two, late_one)
    early_rim = hop(early_two[:, tile_len - RIM :])
    back_three_below = after(back_three_below, early_two)
    back_two = unhop(back_three_below)
    late_two = after(late_two, back_three_below)
    late_rim = hop(late_two[:, tile_len - RIM :])
    back_two = after(back_two, late_two)
    back_one = unhop(back_two)

    early_rim = after(early_rim, back_two)
    out = finish(operator, first_own, early_one, early_two, early_rim, EARLY, batches, None, 0)
    out = finish(
        operator, first_own, back_one, back_two, back_three_below[:, tile_len - RIM :], BACK, batches, out, EARLY[1]
    )
    return finish(operator, late_own, late_one, late_two, late_rim, LATE, batches, out, 0)


def solution(mesh):
    in_specs = (P(None, "len", "wid"), P(), P(), P(), P(), P(), P())
    out_specs = P(None, "len", "wid")
    return jax.shard_map(shards, mesh=mesh, in_specs=in_specs, out_specs=out_specs, check_vma=False)
```

time: 149 us -> 133 us (0.89)
  starting transfers between devices: 41.4 us -> 51.6 us
  Pallas kernels: 42.1 us -> 33.8 us
  waiting for transfers between devices: 41.2 us -> 34.3 us
  between operations: 4.09 us -> 0.27 us
  matrix products: 3.31 us -> 0 us
  local copies, waits for them, and re-layouts: 11.4 us -> 9.45 us
    ppermute x8, starting transfers between devices: 27.1 us -> 40 us  [the longest x1 10 us: shards(): back_away_raw = back_three(density[BACK[0]:BACK[1]])]
    ppermute x8, waiting for transfers between devices: 32.5 us -> 19.8 us  [the longest x1 5.37 us: shards(): side(jnp.concatenate([early_one_raw[:, :, margin:], back_away_raw[:, :, m...]
    ppermute x1, waiting for transfers between devices: 0.01 us -> 10.5 us  [shards(): early_two = hop(early_one)]
    ppermute x1, waiting for transfers between devices: 8.71 us -> 0.01 us  [shards(): early_one_raw = hop(density[EARLY[0]:EARLY[1]])]
    pallas_call x3, Pallas kernels: 15.5 us -> 8.65 us  [finish(): pl.pallas_call(finish_kernel, grid=(count,), in_specs=in_specs, out_specs...]
    ppermute x1, waiting for transfers between devices: 0.01 us -> 3.95 us  [shards(): late_two = hop(late_one)]
    unnamed x39 -> x18, local copies, waits for them, and re-layouts: 5 us -> 1.45 us
    dot_general x3 -> x0, matrix products: 3.31 us -> none  [shards(): jnp.einsum('ml,bmi->bli', kernel, band, precision=HIGHEST)]
  transfers between devices with their start and end apart: 12 -> 12, of which waited for: 5 -> 7; matrix products, arithmetic and copies ran while one was open for 9% -> 8% of each run, Pallas kernels for 25% -> 23%
where the time goes in v3:
time: 133 us
  starting transfers between devices  51.6 us (39%)
  waiting for transfers between devices  34.3 us (26%)
  Pallas kernels  33.8 us (25%)
  local copies, waits for them, and re-layouts  9.45 us (7%)
  other arithmetic  3.18 us (2%)
    pallas_call x4, Pallas kernels, sweep(): pl.pallas_call(functools.partial(kern, lo, taps, step_rows), grid_spec=pl...  18.7 us
    ppermute x1, waiting for transfers between devices, shards(): early_two = hop(early_one)  10.5 us
    ppermute x1, starting transfers between devices, shards(): back_away_raw = back_three(density[BACK[0]:BACK[1]])  10 us
    pallas_call x3, Pallas kernels, finish(): pl.pallas_call(finish_kernel, grid=(count,), in_specs=in_specs, out_specs...  8.65 us
    ppermute x1, starting transfers between devices, shards(): back_three_below = back_five(back_away)  7.6 us
    ppermute x1, starting transfers between devices, shards(): back_one = unhop(back_two)  7.11 us
    pallas_call x1, Pallas kernels, length_operator(): pl.pallas_call(functools.partial(operator_kernel, taps), grid_spec=pltpu....  6.44 us
    ppermute x1, starting transfers between devices, shards(): back_two = unhop(back_three_below)  6.41 us
  transfers between devices with their start and end apart: 12, of which 7 were waited for; matrix products, arithmetic and copies ran while one was open for 8% of the time, Pallas kernels for 23%

profile of v3, /device:TPU:2, one launch (start us, length us, event | category | flops | bytes accessed | tf_op | source)
XLA Modules:
  0.0 132.6 jit_solution(11427986629287043425)
XLA Ops:
  0.0 2.0 %slice.38 = f32[16,64,128]{2,1,0:T(8,128)} slice(f32[16,64,512]{2,1,0:T(8,128)} %field_ref.3), slice={[0:16], [0:64], [384:512]} | slice | bytes 1048576 | tf_op jit(solution)/shard_map/slice | solution.py:233
  4.0 2.1 %slice.41 = f32[6,64,512]{2,1,0:T(8,128)} slice(f32[16,64,512]{2,1,0:T(8,128)} %field_ref.3), slice={[0:6], [0:64], [0:512]} | slice | bytes 1572864 | tf_op jit(solution)/shard_map/slice | solution.py:231
  6.1 4.4 %collective-permute-start.2 = (f32[6,64,512]{2,1,0:T(8,128)}, f32[6,64,512]{2,1,0:T(8,128)S(1)}, u32[]{:S(2)}, u32[]{:S(2)}) collective-permute-start(f32[6,64,512]{2,1,0:T(8,128)} %slice.41), channel_id=1, source_target_pairs={{0,8},{8,16},{16,24},{24,32},{32,40},{40,48},{48,56},{56,64},{64,7... | collective-permute-start | bytes 2359304 | tf_op jit(solution)/shard_map/ppermute | solution.py:231
  11.3 10.0 %collective-permute-start.3 = (f32[3,64,512]{2,1,0:T(8,128)}, f32[3,64,512]{2,1,0:T(8,128)}, u32[]{:S(2)}, u32[]{:S(2)}) collective-permute-start(f32[3,64,512]{2,1,0:T(8,128)} %slice.42), channel_id=1, source_target_pairs={{0,40},{8,48},{16,56},{24,0},{32,8},{40,16},{48,24},{56,32},{64,10... | collective-permute-start | bytes 1179656 | tf_op jit(solution)/shard_map/ppermute | solution.py:232
  28.0 4.8 %sweep.4.own_ref = f32[7,64,512]{2,1,0:T(8,128)S(1)} custom-call(s32[16]{0:T(128)S(1)} %get-tuple-element.34.offset_ref, f32[16,8]{1,0:T(8,128)S(1)} %get-tuple-element.36.scale_ref, f32[16,64,512]{2,1,0:T(8,128)S(1)} %copy-done.1, f32[16,64,128]{2,1,0:T(8,128)S(1)} %collective-permute-done.edge_ref), custom_call_target="tpu_custom_call" | custom-call | flops 1 | bytes 1 | tf_op jit(solution)/shard_map/sweep/pallas_call | solution.py:74
  32.8 3.4 %collective-permute-start.1 = (f32[7,64,512]{2,1,0:T(8,128)S(1)}, f32[7,64,512]{2,1,0:T(8,128)S(1)}, u32[]{:S(2)}, u32[]{:S(2)}) collective-permute-start(f32[7,64,512]{2,1,0:T(8,128)S(1)} %sweep.4.own_ref), channel_id=1, source_target_pairs={{0,8},{8,16},{16,24},{24,32},{32,40},{40,48},{48,56},{56,64},{64,7... | collective-permute-start | bytes 2752520 | tf_op jit(solution)/shard_map/ppermute | solution.py:242
  36.3 6.4 %operator.1.op_ref = bf16[16,256,216]{2,1,0:T(8,128)(2,1)S(1)} custom-call(s32[4]{0:T(128)S(1)} %pad_add_fusion.spot_ref, s32[16]{0:T(128)S(1)} %copy-done.4, f32[16,8]{1,0:T(8,128)S(1)} %copy-done.3, f32[4,64,64]{2,1,0:T(8,128)S(1)} %copy-done.2, f32[4,64,64]{2,1,0:T(8,128)S(1)} %copy-done.2, f32[4,64,64]{2,1,0:T(8,128)S(1)} %copy-done.2), custom_call_target="tpu_custom_call" | custom-call | flops 1 | bytes 1 | tf_op jit(solution)/shard_map/operator/pallas_call | solution.py:131
  42.7 6.0 %sweep.5.own_ref = f32[9,64,512]{2,1,0:T(8,128)S(1)} custom-call(s32[16]{0:T(128)S(1)} %get-tuple-element.34.offset_ref, f32[16,8]{1,0:T(8,128)S(1)} %get-tuple-element.36.scale_ref, f32[16,64,512]{2,1,0:T(8,128)S(1)} %copy-done.1, f32[16,64,128]{2,1,0:T(8,128)S(1)} %collective-permute-done.edge_ref), custom_call_target="tpu_custom_call" | custom-call | flops 1 | bytes 1 | tf_op jit(solution)/shard_map/sweep/pallas_call | solution.py:74
  49.7 2.7 %collective-permute-start.4 = (f32[9,64,128]{2,1,0:T(8,128)S(1)}, f32[9,64,128]{2,1,0:T(8,128)S(1)}, u32[]{:S(2)}, u32[]{:S(2)}) collective-permute-start(f32[9,64,128]{2,1,0:T(8,128)S(1)} %pad_maximum_fusion), channel_id=1, source_target_pairs={{0,1},{1,2},{2,3},{3,4},{4,5},{5,6},{6,7},{8,9},{9,10},{10,11},{11... | collective-permute-start | bytes 884744 | tf_op jit(solution)/shard_map/ppermute | solution.py:247
  52.4 5.4 %collective-permute-done.4.edge_ref = f32[9,64,128]{2,1,0:T(8,128)S(1)} collective-permute-done((f32[9,64,128]{2,1,0:T(8,128)S(1)}, f32[9,64,128]{2,1,0:T(8,128)S(1)}, u32[]{:S(2)}, u32[]{:S(2)}) %collective-permute-start.4) | collective-permute-done | bytes 294944 | tf_op jit(solution)/shard_map/ppermute | solution.py:247
  57.7 4.2 %sweep.6.one_ref = f32[6,64,512]{2,1,0:T(8,128)S(1)} custom-call(s32[16]{0:T(128)S(1)} %get-tuple-element.34.offset_ref, f32[16,8]{1,0:T(8,128)S(1)} %get-tuple-element.36.scale_ref, f32[6,64,512]{2,1,0:T(8,128)S(1)} %collective-permute-done.2.field_ref, f32[9,64,128]{2,1,0:T(8,128)S(1)} %collective-permute-done.4.edge_ref), custom_call_target="tpu_custom_call" | custom-call | flops 1 | bytes 1 | tf_op jit(solution)/shard_map/sweep/pallas_call | solution.py:74
  63.9 3.7 %sweep.7 = f32[3,64,512]{2,1,0:T(8,128)S(1)} custom-call(s32[16]{0:T(128)S(1)} %get-tuple-element.34.offset_ref, f32[16,8]{1,0:T(8,128)S(1)} %get-tuple-element.36.scale_ref, f32[3,64,512]{2,1,0:T(8,128)} %collective-permute-done.3.field_ref, f32[9,64,128]{2,1,0:T(8,128)S(1)} %collective-permute-done.4.edge_ref), custom_call_target="tpu_custom_call" | custom-call | flops 1 | bytes 1 | tf_op jit(solution)/shard_map/sweep/pallas_call | solution.py:74
  69.5 7.6 %collective-permute-start.6 = (f32[3,64,512]{2,1,0:T(8,128)S(1)}, f32[3,64,512]{2,1,0:T(8,128)S(1)}, u32[]{:S(2)}, u32[]{:S(2)}) collective-permute-start(f32[3,64,512]{2,1,0:T(8,128)S(1)} %sweep.7), channel_id=1, source_target_pairs={{40,24},{48,32},{56,40},{0,48},{8,56},{16,64},{24,72},{32,80},{104... | collective-permute-start | bytes 1179656 | tf_op jit(solution)/shard_map/ppermute | solution.py:251
  77.1 10.5 %collective-permute-done.7.two_ref = f32[6,64,512]{2,1,0:T(8,128)S(1)} collective-permute-done((f32[6,64,512]{2,1,0:T(8,128)S(1)}, f32[6,64,512]{2,1,0:T(8,128)S(1)}, u32[]{:S(2)}, u32[]{:S(2)}) %collective-permute-start.7) | collective-permute-done | bytes 786464 | tf_op jit(solution)/shard_map/ppermute | solution.py:249
  87.7 5.0 %collective-permute-done.6 = f32[3,64,512]{2,1,0:T(8,128)S(1)} collective-permute-done((f32[3,64,512]{2,1,0:T(8,128)S(1)}, f32[3,64,512]{2,1,0:T(8,128)S(1)}, u32[]{:S(2)}, u32[]{:S(2)}) %collective-permute-start.6) | collective-permute-done | bytes 393248 | tf_op jit(solution)/shard_map/ppermute | solution.py:251
  92.7 6.4 %collective-permute-start.9 = (f32[3,64,512]{2,1,0:T(8,128)S(1)}, f32[3,64,512]{2,1,0:T(8,128)S(1)}, u32[]{:S(2)}, u32[]{:S(2)}) collective-permute-start(f32[3,64,512]{2,1,0:T(8,128)S(1)} %collective-permute-done.6), channel_id=1, source_target_pairs={{0,504},{8,0},{16,8},{24,16},{32,24},{40,32},{48,40},{56,48},{64,5... | collective-permute-start | bytes 1179656 | tf_op jit(solution)/shard_map/ppermute | solution.py:257
  99.1 2.3 %collective-permute-start.11 = (f32[6,24,512]{2,1,0:T(8,128)S(1)}, f32[6,24,512]{2,1,0:T(8,128)S(1)}, u32[]{:S(2)}, u32[]{:S(2)}) collective-permute-start(f32[6,24,512]{2,1,0:T(8,128)S(1)} %slice.47), channel_id=1, source_target_pairs={{0,8},{8,16},{16,24},{24,32},{32,40},{40,48},{48,56},{56,64},{64,7... | collective-permute-start | bytes 884744 | tf_op jit(solution)/shard_map/ppermute | solution.py:255
  101.5 4.0 %collective-permute-done.5.two_ref = f32[7,64,512]{2,1,0:T(8,128)S(1)} collective-permute-done((f32[7,64,512]{2,1,0:T(8,128)S(1)}, f32[7,64,512]{2,1,0:T(8,128)S(1)}, u32[]{:S(2)}, u32[]{:S(2)}) %collective-permute-start.5) | collective-permute-done | bytes 917536 | tf_op jit(solution)/shard_map/ppermute | solution.py:253
  105.5 2.5 %collective-permute-done.9.two_ref = f32[3,64,512]{2,1,0:T(8,128)S(1)} collective-permute-done((f32[3,64,512]{2,1,0:T(8,128)S(1)}, f32[3,64,512]{2,1,0:T(8,128)S(1)}, u32[]{:S(2)}, u32[]{:S(2)}) %collective-permute-start.9) | collective-permute-done | bytes 393248 | tf_op jit(solution)/shard_map/ppermute | solution.py:257
  108.0 7.1 %collective-permute-start.10 = (f32[3,64,512]{2,1,0:T(8,128)S(1)}, f32[3,64,512]{2,1,0:T(8,128)S(1)}, u32[]{:S(2)}, u32[]{:S(2)}) collective-permute-start(f32[3,64,512]{2,1,0:T(8,128)S(1)} %collective-permute-done.9.two_ref), channel_id=1, source_target_pairs={{0,504},{8,0},{16,8},{24,16},{32,24},{40,32},{48,40},{56,48},{64,5... | collective-permute-start | bytes 1179656 | tf_op jit(solution)/shard_map/ppermute | solution.py:261
  117.0 3.1 %finish.3.rest_0_ = f32[16,64,512]{2,1,0:T(8,128)} custom-call(bf16[16,256,216]{2,1,0:T(8,128)(2,1)S(1)} %operator.1.op_ref, f32[9,64,512]{2,1,0:T(8,128)S(1)} %sweep.5.own_ref, f32[6,64,512]{2,1,0:T(8,128)S(1)} %sweep.6.one_ref, f32[6,64,512]{2,1,0:T(8,128)S(1)} %collective-permute-done.7.two_ref, f32[6,24,512]{2,1,0:T(8,128)S(1)} %collective-permute-done.11.rim_ref), custom_call_target="tpu_custom_call" | custom-call | flops 10000000000 | bytes 1 | tf_op jit(solution)/shard_map/finish/pallas_call | solution.py:181
  120.1 2.4 %collective-permute-done.10.one_ref = f32[3,64,512]{2,1,0:T(8,128)S(1)} collective-permute-done((f32[3,64,512]{2,1,0:T(8,128)S(1)}, f32[3,64,512]{2,1,0:T(8,128)S(1)}, u32[]{:S(2)}, u32[]{:S(2)}) %collective-permute-start.10) | collective-permute-done | bytes 393248 | tf_op jit(solution)/shard_map/ppermute | solution.py:261
  124.4 4.5 %collective-permute-done.8.rim_ref = f32[7,24,512]{2,1,0:T(8,128)S(1)} collective-permute-done((f32[7,24,512]{2,1,0:T(8,128)S(1)}, f32[7,24,512]{2,1,0:T(8,128)S(1)}, u32[]{:S(2)}, u32[]{:S(2)}) %collective-permute-start.8) | collective-permute-done | bytes 344096 | tf_op jit(solution)/shard_map/ppermute | solution.py:259
  128.9 3.7 %finish.5 = f32[16,64,512]{2,1,0:T(8,128)} custom-call(bf16[16,256,216]{2,1,0:T(8,128)(2,1)S(1)} %operator.1.op_ref, f32[7,64,512]{2,1,0:T(8,128)S(1)} %sweep.4.own_ref, f32[7,64,512]{2,1,0:T(8,128)S(1)} %collective-permute-done.1.one_ref, f32[7,64,512]{2,1,0:T(8,128)S(1)} %collective-permute-done.5.two_ref, ...), custom_call_target="tpu_custom_call", output_to_operand_aliasing={{}: (5, {})} | custom-call | flops 10000000000 | bytes 1 | tf_op jit(solution)/shard_map/finish/pallas_call | solution.py:181
  (42 shorter events, 18.0 us)
Async XLA Ops:
  0.0 27.7 %copy-start = (s32[64,3]{0,1:T(4,128)S(1)}, s32[64,3]{0,1:T(4,128)}, u32[]{:S(2)}) copy-start(s32[64,3]{0,1:T(4,128)} %param.12) | copy-start | bytes 2308
  0.0 10.5 %copy-start.1 = (f32[16,64,512]{2,1,0:T(8,128)S(1)}, f32[16,64,512]{2,1,0:T(8,128)}, u32[]{:S(2)}) copy-start(f32[16,64,512]{2,1,0:T(8,128)} %field_ref.3) | copy-start | bytes 6291460
  0.0 21.3 %copy-start.7 = (s32[2,16]{1,0:T(2,128)S(1)}, s32[2,16]{1,0:T(2,128)}, u32[]{:S(2)}) copy-start(s32[2,16]{1,0:T(2,128)} %param.8) | copy-start | bytes 388
  0.0 21.9 %copy-start.6 = (f32[16,8]{0,1:T(8,128)S(1)}, f32[16,8]{0,1:T(8,128)}, u32[]{:S(2)}) copy-start(f32[16,8]{0,1:T(8,128)} %param.10) | copy-start | bytes 1540
  2.1 26.0 %collective-permute-start = (f32[16,64,128]{2,1,0:T(8,128)}, f32[16,64,128]{2,1,0:T(8,128)S(1)}, u32[]{:S(2)}, u32[]{:S(2)}) collective-permute-start(f32[16,64,128]{2,1,0:T(8,128)} %slice.38), channel_id=1, source_target_pairs={{0,1},{1,2},{2,3},{3,4},{4,5},{5,6},{6,7},{8,9},{9,10},{10,11},{11... | collective-permute-start | bytes 1572872 | tf_op jit(solution)/shard_map/ppermute | solution.py:233
  6.1 30.2 %copy-start.2 = (f32[4,64,64]{2,1,0:T(8,128)S(1)}, f32[4,64,64]{2,1,0:T(8,128)}, u32[]{:S(2)}) copy-start(f32[4,64,64]{2,1,0:T(8,128)} %two_ref.1) | copy-start | bytes 196612
  6.1 42.7 %collective-permute-start.2 = (f32[6,64,512]{2,1,0:T(8,128)}, f32[6,64,512]{2,1,0:T(8,128)S(1)}, u32[]{:S(2)}, u32[]{:S(2)}) collective-permute-start(f32[6,64,512]{2,1,0:T(8,128)} %slice.41), channel_id=1, source_target_pairs={{0,8},{8,16},{16,24},{24,32},{32,40},{40,48},{48,56},{56,64},{64,7... | collective-permute-start | bytes 2359304 | tf_op jit(solution)/shard_map/ppermute | solution.py:231
  11.3 37.5 %collective-permute-start.3 = (f32[3,64,512]{2,1,0:T(8,128)}, f32[3,64,512]{2,1,0:T(8,128)}, u32[]{:S(2)}, u32[]{:S(2)}) collective-permute-start(f32[3,64,512]{2,1,0:T(8,128)} %slice.42), channel_id=1, source_target_pairs={{0,40},{8,48},{16,56},{24,0},{32,8},{40,16},{48,24},{56,32},{64,10... | collective-permute-start | bytes 1179656 | tf_op jit(solution)/shard_map/ppermute | solution.py:232
  22.0 3.5 %copy-start.5 = (f32[16,8]{1,0:T(8,128)}, f32[16,8]{1,0:T(8,128)S(1)}, u32[]{:S(2)}) copy-start(f32[16,8]{1,0:T(8,128)S(1)} %copy.11) | copy-start | bytes 1540
  27.7 8.5 %copy-start.3 = (f32[16,8]{1,0:T(8,128)S(1)}, f32[16,8]{1,0:T(8,128)}, u32[]{:S(2)}) copy-start(f32[16,8]{1,0:T(8,128)} %get-tuple-element.35.scale_ref) | copy-start | bytes 1540
  27.7 8.5 %copy-start.4 = (s32[16]{0:T(128)S(1)}, s32[16]{0:T(128)}, u32[]{:S(2)}) copy-start(s32[16]{0:T(128)} %get-tuple-element.31.offset_ref) | copy-start | bytes 196
  32.8 34.8 %collective-permute-start.1 = (f32[7,64,512]{2,1,0:T(8,128)S(1)}, f32[7,64,512]{2,1,0:T(8,128)S(1)}, u32[]{:S(2)}, u32[]{:S(2)}) collective-permute-start(f32[7,64,512]{2,1,0:T(8,128)S(1)} %sweep.4.own_ref), channel_id=1, source_target_pairs={{0,8},{8,16},{16,24},{24,32},{32,40},{40,48},{48,56},{56,64},{64,7... | collective-permute-start | bytes 2752520 | tf_op jit(solution)/shard_map/ppermute | solution.py:242
  49.7 8.0 %collective-permute-start.4 = (f32[9,64,128]{2,1,0:T(8,128)S(1)}, f32[9,64,128]{2,1,0:T(8,128)S(1)}, u32[]{:S(2)}, u32[]{:S(2)}) collective-permute-start(f32[9,64,128]{2,1,0:T(8,128)S(1)} %pad_maximum_fusion), channel_id=1, source_target_pairs={{0,1},{1,2},{2,3},{3,4},{4,5},{5,6},{6,7},{8,9},{9,10},{10,11},{11... | collective-permute-start | bytes 884744 | tf_op jit(solution)/shard_map/ppermute | solution.py:247
  62.0 25.7 %collective-permute-start.7 = (f32[6,64,512]{2,1,0:T(8,128)S(1)}, f32[6,64,512]{2,1,0:T(8,128)S(1)}, u32[]{:S(2)}, u32[]{:S(2)}) collective-permute-start(f32[6,64,512]{2,1,0:T(8,128)S(1)} %sweep.6.one_ref), channel_id=1, source_target_pairs={{0,8},{8,16},{16,24},{24,32},{32,40},{40,48},{48,56},{56,64},{64,7... | collective-permute-start | bytes 2359304 | tf_op jit(solution)/shard_map/ppermute | solution.py:249
  67.6 37.8 %collective-permute-start.5 = (f32[7,64,512]{2,1,0:T(8,128)S(1)}, f32[7,64,512]{2,1,0:T(8,128)S(1)}, u32[]{:S(2)}, u32[]{:S(2)}) collective-permute-start(f32[7,64,512]{2,1,0:T(8,128)S(1)} %collective-permute-done.1.one_ref), channel_id=1, source_target_pairs={{0,8},{8,16},{16,24},{24,32},{32,40},{40,48},{48,56},{56,64},{64,7... | collective-permute-start | bytes 2752520 | tf_op jit(solution)/shard_map/ppermute | solution.py:253
  69.5 23.1 %collective-permute-start.6 = (f32[3,64,512]{2,1,0:T(8,128)S(1)}, f32[3,64,512]{2,1,0:T(8,128)S(1)}, u32[]{:S(2)}, u32[]{:S(2)}) collective-permute-start(f32[3,64,512]{2,1,0:T(8,128)S(1)} %sweep.7), channel_id=1, source_target_pairs={{40,24},{48,32},{56,40},{0,48},{8,56},{16,64},{24,72},{32,80},{104... | collective-permute-start | bytes 1179656 | tf_op jit(solution)/shard_map/ppermute | solution.py:251
  92.7 15.3 %collective-permute-start.9 = (f32[3,64,512]{2,1,0:T(8,128)S(1)}, f32[3,64,512]{2,1,0:T(8,128)S(1)}, u32[]{:S(2)}, u32[]{:S(2)}) collective-permute-start(f32[3,64,512]{2,1,0:T(8,128)S(1)} %collective-permute-done.6), channel_id=1, source_target_pairs={{0,504},{8,0},{16,8},{24,16},{32,24},{40,32},{48,40},{56,48},{64,5... | collective-permute-start | bytes 1179656 | tf_op jit(solution)/shard_map/ppermute | solution.py:257
  99.1 16.0 %collective-permute-start.11 = (f32[6,24,512]{2,1,0:T(8,128)S(1)}, f32[6,24,512]{2,1,0:T(8,128)S(1)}, u32[]{:S(2)}, u32[]{:S(2)}) collective-permute-start(f32[6,24,512]{2,1,0:T(8,128)S(1)} %slice.47), channel_id=1, source_target_pairs={{0,8},{8,16},{16,24},{24,32},{32,40},{40,48},{48,56},{56,64},{64,7... | collective-permute-start | bytes 884744 | tf_op jit(solution)/shard_map/ppermute | solution.py:255
  108.0 14.6 %collective-permute-start.10 = (f32[3,64,512]{2,1,0:T(8,128)S(1)}, f32[3,64,512]{2,1,0:T(8,128)S(1)}, u32[]{:S(2)}, u32[]{:S(2)}) collective-permute-start(f32[3,64,512]{2,1,0:T(8,128)S(1)} %collective-permute-done.9.two_ref), channel_id=1, source_target_pairs={{0,504},{8,0},{16,8},{24,16},{32,24},{40,32},{48,40},{56,48},{64,5... | collective-permute-start | bytes 1179656 | tf_op jit(solution)/shard_map/ppermute | solution.py:261
  115.1 13.8 %collective-permute-start.8 = (f32[7,24,512]{2,1,0:T(8,128)S(1)}, f32[7,24,512]{2,1,0:T(8,128)S(1)}, u32[]{:S(2)}, u32[]{:S(2)}) collective-permute-start(f32[7,24,512]{2,1,0:T(8,128)S(1)} %slice.45), channel_id=1, source_target_pairs={{0,8},{8,16},{16,24},{24,32},{32,40},{40,48},{48,56},{56,64},{64,7... | collective-permute-start | bytes 1032200 | tf_op jit(solution)/shard_map/ppermute | solution.py:259

commit v4 on v3

v4 whole, which is shorter than its diff:
```python
import functools

import jax
import jax.numpy as jnp
from jax import lax
from jax.experimental import pallas as pl
from jax.experimental.pallas import tpu as pltpu
from jax.sharding import PartitionSpec as P

WBLK = 128
BETA = 0.5
RIM = 24
RING = 8
VMEM = 16 << 20


def cost(flops):
    return pl.CostEstimate(flops=flops, bytes_accessed=1, transcendentals=0)


def split(value):
    high = value.astype(jnp.bfloat16)
    return high, (value - high.astype(jnp.float32)).astype(jnp.bfloat16)


def band_of(distance, batch, band_ref, taps_ref):
    taps = taps_ref.shape[0]
    weights = [jnp.where(tap < band_ref[1, batch], taps_ref[tap, batch], 0.0) for tap in range(taps)]
    total = functools.reduce(lambda a, b: a + b, weights)
    inverse = 1.0 / jnp.full((1, distance.shape[1]), total, jnp.float32)
    matrix = jnp.zeros(distance.shape, jnp.float32)
    for tap in range(taps):
        matrix = jnp.where(distance == band_ref[0, batch] + tap, weights[tap], matrix)
    return matrix * inverse


def sweep_kernel(first, band_ref, taps_ref, field_ref, edge_ref, out_ref):
    batch = pl.program_id(0) + first
    rows = field_ref.shape[1]
    groups = field_ref.shape[2] // WBLK
    source = lax.broadcasted_iota(jnp.int32, (2 * WBLK, WBLK), 0)
    target = lax.broadcasted_iota(jnp.int32, (2 * WBLK, WBLK), 1)
    mat_high, mat_low = split(band_of(WBLK + target - source, batch, band_ref, taps_ref))
    pieces = [edge_ref[0]] + [field_ref[0, :, g * WBLK : (g + 1) * WBLK] for g in range(groups)]
    parts = [split(piece) for piece in pieces]

    def paired(which):
        pairs = [jnp.concatenate([parts[g][which], parts[g + 1][which]], axis=1) for g in range(groups)]
        return jnp.concatenate(pairs, axis=0)

    dot = functools.partial(jnp.dot, preferred_element_type=jnp.float32)
    both = dot(paired(0), jnp.concatenate([mat_high, mat_low], axis=1))
    moved = both[:, :WBLK] + both[:, WBLK:] + dot(paired(1), mat_high)
    for group in range(groups):
        out_ref[0, :, group * WBLK : (group + 1) * WBLK] = moved[group * rows : (group + 1) * rows]


def sweep(field, edge, band, taps, part, field_first, edge_first, flops=1):
    lo, hi = part
    _, rows, width = field.shape
    return pl.pallas_call(
        functools.partial(sweep_kernel, lo),
        grid_spec=pltpu.PrefetchScalarGridSpec(
            num_scalar_prefetch=2,
            grid=(hi - lo,),
            in_specs=[
                pl.BlockSpec((1, rows, width), lambda i, b, t: (i + field_first, 0, 0)),
                pl.BlockSpec((1, rows, WBLK), lambda i, b, t: (i + edge_first, 0, 0)),
            ],
            out_specs=pl.BlockSpec((1, rows, width), lambda i, b, t: (i, 0, 0)),
        ),
        out_shape=jax.ShapeDtypeStruct((hi - lo, rows, width), jnp.float32),
        compiler_params=pltpu.CompilerParams(vmem_limit_bytes=VMEM),
        cost_estimate=cost(flops),
        name="sweep",
    )(band, taps, field, edge)


def carve_kernel(early, back, margin, field_ref, early_ref, back_ref, edge_ref, sems):
    copies = (
        pltpu.make_async_copy(field_ref.at[early[0] : early[1]], early_ref, sems.at[0]),
        pltpu.make_async_copy(field_ref.at[back[0] : back[1]], back_ref, sems.at[1]),
        pltpu.make_async_copy(field_ref.at[:, :, margin:], edge_ref, sems.at[2]),
    )
    for copy in copies:
        copy.start()
    for copy in copies:
        copy.wait()


def carve(field, early, back, margin):
    batches, rows, width = field.shape
    shapes = ((early[1] - early[0], rows, width), (back[1] - back[0], rows, width), (batches, rows, width - margin))
    anywhere = pl.BlockSpec(memory_space=pl.ANY)
    return pl.pallas_call(
        functools.partial(carve_kernel, early, back, margin),
        in_specs=[anywhere],
        out_specs=[anywhere] * 3,
        out_shape=[jax.ShapeDtypeStruct(shape, jnp.float32) for shape in shapes],
        scratch_shapes=[pltpu.SemaphoreType.DMA((3,))],
        compiler_params=pltpu.CompilerParams(vmem_limit_bytes=58 << 20),
        cost_estimate=cost(1),
        name="carve",
    )(field)


def operator_kernel(me_ref, pair_ref, band_ref, taps_ref, own_ref, one_ref, two_ref, out_ref, turn_ref, base_ref):
    tile_len = own_ref.shape[1]
    batch = pl.program_id(0)

    @pl.when(batch == 0)
    def _():
        for below, ref in enumerate((own_ref, one_ref, two_ref)):
            present = (pair_ref[below, me_ref[0]] >= 0).astype(jnp.float32)
            turn_ref[:, below * tile_len : (below + 1) * tile_len] = ref[0].T * present
        column = lax.broadcasted_iota(jnp.int32, base_ref.shape, 1)
        row = lax.broadcasted_iota(jnp.int32, base_ref.shape, 0)
        tile_row, tile_col = row // tile_len, column // tile_len
        place_row = row % tile_len - tile_len * tile_row
        place_col = column % tile_len - tile_len * tile_col + jnp.where(tile_col == 3, tile_len - RIM, 0)
        base_ref[...] = jnp.where(me_ref[0] >= tile_col, place_row - place_col, -1)

    band_high, band_low = split(band_of(base_ref[...], batch, band_ref, taps_ref))
    turn_high, turn_low = split(turn_ref[...])
    dot = functools.partial(jnp.dot, preferred_element_type=jnp.float32)
    high, low = split(dot(turn_high, band_low) + dot(turn_low, band_high) + dot(turn_high, band_high))
    out_ref[0, :tile_len] = high
    out_ref[0, tile_len : 2 * tile_len] = band_high[:tile_len]
    out_ref[0, 2 * tile_len : 3 * tile_len] = low
    out_ref[0, 3 * tile_len :] = band_low[:tile_len]


def length_operator(me, pairs, band, taps, agg_kern):
    batches = taps.shape[1]
    tile_len = agg_kern.shape[1]
    depth = 3 * tile_len + RIM

    def pick(below):
        return pl.BlockSpec((1, tile_len, tile_len), lambda i, m, p, b, t: (jnp.maximum(p[below, m[0]], 0), 0, 0))

    return pl.pallas_call(
        operator_kernel,
        grid_spec=pltpu.PrefetchScalarGridSpec(
            num_scalar_prefetch=4,
            grid=(batches,),
            in_specs=[pick(0), pick(1), pick(2)],
            out_specs=pl.BlockSpec((1, 4 * tile_len, depth), lambda i, m, p, b, t: (i, 0, 0)),
            scratch_shapes=[
                pltpu.VMEM((tile_len, 3 * tile_len), jnp.float32),
                pltpu.VMEM((3 * tile_len, depth), jnp.int32),
            ],
        ),
        out_shape=jax.ShapeDtypeStruct((batches, 4 * tile_len, depth), jnp.bfloat16),
        compiler_params=pltpu.CompilerParams(vmem_limit_bytes=VMEM),
        cost_estimate=cost(1),
        name="operator",
    )(me, pairs, band, taps, agg_kern, agg_kern, agg_kern)


def finish_kernel(op_ref, own_ref, one_ref, two_ref, rim_ref, *rest):
    out_ref, high_ref, low_ref = rest[-3:]
    rows = own_ref.shape[1]
    at = 0
    for ref in (own_ref, one_ref, two_ref, rim_ref):
        high, low = split(ref[0])
        high_ref[at : at + ref.shape[1]] = high
        low_ref[at : at + ref.shape[1]] = low
        at += ref.shape[1]
    dot = functools.partial(jnp.dot, preferred_element_type=jnp.float32)
    four = dot(op_ref[0], high_ref[...])
    both = four[: 2 * rows] + four[2 * rows :] + dot(op_ref[0, : 2 * rows], low_ref[...])
    rate, spread = both[:rows], both[rows:]
    out_ref[0] = spread + BETA * (rate * rate / (1.0 + rate) - spread * rate)


def finish(operator, own, one, two, rim, part, total, before, own_first, flops):
    lo, hi = part
    count, rows, width = one.shape
    depth = operator.shape[2]
    here = lambda i: (i, 0, 0)
    in_specs = [
        pl.BlockSpec((1, operator.shape[1], depth), lambda i: (i + lo, 0, 0)),
        pl.BlockSpec((1, rows, width), lambda i: (i + own_first, 0, 0)),
        pl.BlockSpec((1, rows, width), here),
        pl.BlockSpec((1, rows, width), here),
        pl.BlockSpec((1, RIM, width), here),
    ]
    operands = [operator, own, one, two, rim]
    aliases = {}
    if before is not None:
        in_specs.append(pl.BlockSpec(memory_space=pl.ANY))
        operands.append(before)
        aliases = {5: 0}
    return pl.pallas_call(
        finish_kernel,
        grid=(count,),
        in_specs=in_specs,
        out_specs=pl.BlockSpec((1, rows, width), lambda i: (i + lo, 0, 0)),
        out_shape=jax.ShapeDtypeStruct((total, rows, width), jnp.float32),
        scratch_shapes=[pltpu.VMEM((depth, width), jnp.bfloat16)] * 2,
        input_output_aliases=aliases,
        compiler_params=pltpu.CompilerParams(vmem_limit_bytes=VMEM),
        cost_estimate=cost(flops),
        name="finish",
    )(*operands)


EARLY = (0, 6)
BACK = (6, 9)
LATE = (9, 16)
FIRST = (0, 9)


def after(value, *earlier):
    return lax.optimization_barrier((value,) + earlier)[0]


def shards(density, len_band, wid_band, len_taps, wid_taps, tile_pairs, agg_kern):
    batches, tile_len, group_width = density.shape
    tiles = lax.axis_size("len")
    groups = lax.axis_size("wid")
    margin = group_width - WBLK

    def spot(tile, step):
        return tile // RING * RING + (tile + step) % RING

    def move(pairs):
        return functools.partial(lax.ppermute, axis_name="len", perm=pairs)

    hop = move([(t, (t + 1) % tiles) for t in range(tiles)])
    unhop = move([(t, (t - 1) % tiles) for t in range(tiles)])
    back_three = move([(t, spot(t, -3)) for t in range(tiles)])
    back_five = move([(spot(t, -3), (t + 3) % tiles) for t in range(tiles)])
    side = functools.partial(lax.ppermute, axis_name="wid", perm=[(s, s + 1) for s in range(groups - 1)])
    wide = (wid_band, wid_taps.T)

    early, back, rim = carve(density, EARLY, BACK, margin)
    early_one_raw = hop(early)
    back_away_raw = back_three(back)
    edge = side(rim)

    late_own = sweep(density, edge, *wide, LATE, LATE[0], LATE[0], 1)
    late_one = hop(late_own)
    first_own = sweep(density, after(edge, late_own), *wide, FIRST, FIRST[0], FIRST[0], 1)
    early_one_raw, back_away_raw, first_own = lax.optimization_barrier((early_one_raw, back_away_raw, first_own))

    first_edge = side(jnp.concatenate([early_one_raw[:, :, margin:], back_away_raw[:, :, margin:]], axis=0))
    me = after(lax.axis_index("len")[None].astype(jnp.int32), first_own)
    operator = length_operator(me, tile_pairs.T, len_band, len_taps.T, agg_kern)
    first_edge = after(first_edge, operator)
    early_one = sweep(early_one_raw, first_edge, *wide, EARLY, 0, 0)
    early_two = hop(early_one)
    back_away = sweep(back_away_raw, after(first_edge, early_one), *wide, BACK, 0, EARLY[1])
    back_three_below = back_five(back_away)
    late_one = after(late_one, back_away)
    late_two = hop(late_one)
    early_two = after(early_two, late_one)
    early_rim = hop(early_two[:, tile_len - RIM :])
    back_three_below = after(back_three_below, early_two)
    back_two = unhop(back_three_below)
    late_two = after(late_two, back_three_below)
    late_rim = hop(late_two[:, tile_len - RIM :])
    back_two = after(back_two, late_two)
    back_one = unhop(back_two)

    early_rim = after(early_rim, back_two)
    out = finish(operator, first_own, early_one, early_two, early_rim, EARLY, batches, None, 0, 1000000000)
    out = finish(operator, late_own, late_one, late_two, late_rim, LATE, batches, out, 0, 1000000000)
    back_rim = back_three_below[:, tile_len - RIM :]
    return finish(operator, first_own, back_one, back_two, back_rim, BACK, batches, out, EARLY[1], 1)


def solution(mesh):
    in_specs = (P(None, "len", "wid"), P(), P(), P(), P(), P(), P())
    out_specs = P(None, "len", "wid")
    return jax.shard_map(shards, mesh=mesh, in_specs=in_specs, out_specs=out_specs, check_vma=False)
```

time: 133 us -> 176 us (1.32)
  Pallas kernels: 33.8 us -> 79.6 us
  local copies, waits for them, and re-layouts: 9.45 us -> 0.84 us
  starting transfers between devices: 51.6 us -> 56.7 us
  waiting for transfers between devices: 34.3 us -> 37.5 us
  other arithmetic: 3.18 us -> 0.73 us
    pallas_call x5 -> x6, Pallas kernels: 25.2 us -> 69.1 us  [the longest x1 52.7 us: carve(): pl.pallas_call(functools.partial(carve_kernel, early, back, margin), in_s...]
    ppermute x3, waiting for transfers between devices: 0.01 us -> 15.6 us  [the longest x1 15.6 us: shards(): back_away_raw = back_three(back)]
    ppermute x1, waiting for transfers between devices: 5.37 us -> 0.01 us  [shards(): side(jnp.concatenate([early_one_raw[:, :, margin:], back_away_raw[:, :, m...]
    slice x4 -> x1, local copies, waits for them, and re-layouts: 4.92 us -> 0.01 us  [shards(): back_rim = back_three_below[:, tile_len - RIM:]]
    ppermute x1, starting transfers between devices: 6.41 us -> 11 us  [shards(): back_two = unhop(back_three_below)]
    ppermute x1, waiting for transfers between devices: 4.98 us -> 1 us  [shards(): back_three_below = back_five(back_away)]
    ppermute x1, waiting for transfers between devices: 2.4 us -> 0.01 us  [shards(): back_one = unhop(back_two)]
    ppermute x1, starting transfers between devices: 7.6 us -> 5.56 us  [shards(): back_three_below = back_five(back_away)]
  transfers between devices with their start and end apart: 12 -> 12, of which waited for: 7 -> 6; matrix products, arithmetic and copies ran while one was open for 8% -> 0% of each run, Pallas kernels for 23% -> 14%
where the time goes in v4:
time: 176 us
  Pallas kernels  79.6 us (45%)
  starting transfers between devices  56.7 us (32%)
  waiting for transfers between devices  37.5 us (21%)
    pallas_call x1, Pallas kernels, carve(): pl.pallas_call(functools.partial(carve_kernel, early, back, margin), in_s...  52.7 us
    ppermute x1, waiting for transfers between devices, shards(): back_away_raw = back_three(back)  15.6 us
    ppermute x1, waiting for transfers between devices, shards(): early_two = hop(early_one)  12 us
    ppermute x1, starting transfers between devices, shards(): back_two = unhop(back_three_below)  11 us
    pallas_call x3, Pallas kernels, finish(): pl.pallas_call(finish_kernel, grid=(count,), in_specs=in_specs, out_specs...  10.5 us
    pallas_call x4, Pallas kernels, sweep(): pl.pallas_call(functools.partial(sweep_kernel, lo), grid_spec=pltpu.Prefe...  10.2 us
    ppermute x1, starting transfers between devices, shards(): back_away_raw = back_three(back)  10 us
    ppermute x1, starting transfers between devices, shards(): back_one = unhop(back_two)  6.69 us
  transfers between devices with their start and end apart: 12, of which 6 were waited for; matrix products, arithmetic and copies ran while one was open for 0% of the time, Pallas kernels for 14%

profile of v4, /device:TPU:2, one launch (start us, length us, event | category | flops | bytes accessed | tf_op | source)
XLA Modules:
  0.0 175.7 jit_solution(12506749318988318094)
XLA Ops:
  0.0 52.7 %carve.1 = (f32[6,64,512]{2,1,0:T(8,128)}, f32[3,64,512]{2,1,0:T(8,128)}, f32[16,64,128]{2,1,0:T(8,128)}) custom-call(f32[16,64,512]{2,1,0:T(8,128)} %field_ref.5), custom_call_target="tpu_custom_call" | custom-call | flops 1 | bytes 1 | tf_op jit(solution)/shard_map/carve/pallas_call | solution.py:95
  52.8 1.9 %collective-permute-start.2 = (f32[16,64,128]{2,1,0:T(8,128)}, f32[16,64,128]{2,1,0:T(8,128)S(1)}, u32[]{:S(2)}, u32[]{:S(2)}) collective-permute-start(f32[16,64,128]{2,1,0:T(8,128)} %get-tuple-element.23), channel_id=1, source_target_pairs={{0,1},{1,2},{2,3},{3,4},{4,5},{5,6},{6,7},{8,9},{9,10},{10,11},{11... | collective-permute-start | bytes 1572872 | tf_op jit(solution)/shard_map/ppermute | solution.py:240
  54.7 4.3 %collective-permute-start = (f32[6,64,512]{2,1,0:T(8,128)}, f32[6,64,512]{2,1,0:T(8,128)S(1)}, u32[]{:S(2)}, u32[]{:S(2)}) collective-permute-start(f32[6,64,512]{2,1,0:T(8,128)} %get-tuple-element.21), channel_id=1, source_target_pairs={{0,8},{8,16},{16,24},{24,32},{32,40},{40,48},{48,56},{56,64},{64,7... | collective-permute-start | bytes 2359304 | tf_op jit(solution)/shard_map/ppermute | solution.py:238
  59.0 10.0 %collective-permute-start.1 = (f32[3,64,512]{2,1,0:T(8,128)}, f32[3,64,512]{2,1,0:T(8,128)S(1)}, u32[]{:S(2)}, u32[]{:S(2)}) collective-permute-start(f32[3,64,512]{2,1,0:T(8,128)} %get-tuple-element.22), channel_id=1, source_target_pairs={{0,40},{8,48},{16,56},{24,0},{32,8},{40,16},{48,24},{56,32},{64,10... | collective-permute-start | bytes 1179656 | tf_op jit(solution)/shard_map/ppermute | solution.py:239
  69.1 2.8 %sweep.4.own_ref = f32[7,64,512]{2,1,0:T(8,128)S(1)} custom-call(s32[2,16]{1,0:T(2,128)S(1)} %copy-done.5, f32[8,16]{1,0:T(8,128)S(1)} %bitcast.4, f32[16,64,512]{2,1,0:T(8,128)S(1)} %copy-done, f32[16,64,128]{2,1,0:T(8,128)S(1)} %collective-permute-done.2.edge_ref), custom_call_target="tpu_custom_call" | custom-call | flops 1 | bytes 1 | tf_op jit(solution)/shard_map/sweep/pallas_call | solution.py:61
  71.9 3.5 %collective-permute-start.6 = (f32[7,64,512]{2,1,0:T(8,128)S(1)}, f32[7,64,512]{2,1,0:T(8,128)}, u32[]{:S(2)}, u32[]{:S(2)}) collective-permute-start(f32[7,64,512]{2,1,0:T(8,128)S(1)} %sweep.4.own_ref), channel_id=1, source_target_pairs={{0,8},{8,16},{16,24},{24,32},{32,40},{40,48},{48,56},{56,64},{64,7... | collective-permute-start | bytes 2752520 | tf_op jit(solution)/shard_map/ppermute | solution.py:243
  75.4 3.4 %sweep.5.own_ref = f32[9,64,512]{2,1,0:T(8,128)S(1)} custom-call(s32[2,16]{1,0:T(2,128)S(1)} %copy-done.5, f32[8,16]{1,0:T(8,128)S(1)} %bitcast.5, f32[16,64,512]{2,1,0:T(8,128)S(1)} %copy-done, f32[16,64,128]{2,1,0:T(8,128)S(1)} %collective-permute-done.2.edge_ref), custom_call_target="tpu_custom_call" | custom-call | flops 1 | bytes 1 | tf_op jit(solution)/shard_map/sweep/pallas_call | solution.py:61
  78.8 15.6 %collective-permute-done.1.field_ref = f32[3,64,512]{2,1,0:T(8,128)S(1)} collective-permute-done((f32[3,64,512]{2,1,0:T(8,128)}, f32[3,64,512]{2,1,0:T(8,128)S(1)}, u32[]{:S(2)}, u32[]{:S(2)}) %collective-permute-start.1) | collective-permute-done | bytes 393248 | tf_op jit(solution)/shard_map/ppermute | solution.py:239
  95.9 3.3 %collective-permute-start.3 = (f32[9,64,128]{2,1,0:T(8,128)}, f32[9,64,128]{2,1,0:T(8,128)S(1)}, u32[]{:S(2)}, u32[]{:S(2)}) collective-permute-start(f32[9,64,128]{2,1,0:T(8,128)} %pad_maximum_fusion), channel_id=1, source_target_pairs={{0,1},{1,2},{2,3},{3,4},{4,5},{5,6},{6,7},{8,9},{9,10},{10,11},{11... | collective-permute-start | bytes 884744 | tf_op jit(solution)/shard_map/ppermute | solution.py:247
  99.3 6.1 %operator.1.op_ref = bf16[16,256,216]{2,1,0:T(8,128)(2,1)S(1)} custom-call(s32[1]{0:T(128)} %bitcast.me_ref, s32[3,64]{1,0:T(4,128)S(1)} %bitcast.9, s32[2,16]{1,0:T(2,128)S(1)} %copy-done.8, f32[8,16]{1,0:T(8,128)S(1)} %bitcast.8, f32[4,64,64]{2,1,0:T(8,128)S(1)} %copy-done.1, f32[4,64,64]{2,1,0:T(8,128)S(1)} %copy-done.1, f32[4,64,64]{2,1,0:T(8,128)S(1)} %copy-done.1), custom_call_target="tpu_custom_call" | custom-call | flops 1 | bytes 1 | tf_op jit(solution)/shard_map/operator/pallas_call | solution.py:141
  105.4 2.5 %sweep.6.one_ref = f32[6,64,512]{2,1,0:T(8,128)S(1)} custom-call(s32[2,16]{1,0:T(2,128)S(1)} %copy-done.5, f32[8,16]{1,0:T(8,128)S(1)} %bitcast.6, f32[6,64,512]{2,1,0:T(8,128)S(1)} %collective-permute-done.field_ref, f32[9,64,128]{2,1,0:T(8,128)S(1)} %collective-permute-done.3.edge_ref), custom_call_target="tpu_custom_call" | custom-call | flops 1 | bytes 1 | tf_op jit(solution)/shard_map/sweep/pallas_call | solution.py:61
  107.9 2.1 %collective-permute-start.5 = (f32[6,64,512]{2,1,0:T(8,128)S(1)}, f32[6,64,512]{2,1,0:T(8,128)S(1)}, u32[]{:S(2)}, u32[]{:S(2)}) collective-permute-start(f32[6,64,512]{2,1,0:T(8,128)S(1)} %sweep.6.one_ref), channel_id=1, source_target_pairs={{0,8},{8,16},{16,24},{24,32},{32,40},{40,48},{48,56},{56,64},{64,7... | collective-permute-start | bytes 2359304 | tf_op jit(solution)/shard_map/ppermute | solution.py:252
  111.6 3.8 %collective-permute-start.8 = (f32[7,64,512]{2,1,0:T(8,128)}, f32[7,64,512]{2,1,0:T(8,128)S(1)}, u32[]{:S(2)}, u32[]{:S(2)}) collective-permute-start(f32[7,64,512]{2,1,0:T(8,128)} %collective-permute-done.6.one_ref), channel_id=1, source_target_pairs={{0,8},{8,16},{16,24},{24,32},{32,40},{40,48},{48,56},{56,64},{64,7... | collective-permute-start | bytes 2752520 | tf_op jit(solution)/shard_map/ppermute | solution.py:256
  115.4 5.6 %collective-permute-start.4 = (f32[3,64,512]{2,1,0:T(8,128)S(1)}, f32[3,64,512]{2,1,0:T(8,128)S(1)}, u32[]{:S(2)}, u32[]{:S(2)}) collective-permute-start(f32[3,64,512]{2,1,0:T(8,128)S(1)} %sweep.7), channel_id=1, source_target_pairs={{40,24},{48,32},{56,40},{0,48},{8,56},{16,64},{24,72},{32,80},{104... | collective-permute-start | bytes 1179656 | tf_op jit(solution)/shard_map/ppermute | solution.py:254
  121.0 12.0 %collective-permute-done.5.two_ref = f32[6,64,512]{2,1,0:T(8,128)S(1)} collective-permute-done((f32[6,64,512]{2,1,0:T(8,128)S(1)}, f32[6,64,512]{2,1,0:T(8,128)S(1)}, u32[]{:S(2)}, u32[]{:S(2)}) %collective-permute-start.5) | collective-permute-done | bytes 786464 | tf_op jit(solution)/shard_map/ppermute | solution.py:252
  134.0 11.0 %collective-permute-start.7 = (f32[3,64,512]{2,1,0:T(8,128)S(1)}, f32[3,64,512]{2,1,0:T(8,128)S(1)}, u32[]{:S(2)}, u32[]{:S(2)}) collective-permute-start(f32[3,64,512]{2,1,0:T(8,128)S(1)} %collective-permute-done.4), channel_id=1, source_target_pairs={{0,504},{8,0},{16,8},{24,16},{32,24},{40,32},{48,40},{56,48},{64,5... | collective-permute-start | bytes 1179656 | tf_op jit(solution)/shard_map/ppermute | solution.py:260
  145.1 2.6 %collective-permute-start.11 = (f32[6,24,512]{2,1,0:T(8,128)S(1)}, f32[6,24,512]{2,1,0:T(8,128)S(1)}, u32[]{:S(2)}, u32[]{:S(2)}) collective-permute-start(f32[6,24,512]{2,1,0:T(8,128)S(1)} %slice.19), channel_id=1, source_target_pairs={{0,8},{8,16},{16,24},{24,32},{32,40},{40,48},{48,56},{56,64},{64,7... | collective-permute-start | bytes 884744 | tf_op jit(solution)/shard_map/ppermute | solution.py:258
  147.6 5.0 %collective-permute-done.8.two_ref = f32[7,64,512]{2,1,0:T(8,128)S(1)} collective-permute-done((f32[7,64,512]{2,1,0:T(8,128)}, f32[7,64,512]{2,1,0:T(8,128)S(1)}, u32[]{:S(2)}, u32[]{:S(2)}) %collective-permute-start.8) | collective-permute-done | bytes 917536 | tf_op jit(solution)/shard_map/ppermute | solution.py:256
  152.7 1.9 %collective-permute-start.10 = (f32[7,24,512]{2,1,0:T(8,128)S(1)}, f32[7,24,512]{2,1,0:T(8,128)S(1)}, u32[]{:S(2)}, u32[]{:S(2)}) collective-permute-start(f32[7,24,512]{2,1,0:T(8,128)S(1)} %slice.18), channel_id=1, source_target_pairs={{0,8},{8,16},{16,24},{24,32},{32,40},{40,48},{48,56},{56,64},{64,7... | collective-permute-start | bytes 1032200 | tf_op jit(solution)/shard_map/ppermute | solution.py:262
  155.2 6.7 %collective-permute-start.9 = (f32[3,64,512]{2,1,0:T(8,128)S(1)}, f32[3,64,512]{2,1,0:T(8,128)S(1)}, u32[]{:S(2)}, u32[]{:S(2)}) collective-permute-start(f32[3,64,512]{2,1,0:T(8,128)S(1)} %collective-permute-done.7.two_ref), channel_id=1, source_target_pairs={{0,504},{8,0},{16,8},{24,16},{32,24},{40,32},{48,40},{56,48},{64,5... | collective-permute-start | bytes 1179656 | tf_op jit(solution)/shard_map/ppermute | solution.py:264
  161.9 3.1 %finish.3.rest_0_ = f32[16,64,512]{2,1,0:T(8,128)} custom-call(bf16[16,256,216]{2,1,0:T(8,128)(2,1)S(1)} %operator.1.op_ref, f32[9,64,512]{2,1,0:T(8,128)S(1)} %sweep.5.own_ref, f32[6,64,512]{2,1,0:T(8,128)S(1)} %sweep.6.one_ref, f32[6,64,512]{2,1,0:T(8,128)S(1)} %collective-permute-done.5.two_ref, f32[6,24,512]{2,1,0:T(8,128)S(1)} %collective-permute-done.11.rim_ref), custom_call_target="tpu_custom_call" | custom-call | flops 1000000000 | bytes 1 | tf_op jit(solution)/shard_map/finish/pallas_call | solution.py:194
  165.0 3.3 %collective-permute-done.10.rim_ref = f32[7,24,512]{2,1,0:T(8,128)S(1)} collective-permute-done((f32[7,24,512]{2,1,0:T(8,128)S(1)}, f32[7,24,512]{2,1,0:T(8,128)S(1)}, u32[]{:S(2)}, u32[]{:S(2)}) %collective-permute-start.10) | collective-permute-done | bytes 344096 | tf_op jit(solution)/shard_map/ppermute | solution.py:262
  168.3 5.6 %finish.4.rest_0_ = f32[16,64,512]{2,1,0:T(8,128)} custom-call(bf16[16,256,216]{2,1,0:T(8,128)(2,1)S(1)} %operator.1.op_ref, f32[7,64,512]{2,1,0:T(8,128)S(1)} %sweep.4.own_ref, f32[7,64,512]{2,1,0:T(8,128)} %collective-permute-done.6.one_ref, f32[7,64,512]{2,1,0:T(8,128)S(1)} %collective-permute-done.8.two_ref, ...), custom_call_target="tpu_custom_call", output_to_operand_aliasing={{}: (5, {})} | custom-call | flops 1000000000 | bytes 1 | tf_op jit(solution)/shard_map/finish/pallas_call | solution.py:194
  173.9 1.9 %finish.5 = f32[16,64,512]{2,1,0:T(8,128)} custom-call(bf16[16,256,216]{2,1,0:T(8,128)(2,1)S(1)} %operator.1.op_ref, f32[9,64,512]{2,1,0:T(8,128)S(1)} %sweep.5.own_ref, f32[3,64,512]{2,1,0:T(8,128)S(1)} %collective-permute-done.9.one_ref, f32[3,64,512]{2,1,0:T(8,128)S(1)} %collective-permute-done.7.two_ref, ...), custom_call_target="tpu_custom_call", output_to_operand_aliasing={{}: (5, {})} | custom-call | flops 1 | bytes 1 | tf_op jit(solution)/shard_map/finish/pallas_call | solution.py:194
  (33 shorter events, 4.7 us)
Async XLA Ops:
  0.0 69.0 %copy-start = (f32[16,64,512]{2,1,0:T(8,128)S(1)}, f32[16,64,512]{2,1,0:T(8,128)}, u32[]{:S(2)}) copy-start(f32[16,64,512]{2,1,0:T(8,128)} %field_ref.5) | copy-start | bytes 6291460
  0.0 69.0 %copy-start.5 = (s32[2,16]{1,0:T(2,128)S(1)}, s32[2,16]{1,0:T(2,128)}, u32[]{:S(2)}) copy-start(s32[2,16]{1,0:T(2,128)} %band_ref.9) | copy-start | bytes 388
  0.0 69.0 %copy-start.4 = (f32[16,8]{0,1:T(8,128)S(1)}, f32[16,8]{0,1:T(8,128)}, u32[]{:S(2)}) copy-start(f32[16,8]{0,1:T(8,128)} %param.11) | copy-start | bytes 1540
  52.8 16.3 %collective-permute-start.2 = (f32[16,64,128]{2,1,0:T(8,128)}, f32[16,64,128]{2,1,0:T(8,128)S(1)}, u32[]{:S(2)}, u32[]{:S(2)}) collective-permute-start(f32[16,64,128]{2,1,0:T(8,128)} %get-tuple-element.23), channel_id=1, source_target_pairs={{0,1},{1,2},{2,3},{3,4},{4,5},{5,6},{6,7},{8,9},{9,10},{10,11},{11... | collective-permute-start | bytes 1572872 | tf_op jit(solution)/shard_map/ppermute | solution.py:240
  54.7 39.8 %collective-permute-start = (f32[6,64,512]{2,1,0:T(8,128)}, f32[6,64,512]{2,1,0:T(8,128)S(1)}, u32[]{:S(2)}, u32[]{:S(2)}) collective-permute-start(f32[6,64,512]{2,1,0:T(8,128)} %get-tuple-element.21), channel_id=1, source_target_pairs={{0,8},{8,16},{16,24},{24,32},{32,40},{40,48},{48,56},{56,64},{64,7... | collective-permute-start | bytes 2359304 | tf_op jit(solution)/shard_map/ppermute | solution.py:238
  59.0 35.5 %collective-permute-start.1 = (f32[3,64,512]{2,1,0:T(8,128)}, f32[3,64,512]{2,1,0:T(8,128)S(1)}, u32[]{:S(2)}, u32[]{:S(2)}) collective-permute-start(f32[3,64,512]{2,1,0:T(8,128)} %get-tuple-element.22), channel_id=1, source_target_pairs={{0,40},{8,48},{16,56},{24,0},{32,8},{40,16},{48,24},{56,32},{64,10... | collective-permute-start | bytes 1179656 | tf_op jit(solution)/shard_map/ppermute | solution.py:239
  71.8 27.4 %copy-start.1 = (f32[4,64,64]{2,1,0:T(8,128)S(1)}, f32[4,64,64]{2,1,0:T(8,128)}, u32[]{:S(2)}) copy-start(f32[4,64,64]{2,1,0:T(8,128)} %two_ref.1) | copy-start | bytes 196612
  71.9 27.4 %copy-start.6 = (f32[16,8]{0,1:T(8,128)S(1)}, f32[16,8]{0,1:T(8,128)}, u32[]{:S(2)}) copy-start(f32[16,8]{0,1:T(8,128)} %param.10) | copy-start | bytes 1540
  71.9 27.4 %copy-start.7 = (s32[64,3]{0,1:T(4,128)S(1)}, s32[64,3]{0,1:T(4,128)}, u32[]{:S(2)}) copy-start(s32[64,3]{0,1:T(4,128)} %param.12) | copy-start | bytes 2308
  71.9 27.4 %copy-start.8 = (s32[2,16]{1,0:T(2,128)S(1)}, s32[2,16]{1,0:T(2,128)}, u32[]{:S(2)}) copy-start(s32[2,16]{1,0:T(2,128)} %band_ref.7) | copy-start | bytes 388
  71.9 39.7 %collective-permute-start.6 = (f32[7,64,512]{2,1,0:T(8,128)S(1)}, f32[7,64,512]{2,1,0:T(8,128)}, u32[]{:S(2)}, u32[]{:S(2)}) collective-permute-start(f32[7,64,512]{2,1,0:T(8,128)S(1)} %sweep.4.own_ref), channel_id=1, source_target_pairs={{0,8},{8,16},{16,24},{24,32},{32,40},{40,48},{48,56},{56,64},{64,7... | collective-permute-start | bytes 2752520 | tf_op jit(solution)/shard_map/ppermute | solution.py:243
  94.5 0.8 copy-start.2
  95.9 9.5 %collective-permute-start.3 = (f32[9,64,128]{2,1,0:T(8,128)}, f32[9,64,128]{2,1,0:T(8,128)S(1)}, u32[]{:S(2)}, u32[]{:S(2)}) collective-permute-start(f32[9,64,128]{2,1,0:T(8,128)} %pad_maximum_fusion), channel_id=1, source_target_pairs={{0,1},{1,2},{2,3},{3,4},{4,5},{5,6},{6,7},{8,9},{9,10},{10,11},{11... | collective-permute-start | bytes 884744 | tf_op jit(solution)/shard_map/ppermute | solution.py:247
  99.3 10.7 %copy-start.3 = (f32[3,64,512]{2,1,0:T(8,128)S(1)}, f32[3,64,512]{2,1,0:T(8,128)}, u32[]{:S(2)}) copy-start(f32[3,64,512]{2,1,0:T(8,128)} %copy-done.2) | copy-start | bytes 1179652
  107.9 25.1 %collective-permute-start.5 = (f32[6,64,512]{2,1,0:T(8,128)S(1)}, f32[6,64,512]{2,1,0:T(8,128)S(1)}, u32[]{:S(2)}, u32[]{:S(2)}) collective-permute-start(f32[6,64,512]{2,1,0:T(8,128)S(1)} %sweep.6.one_ref), channel_id=1, source_target_pairs={{0,8},{8,16},{16,24},{24,32},{32,40},{40,48},{48,56},{56,64},{64,7... | collective-permute-start | bytes 2359304 | tf_op jit(solution)/shard_map/ppermute | solution.py:252
  111.6 41.0 %collective-permute-start.8 = (f32[7,64,512]{2,1,0:T(8,128)}, f32[7,64,512]{2,1,0:T(8,128)S(1)}, u32[]{:S(2)}, u32[]{:S(2)}) collective-permute-start(f32[7,64,512]{2,1,0:T(8,128)} %collective-permute-done.6.one_ref), channel_id=1, source_target_pairs={{0,8},{8,16},{16,24},{24,32},{32,40},{40,48},{48,56},{56,64},{64,7... | collective-permute-start | bytes 2752520 | tf_op jit(solution)/shard_map/ppermute | solution.py:256
  115.4 18.6 %collective-permute-start.4 = (f32[3,64,512]{2,1,0:T(8,128)S(1)}, f32[3,64,512]{2,1,0:T(8,128)S(1)}, u32[]{:S(2)}, u32[]{:S(2)}) collective-permute-start(f32[3,64,512]{2,1,0:T(8,128)S(1)} %sweep.7), channel_id=1, source_target_pairs={{40,24},{48,32},{56,40},{0,48},{8,56},{16,64},{24,72},{32,80},{104... | collective-permute-start | bytes 1179656 | tf_op jit(solution)/shard_map/ppermute | solution.py:254
  134.0 21.2 %collective-permute-start.7 = (f32[3,64,512]{2,1,0:T(8,128)S(1)}, f32[3,64,512]{2,1,0:T(8,128)S(1)}, u32[]{:S(2)}, u32[]{:S(2)}) collective-permute-start(f32[3,64,512]{2,1,0:T(8,128)S(1)} %collective-permute-done.4), channel_id=1, source_target_pairs={{0,504},{8,0},{16,8},{24,16},{32,24},{40,32},{48,40},{56,48},{64,5... | collective-permute-start | bytes 1179656 | tf_op jit(solution)/shard_map/ppermute | solution.py:260
  145.1 16.8 %collective-permute-start.11 = (f32[6,24,512]{2,1,0:T(8,128)S(1)}, f32[6,24,512]{2,1,0:T(8,128)S(1)}, u32[]{:S(2)}, u32[]{:S(2)}) collective-permute-start(f32[6,24,512]{2,1,0:T(8,128)S(1)} %slice.19), channel_id=1, source_target_pairs={{0,8},{8,16},{16,24},{24,32},{32,40},{40,48},{48,56},{56,64},{64,7... | collective-permute-start | bytes 884744 | tf_op jit(solution)/shard_map/ppermute | solution.py:258
  152.7 15.6 %collective-permute-start.10 = (f32[7,24,512]{2,1,0:T(8,128)S(1)}, f32[7,24,512]{2,1,0:T(8,128)S(1)}, u32[]{:S(2)}, u32[]{:S(2)}) collective-permute-start(f32[7,24,512]{2,1,0:T(8,128)S(1)} %slice.18), channel_id=1, source_target_pairs={{0,8},{8,16},{16,24},{24,32},{32,40},{40,48},{48,56},{56,64},{64,7... | collective-permute-start | bytes 1032200 | tf_op jit(solution)/shard_map/ppermute | solution.py:262
  155.2 18.7 %collective-permute-start.9 = (f32[3,64,512]{2,1,0:T(8,128)S(1)}, f32[3,64,512]{2,1,0:T(8,128)S(1)}, u32[]{:S(2)}, u32[]{:S(2)}) collective-permute-start(f32[3,64,512]{2,1,0:T(8,128)S(1)} %collective-permute-done.7.two_ref), channel_id=1, source_target_pairs={{0,504},{8,0},{16,8},{24,16},{32,24},{40,32},{48,40},{56,48},{64,5... | collective-permute-start | bytes 1179656 | tf_op jit(solution)/shard_map/ppermute | solution.py:264

commit v5 on v4

--- a/solution.py
+++ b/solution.py
@@ -76,29 +76,19 @@
     )(band, taps, field, edge)
 
 
-def carve_kernel(early, back, margin, field_ref, early_ref, back_ref, edge_ref, sems):
-    copies = (
-        pltpu.make_async_copy(field_ref.at[early[0] : early[1]], early_ref, sems.at[0]),
-        pltpu.make_async_copy(field_ref.at[back[0] : back[1]], back_ref, sems.at[1]),
-        pltpu.make_async_copy(field_ref.at[:, :, margin:], edge_ref, sems.at[2]),
-    )
-    for copy in copies:
-        copy.start()
-    for copy in copies:
-        copy.wait()
+def carve_kernel(early, back, margin, field_ref, early_ref, back_ref, edge_ref):
+    early_ref[...] = field_ref[early[0] : early[1]]
+    back_ref[...] = field_ref[back[0] : back[1]]
+    edge_ref[...] = field_ref[:, :, margin:]
 
 
 def carve(field, early, back, margin):
     batches, rows, width = field.shape
     shapes = ((early[1] - early[0], rows, width), (back[1] - back[0], rows, width), (batches, rows, width - margin))
-    anywhere = pl.BlockSpec(memory_space=pl.ANY)
     return pl.pallas_call(
         functools.partial(carve_kernel, early, back, margin),
-        in_specs=[anywhere],
-        out_specs=[anywhere] * 3,
         out_shape=[jax.ShapeDtypeStruct(shape, jnp.float32) for shape in shapes],
-        scratch_shapes=[pltpu.SemaphoreType.DMA((3,))],
-        compiler_params=pltpu.CompilerParams(vmem_limit_bytes=58 << 20),
+        compiler_params=pltpu.CompilerParams(vmem_limit_bytes=VMEM),
         cost_estimate=cost(1),
         name="carve",
     )(field)
@@ -229,14 +219,14 @@
 
     hop = move([(t, (t + 1) % tiles) for t in range(tiles)])
     unhop = move([(t, (t - 1) % tiles) for t in range(tiles)])
-    back_three = move([(t, spot(t, -3)) for t in range(tiles)])
-    back_five = move([(spot(t, -3), (t + 3) % tiles) for t in range(tiles)])
+    back_first = move([(t, spot(t, -2)) for t in range(tiles)])
+    back_rest = move([(spot(t, -2), (t + 3) % tiles) for t in range(tiles)])
     side = functools.partial(lax.ppermute, axis_name="wid", perm=[(s, s + 1) for s in range(groups - 1)])
     wide = (wid_band, wid_taps.T)
 
     early, back, rim = carve(density, EARLY, BACK, margin)
     early_one_raw = hop(early)
-    back_away_raw = back_three(back)
+    back_away_raw = back_first(back)
     edge = side(rim)
 
     late_own = sweep(density, edge, *wide, LATE, LATE[0], LATE[0], 1)
@@ -251,7 +241,7 @@
     early_one = sweep(early_one_raw, first_edge, *wide, EARLY, 0, 0)
     early_two = hop(early_one)
     back_away = sweep(back_away_raw, after(first_edge, early_one), *wide, BACK, 0, EARLY[1])
-    back_three_below = back_five(back_away)
+    back_three_below = back_rest(back_away)
     late_one = after(late_one, back_away)
     late_two = hop(late_one)
     early_two = after(early_two, late_one)

time: 176 us -> 125 us (0.71)
  Pallas kernels: 79.6 us -> 27 us
  starting transfers between devices: 56.7 us -> 46 us
  waiting for transfers between devices: 37.5 us -> 47.5 us
    pallas_call x1, Pallas kernels: 52.7 us -> 0.11 us  [carve(): pl.pallas_call(functools.partial(carve_kernel, early, back, margin), out_...]
    ppermute x2, waiting for transfers between devices: 16.6 us -> 25 us  [the longest x1 16.1 us: shards(): back_three_below = back_rest(back_away)]
    ppermute x1, starting transfers between devices: 11 us -> 5.17 us  [shards(): back_two = unhop(back_three_below)]
    ppermute x1, waiting for transfers between devices: 5.02 us -> 0.01 us  [shards(): late_two = hop(late_one)]
    ppermute x1, waiting for transfers between devices: 0.56 us -> 4.62 us  [shards(): back_two = unhop(back_three_below)]
    ppermute x1, waiting for transfers between devices: 0.01 us -> 2.87 us  [shards(): late_one = hop(late_own)]
    ppermute x1, starting transfers between devices: 3.78 us -> 1.91 us  [shards(): late_two = hop(late_one)]
  transfers between devices with their start and end apart: 12 -> 12, of which waited for: 6 -> 6; matrix products, arithmetic and copies ran while one was open for 0% -> 1% of each run, Pallas kernels for 14% -> 20%
where the time goes in v5:
time: 125 us; the launch traced here: 124 us
  waiting for transfers between devices  47.5 us (38%)
  starting transfers between devices  46 us (37%)
  Pallas kernels  27 us (22%)
  local copies, waits for them, and re-layouts  2.42 us (2%)
    ppermute x1, waiting for transfers between devices, shards(): back_three_below = back_rest(back_away)  16.1 us
    ppermute x1, waiting for transfers between devices, shards(): early_two = hop(early_one)  13.1 us
    pallas_call x3, Pallas kernels, finish(): pl.pallas_call(finish_kernel, grid=(count,), in_specs=in_specs, out_specs...  10.5 us
    pallas_call x4, Pallas kernels, sweep(): pl.pallas_call(functools.partial(sweep_kernel, lo), grid_spec=pltpu.Prefe...  10.2 us
    ppermute x1, starting transfers between devices, shards(): back_away_raw = back_first(back)  10 us
    ppermute x1, waiting for transfers between devices, shards(): back_away_raw = back_first(back)  8.98 us
    ppermute x1, starting transfers between devices, shards(): back_one = unhop(back_two)  7.7 us
    pallas_call x1, Pallas kernels, length_operator(): pl.pallas_call(operator_kernel, grid_spec=pltpu.PrefetchScalarGridSpec(nu...  6.11 us
  transfers between devices with their start and end apart: 12, of which 6 were waited for; matrix products, arithmetic and copies ran while one was open for 1% of the time, Pallas kernels for 20%

profile of v5, /device:TPU:2, one launch (start us, length us, event | category | flops | bytes accessed | tf_op | source)
XLA Modules:
  0.0 124.0 jit_solution(3245465968164893097)
XLA Ops:
  1.7 1.9 %collective-permute-start.2 = (f32[16,64,128]{2,1,0:T(8,128)S(1)}, f32[16,64,128]{2,1,0:T(8,128)S(1)}, u32[]{:S(2)}, u32[]{:S(2)}) collective-permute-start(f32[16,64,128]{2,1,0:T(8,128)S(1)} %get-tuple-element.23), channel_id=1, source_target_pairs={{0,1},{1,2},{2,3},{3,4},{4,5},{5,6},{6,7},{8,9},{9,10},{10,11},{11... | collective-permute-start | bytes 1572872 | tf_op jit(solution)/shard_map/ppermute | solution.py:230
  3.6 4.3 %collective-permute-start = (f32[6,64,512]{2,1,0:T(8,128)S(1)}, f32[6,64,512]{2,1,0:T(8,128)S(1)}, u32[]{:S(2)}, u32[]{:S(2)}) collective-permute-start(f32[6,64,512]{2,1,0:T(8,128)S(1)} %get-tuple-element.21), channel_id=1, source_target_pairs={{0,8},{8,16},{16,24},{24,32},{32,40},{40,48},{48,56},{56,64},{64,7... | collective-permute-start | bytes 2359304 | tf_op jit(solution)/shard_map/ppermute | solution.py:228
  7.9 10.0 %collective-permute-start.1 = (f32[3,64,512]{2,1,0:T(8,128)S(1)}, f32[3,64,512]{2,1,0:T(8,128)S(1)}, u32[]{:S(2)}, u32[]{:S(2)}) collective-permute-start(f32[3,64,512]{2,1,0:T(8,128)S(1)} %get-tuple-element.22), channel_id=1, source_target_pairs={{0,48},{8,56},{16,0},{24,8},{32,16},{40,24},{48,32},{56,40},{64,11... | collective-permute-start | bytes 1179656 | tf_op jit(solution)/shard_map/ppermute | solution.py:229
  18.0 2.8 %sweep.4.own_ref = f32[7,64,512]{2,1,0:T(8,128)S(1)} custom-call(s32[2,16]{1,0:T(2,128)S(1)} %copy-done.5, f32[8,16]{1,0:T(8,128)S(1)} %bitcast.4, f32[16,64,512]{2,1,0:T(8,128)S(1)} %copy-done, f32[16,64,128]{2,1,0:T(8,128)S(1)} %collective-permute-done.2.edge_ref), custom_call_target="tpu_custom_call" | custom-call | flops 1 | bytes 1 | tf_op jit(solution)/shard_map/sweep/pallas_call | solution.py:61
  20.9 2.1 %collective-permute-start.6 = (f32[7,64,512]{2,1,0:T(8,128)S(1)}, f32[7,64,512]{2,1,0:T(8,128)}, u32[]{:S(2)}, u32[]{:S(2)}) collective-permute-start(f32[7,64,512]{2,1,0:T(8,128)S(1)} %sweep.4.own_ref), channel_id=1, source_target_pairs={{0,8},{8,16},{16,24},{24,32},{32,40},{40,48},{48,56},{56,64},{64,7... | collective-permute-start | bytes 2752520 | tf_op jit(solution)/shard_map/ppermute | solution.py:233
  22.9 3.4 %sweep.5.own_ref = f32[9,64,512]{2,1,0:T(8,128)S(1)} custom-call(s32[2,16]{1,0:T(2,128)S(1)} %copy-done.5, f32[8,16]{1,0:T(8,128)S(1)} %bitcast.5, f32[16,64,512]{2,1,0:T(8,128)S(1)} %copy-done, f32[16,64,128]{2,1,0:T(8,128)S(1)} %collective-permute-done.2.edge_ref), custom_call_target="tpu_custom_call" | custom-call | flops 1 | bytes 1 | tf_op jit(solution)/shard_map/sweep/pallas_call | solution.py:61
  26.3 9.0 %collective-permute-done.1.field_ref = f32[3,64,512]{2,1,0:T(8,128)S(1)} collective-permute-done((f32[3,64,512]{2,1,0:T(8,128)S(1)}, f32[3,64,512]{2,1,0:T(8,128)S(1)}, u32[]{:S(2)}, u32[]{:S(2)}) %collective-permute-start.1) | collective-permute-done | bytes 393248 | tf_op jit(solution)/shard_map/ppermute | solution.py:229
  36.8 2.9 %collective-permute-start.3 = (f32[9,64,128]{2,1,0:T(8,128)}, f32[9,64,128]{2,1,0:T(8,128)S(1)}, u32[]{:S(2)}, u32[]{:S(2)}) collective-permute-start(f32[9,64,128]{2,1,0:T(8,128)} %pad_maximum_fusion), channel_id=1, source_target_pairs={{0,1},{1,2},{2,3},{3,4},{4,5},{5,6},{6,7},{8,9},{9,10},{10,11},{11... | collective-permute-start | bytes 884744 | tf_op jit(solution)/shard_map/ppermute | solution.py:237
  39.8 6.1 %operator.1.op_ref = bf16[16,256,216]{2,1,0:T(8,128)(2,1)S(1)} custom-call(s32[1]{0:T(128)} %bitcast.me_ref, s32[3,64]{1,0:T(4,128)S(1)} %bitcast.9, s32[2,16]{1,0:T(2,128)S(1)} %copy-done.8, f32[8,16]{1,0:T(8,128)S(1)} %bitcast.8, f32[4,64,64]{2,1,0:T(8,128)S(1)} %copy-done.1, f32[4,64,64]{2,1,0:T(8,128)S(1)} %copy-done.1, f32[4,64,64]{2,1,0:T(8,128)S(1)} %copy-done.1), custom_call_target="tpu_custom_call" | custom-call | flops 1 | bytes 1 | tf_op jit(solution)/shard_map/operator/pallas_call | solution.py:131
  45.9 2.5 %sweep.6.one_ref = f32[6,64,512]{2,1,0:T(8,128)S(1)} custom-call(s32[2,16]{1,0:T(2,128)S(1)} %copy-done.5, f32[8,16]{1,0:T(8,128)S(1)} %bitcast.6, f32[6,64,512]{2,1,0:T(8,128)S(1)} %collective-permute-done.field_ref, f32[9,64,128]{2,1,0:T(8,128)S(1)} %collective-permute-done.3.edge_ref), custom_call_target="tpu_custom_call" | custom-call | flops 1 | bytes 1 | tf_op jit(solution)/shard_map/sweep/pallas_call | solution.py:61
  48.4 1.9 %collective-permute-start.5 = (f32[6,64,512]{2,1,0:T(8,128)S(1)}, f32[6,64,512]{2,1,0:T(8,128)S(1)}, u32[]{:S(2)}, u32[]{:S(2)}) collective-permute-start(f32[6,64,512]{2,1,0:T(8,128)S(1)} %sweep.6.one_ref), channel_id=1, source_target_pairs={{0,8},{8,16},{16,24},{24,32},{32,40},{40,48},{48,56},{56,64},{64,7... | collective-permute-start | bytes 2359304 | tf_op jit(solution)/shard_map/ppermute | solution.py:242
  51.9 2.9 %collective-permute-done.6.one_ref = f32[7,64,512]{2,1,0:T(8,128)} collective-permute-done((f32[7,64,512]{2,1,0:T(8,128)S(1)}, f32[7,64,512]{2,1,0:T(8,128)}, u32[]{:S(2)}, u32[]{:S(2)}) %collective-permute-start.6) | collective-permute-done | bytes 917536 | tf_op jit(solution)/shard_map/ppermute | solution.py:233
  54.8 1.9 %collective-permute-start.8 = (f32[7,64,512]{2,1,0:T(8,128)}, f32[7,64,512]{2,1,0:T(8,128)S(1)}, u32[]{:S(2)}, u32[]{:S(2)}) collective-permute-start(f32[7,64,512]{2,1,0:T(8,128)} %collective-permute-done.6.one_ref), channel_id=1, source_target_pairs={{0,8},{8,16},{16,24},{24,32},{32,40},{40,48},{48,56},{56,64},{64,7... | collective-permute-start | bytes 2752520 | tf_op jit(solution)/shard_map/ppermute | solution.py:246
  56.7 4.3 %collective-permute-start.4 = (f32[3,64,512]{2,1,0:T(8,128)S(1)}, f32[3,64,512]{2,1,0:T(8,128)S(1)}, u32[]{:S(2)}, u32[]{:S(2)}) collective-permute-start(f32[3,64,512]{2,1,0:T(8,128)S(1)} %sweep.7), channel_id=1, source_target_pairs={{48,24},{56,32},{0,40},{8,48},{16,56},{24,64},{32,72},{40,80},{112... | collective-permute-start | bytes 1179656 | tf_op jit(solution)/shard_map/ppermute | solution.py:244
  60.9 13.1 %collective-permute-done.5.two_ref = f32[6,64,512]{2,1,0:T(8,128)S(1)} collective-permute-done((f32[6,64,512]{2,1,0:T(8,128)S(1)}, f32[6,64,512]{2,1,0:T(8,128)S(1)}, u32[]{:S(2)}, u32[]{:S(2)}) %collective-permute-start.5) | collective-permute-done | bytes 786464 | tf_op jit(solution)/shard_map/ppermute | solution.py:242
  74.0 16.1 %collective-permute-done.4 = f32[3,64,512]{2,1,0:T(8,128)S(1)} collective-permute-done((f32[3,64,512]{2,1,0:T(8,128)S(1)}, f32[3,64,512]{2,1,0:T(8,128)S(1)}, u32[]{:S(2)}, u32[]{:S(2)}) %collective-permute-start.4) | collective-permute-done | bytes 393248 | tf_op jit(solution)/shard_map/ppermute | solution.py:244
  90.1 5.2 %collective-permute-start.7 = (f32[3,64,512]{2,1,0:T(8,128)S(1)}, f32[3,64,512]{2,1,0:T(8,128)S(1)}, u32[]{:S(2)}, u32[]{:S(2)}) collective-permute-start(f32[3,64,512]{2,1,0:T(8,128)S(1)} %collective-permute-done.4), channel_id=1, source_target_pairs={{0,504},{8,0},{16,8},{24,16},{32,24},{40,32},{48,40},{56,48},{64,5... | collective-permute-start | bytes 1179656 | tf_op jit(solution)/shard_map/ppermute | solution.py:250
  95.3 1.9 %collective-permute-start.11 = (f32[6,24,512]{2,1,0:T(8,128)S(1)}, f32[6,24,512]{2,1,0:T(8,128)S(1)}, u32[]{:S(2)}, u32[]{:S(2)}) collective-permute-start(f32[6,24,512]{2,1,0:T(8,128)S(1)} %slice.19), channel_id=1, source_target_pairs={{0,8},{8,16},{16,24},{24,32},{32,40},{40,48},{48,56},{56,64},{64,7... | collective-permute-start | bytes 884744 | tf_op jit(solution)/shard_map/ppermute | solution.py:248
  97.3 1.9 %collective-permute-start.10 = (f32[7,24,512]{2,1,0:T(8,128)S(1)}, f32[7,24,512]{2,1,0:T(8,128)S(1)}, u32[]{:S(2)}, u32[]{:S(2)}) collective-permute-start(f32[7,24,512]{2,1,0:T(8,128)S(1)} %slice.18), channel_id=1, source_target_pairs={{0,8},{8,16},{16,24},{24,32},{32,40},{40,48},{48,56},{56,64},{64,7... | collective-permute-start | bytes 1032200 | tf_op jit(solution)/shard_map/ppermute | solution.py:252
  99.2 4.6 %collective-permute-done.7.two_ref = f32[3,64,512]{2,1,0:T(8,128)S(1)} collective-permute-done((f32[3,64,512]{2,1,0:T(8,128)S(1)}, f32[3,64,512]{2,1,0:T(8,128)S(1)}, u32[]{:S(2)}, u32[]{:S(2)}) %collective-permute-start.7) | collective-permute-done | bytes 393248 | tf_op jit(solution)/shard_map/ppermute | solution.py:250
  103.8 7.7 %collective-permute-start.9 = (f32[3,64,512]{2,1,0:T(8,128)S(1)}, f32[3,64,512]{2,1,0:T(8,128)S(1)}, u32[]{:S(2)}, u32[]{:S(2)}) collective-permute-start(f32[3,64,512]{2,1,0:T(8,128)S(1)} %collective-permute-done.7.two_ref), channel_id=1, source_target_pairs={{0,504},{8,0},{16,8},{24,16},{32,24},{40,32},{48,40},{56,48},{64,5... | collective-permute-start | bytes 1179656 | tf_op jit(solution)/shard_map/ppermute | solution.py:254
  111.5 3.1 %finish.3.rest_0_ = f32[16,64,512]{2,1,0:T(8,128)} custom-call(bf16[16,256,216]{2,1,0:T(8,128)(2,1)S(1)} %operator.1.op_ref, f32[9,64,512]{2,1,0:T(8,128)S(1)} %sweep.5.own_ref, f32[6,64,512]{2,1,0:T(8,128)S(1)} %sweep.6.one_ref, f32[6,64,512]{2,1,0:T(8,128)S(1)} %collective-permute-done.5.two_ref, f32[6,24,512]{2,1,0:T(8,128)S(1)} %collective-permute-done.11.rim_ref), custom_call_target="tpu_custom_call" | custom-call | flops 1000000000 | bytes 1 | tf_op jit(solution)/shard_map/finish/pallas_call | solution.py:184
  114.6 1.9 %collective-permute-done.10.rim_ref = f32[7,24,512]{2,1,0:T(8,128)S(1)} collective-permute-done((f32[7,24,512]{2,1,0:T(8,128)S(1)}, f32[7,24,512]{2,1,0:T(8,128)S(1)}, u32[]{:S(2)}, u32[]{:S(2)}) %collective-permute-start.10) | collective-permute-done | bytes 344096 | tf_op jit(solution)/shard_map/ppermute | solution.py:252
  116.5 5.6 %finish.4.rest_0_ = f32[16,64,512]{2,1,0:T(8,128)} custom-call(bf16[16,256,216]{2,1,0:T(8,128)(2,1)S(1)} %operator.1.op_ref, f32[7,64,512]{2,1,0:T(8,128)S(1)} %sweep.4.own_ref, f32[7,64,512]{2,1,0:T(8,128)} %collective-permute-done.6.one_ref, f32[7,64,512]{2,1,0:T(8,128)S(1)} %collective-permute-done.8.two_ref, ...), custom_call_target="tpu_custom_call", output_to_operand_aliasing={{}: (5, {})} | custom-call | flops 1000000000 | bytes 1 | tf_op jit(solution)/shard_map/finish/pallas_call | solution.py:184
  (33 shorter events, 6.7 us)
Async XLA Ops:
  0.0 1.6 %copy-start = (f32[16,64,512]{2,1,0:T(8,128)S(1)}, f32[16,64,512]{2,1,0:T(8,128)}, u32[]{:S(2)}) copy-start(f32[16,64,512]{2,1,0:T(8,128)} %field_ref.5) | copy-start | bytes 6291460
  1.6 16.4 %copy-start.4 = (f32[16,8]{0,1:T(8,128)S(1)}, f32[16,8]{0,1:T(8,128)}, u32[]{:S(2)}) copy-start(f32[16,8]{0,1:T(8,128)} %param.11) | copy-start | bytes 1540
  1.6 16.4 %copy-start.5 = (s32[2,16]{1,0:T(2,128)S(1)}, s32[2,16]{1,0:T(2,128)}, u32[]{:S(2)}) copy-start(s32[2,16]{1,0:T(2,128)} %band_ref.9) | copy-start | bytes 388
  1.7 16.3 %collective-permute-start.2 = (f32[16,64,128]{2,1,0:T(8,128)S(1)}, f32[16,64,128]{2,1,0:T(8,128)S(1)}, u32[]{:S(2)}, u32[]{:S(2)}) collective-permute-start(f32[16,64,128]{2,1,0:T(8,128)S(1)} %get-tuple-element.23), channel_id=1, source_target_pairs={{0,1},{1,2},{2,3},{3,4},{4,5},{5,6},{6,7},{8,9},{9,10},{10,11},{11... | collective-permute-start | bytes 1572872 | tf_op jit(solution)/shard_map/ppermute | solution.py:230
  3.6 31.7 %collective-permute-start = (f32[6,64,512]{2,1,0:T(8,128)S(1)}, f32[6,64,512]{2,1,0:T(8,128)S(1)}, u32[]{:S(2)}, u32[]{:S(2)}) collective-permute-start(f32[6,64,512]{2,1,0:T(8,128)S(1)} %get-tuple-element.21), channel_id=1, source_target_pairs={{0,8},{8,16},{16,24},{24,32},{32,40},{40,48},{48,56},{56,64},{64,7... | collective-permute-start | bytes 2359304 | tf_op jit(solution)/shard_map/ppermute | solution.py:228
  7.9 27.4 %collective-permute-start.1 = (f32[3,64,512]{2,1,0:T(8,128)S(1)}, f32[3,64,512]{2,1,0:T(8,128)S(1)}, u32[]{:S(2)}, u32[]{:S(2)}) collective-permute-start(f32[3,64,512]{2,1,0:T(8,128)S(1)} %get-tuple-element.22), channel_id=1, source_target_pairs={{0,48},{8,56},{16,0},{24,8},{32,16},{40,24},{48,32},{56,40},{64,11... | collective-permute-start | bytes 1179656 | tf_op jit(solution)/shard_map/ppermute | solution.py:229
  20.8 18.9 %copy-start.1 = (f32[4,64,64]{2,1,0:T(8,128)S(1)}, f32[4,64,64]{2,1,0:T(8,128)}, u32[]{:S(2)}) copy-start(f32[4,64,64]{2,1,0:T(8,128)} %two_ref.1) | copy-start | bytes 196612
  20.8 18.9 %copy-start.6 = (f32[16,8]{0,1:T(8,128)S(1)}, f32[16,8]{0,1:T(8,128)}, u32[]{:S(2)}) copy-start(f32[16,8]{0,1:T(8,128)} %param.10) | copy-start | bytes 1540
  20.8 18.9 %copy-start.7 = (s32[64,3]{0,1:T(4,128)S(1)}, s32[64,3]{0,1:T(4,128)}, u32[]{:S(2)}) copy-start(s32[64,3]{0,1:T(4,128)} %param.12) | copy-start | bytes 2308
  20.8 18.9 %copy-start.8 = (s32[2,16]{1,0:T(2,128)S(1)}, s32[2,16]{1,0:T(2,128)}, u32[]{:S(2)}) copy-start(s32[2,16]{1,0:T(2,128)} %band_ref.7) | copy-start | bytes 388
  20.9 33.9 %collective-permute-start.6 = (f32[7,64,512]{2,1,0:T(8,128)S(1)}, f32[7,64,512]{2,1,0:T(8,128)}, u32[]{:S(2)}, u32[]{:S(2)}) collective-permute-start(f32[7,64,512]{2,1,0:T(8,128)S(1)} %sweep.4.own_ref), channel_id=1, source_target_pairs={{0,8},{8,16},{16,24},{24,32},{32,40},{40,48},{48,56},{56,64},{64,7... | collective-permute-start | bytes 2752520 | tf_op jit(solution)/shard_map/ppermute | solution.py:233
  35.3 0.7 copy-start.2
  36.8 9.1 %collective-permute-start.3 = (f32[9,64,128]{2,1,0:T(8,128)}, f32[9,64,128]{2,1,0:T(8,128)S(1)}, u32[]{:S(2)}, u32[]{:S(2)}) collective-permute-start(f32[9,64,128]{2,1,0:T(8,128)} %pad_maximum_fusion), channel_id=1, source_target_pairs={{0,1},{1,2},{2,3},{3,4},{4,5},{5,6},{6,7},{8,9},{9,10},{10,11},{11... | collective-permute-start | bytes 884744 | tf_op jit(solution)/shard_map/ppermute | solution.py:237
  39.8 10.6 %copy-start.3 = (f32[3,64,512]{2,1,0:T(8,128)S(1)}, f32[3,64,512]{2,1,0:T(8,128)}, u32[]{:S(2)}) copy-start(f32[3,64,512]{2,1,0:T(8,128)} %copy-done.2) | copy-start | bytes 1179652
  48.4 25.6 %collective-permute-start.5 = (f32[6,64,512]{2,1,0:T(8,128)S(1)}, f32[6,64,512]{2,1,0:T(8,128)S(1)}, u32[]{:S(2)}, u32[]{:S(2)}) collective-permute-start(f32[6,64,512]{2,1,0:T(8,128)S(1)} %sweep.6.one_ref), channel_id=1, source_target_pairs={{0,8},{8,16},{16,24},{24,32},{32,40},{40,48},{48,56},{56,64},{64,7... | collective-permute-start | bytes 2359304 | tf_op jit(solution)/shard_map/ppermute | solution.py:242
  54.8 42.5 %collective-permute-start.8 = (f32[7,64,512]{2,1,0:T(8,128)}, f32[7,64,512]{2,1,0:T(8,128)S(1)}, u32[]{:S(2)}, u32[]{:S(2)}) collective-permute-start(f32[7,64,512]{2,1,0:T(8,128)} %collective-permute-done.6.one_ref), channel_id=1, source_target_pairs={{0,8},{8,16},{16,24},{24,32},{32,40},{40,48},{48,56},{56,64},{64,7... | collective-permute-start | bytes 2752520 | tf_op jit(solution)/shard_map/ppermute | solution.py:246
  56.7 33.4 %collective-permute-start.4 = (f32[3,64,512]{2,1,0:T(8,128)S(1)}, f32[3,64,512]{2,1,0:T(8,128)S(1)}, u32[]{:S(2)}, u32[]{:S(2)}) collective-permute-start(f32[3,64,512]{2,1,0:T(8,128)S(1)} %sweep.7), channel_id=1, source_target_pairs={{48,24},{56,32},{0,40},{8,48},{16,56},{24,64},{32,72},{40,80},{112... | collective-permute-start | bytes 1179656 | tf_op jit(solution)/shard_map/ppermute | solution.py:244
  90.1 13.7 %collective-permute-start.7 = (f32[3,64,512]{2,1,0:T(8,128)S(1)}, f32[3,64,512]{2,1,0:T(8,128)S(1)}, u32[]{:S(2)}, u32[]{:S(2)}) collective-permute-start(f32[3,64,512]{2,1,0:T(8,128)S(1)} %collective-permute-done.4), channel_id=1, source_target_pairs={{0,504},{8,0},{16,8},{24,16},{32,24},{40,32},{48,40},{56,48},{64,5... | collective-permute-start | bytes 1179656 | tf_op jit(solution)/shard_map/ppermute | solution.py:250
  95.3 16.2 %collective-permute-start.11 = (f32[6,24,512]{2,1,0:T(8,128)S(1)}, f32[6,24,512]{2,1,0:T(8,128)S(1)}, u32[]{:S(2)}, u32[]{:S(2)}) collective-permute-start(f32[6,24,512]{2,1,0:T(8,128)S(1)} %slice.19), channel_id=1, source_target_pairs={{0,8},{8,16},{16,24},{24,32},{32,40},{40,48},{48,56},{56,64},{64,7... | collective-permute-start | bytes 884744 | tf_op jit(solution)/shard_map/ppermute | solution.py:248
  97.3 19.3 %collective-permute-start.10 = (f32[7,24,512]{2,1,0:T(8,128)S(1)}, f32[7,24,512]{2,1,0:T(8,128)S(1)}, u32[]{:S(2)}, u32[]{:S(2)}) collective-permute-start(f32[7,24,512]{2,1,0:T(8,128)S(1)} %slice.18), channel_id=1, source_target_pairs={{0,8},{8,16},{16,24},{24,32},{32,40},{40,48},{48,56},{56,64},{64,7... | collective-permute-start | bytes 1032200 | tf_op jit(solution)/shard_map/ppermute | solution.py:252
  103.8 18.3 %collective-permute-start.9 = (f32[3,64,512]{2,1,0:T(8,128)S(1)}, f32[3,64,512]{2,1,0:T(8,128)S(1)}, u32[]{:S(2)}, u32[]{:S(2)}) collective-permute-start(f32[3,64,512]{2,1,0:T(8,128)S(1)} %collective-permute-done.7.two_ref), channel_id=1, source_target_pairs={{0,504},{8,0},{16,8},{24,16},{32,24},{40,32},{48,40},{56,48},{64,5... | collective-permute-start | bytes 1179656 | tf_op jit(solution)/shard_map/ppermute | solution.py:254

commit v6 on v5

--- a/solution.py
+++ b/solution.py
@@ -147,42 +147,77 @@
     )(me, pairs, band, taps, agg_kern, agg_kern, agg_kern)
 
 
-def finish_kernel(op_ref, own_ref, one_ref, two_ref, rim_ref, *rest):
-    out_ref, high_ref, low_ref = rest[-3:]
-    rows = own_ref.shape[1]
+def product(op_ref, columns, pieces, high_ref, low_ref):
     at = 0
-    for ref in (own_ref, one_ref, two_ref, rim_ref):
+    for ref in pieces:
         high, low = split(ref[0])
         high_ref[at : at + ref.shape[1]] = high
         low_ref[at : at + ref.shape[1]] = low
         at += ref.shape[1]
+    half = op_ref.shape[1] // 2
     dot = functools.partial(jnp.dot, preferred_element_type=jnp.float32)
-    four = dot(op_ref[0], high_ref[...])
-    both = four[: 2 * rows] + four[2 * rows :] + dot(op_ref[0, : 2 * rows], low_ref[...])
-    rate, spread = both[:rows], both[rows:]
-    out_ref[0] = spread + BETA * (rate * rate / (1.0 + rate) - spread * rate)
-
-
-def finish(operator, own, one, two, rim, part, total, before, own_first, flops):
+    four = dot(op_ref[0, :, columns], high_ref[:at])
+    return four[:half] + four[half:] + dot(op_ref[0, :half, columns], low_ref[:at])
+
+
+def prepare_kernel(op_ref, own_ref, one_ref, out_ref, high_ref, low_ref):
+    rows = own_ref.shape[1]
+    out_ref[0] = product(op_ref, slice(0, 2 * rows), (own_ref, one_ref), high_ref, low_ref)
+
+
+def prepare(operator, own, one, part):
     lo, hi = part
     count, rows, width = one.shape
+    tile = pl.BlockSpec((1, rows, width), lambda i: (i, 0, 0))
+    return pl.pallas_call(
+        prepare_kernel,
+        grid=(count,),
+        in_specs=[pl.BlockSpec((1,) + operator.shape[1:], lambda i: (i + lo, 0, 0)), tile, tile],
+        out_specs=pl.BlockSpec((1, 2 * rows, width), lambda i: (i, 0, 0)),
+        out_shape=jax.ShapeDtypeStruct((count, 2 * rows, width), jnp.float32),
+        scratch_shapes=[pltpu.VMEM((2 * rows, width), jnp.bfloat16)] * 2,
+        compiler_params=pltpu.CompilerParams(vmem_limit_bytes=VMEM),
+        cost_estimate=cost(1),
+        name="prepare",
+    )(operator, own, one)
+
+
+def update(both):
+    rows = both.shape[0] // 2
+    rate, spread = both[:rows], both[rows:]
+    return spread + BETA * (rate * rate / (1.0 + rate) - spread * rate)
+
+
+def finish_kernel(op_ref, own_ref, one_ref, two_ref, rim_ref, *rest):
+    out_ref, high_ref, low_ref = rest[-3:]
+    pieces = (own_ref, one_ref, two_ref, rim_ref)
+    out_ref[0] = update(product(op_ref, slice(None), pieces, high_ref, low_ref))
+
+
+def complete_kernel(op_ref, sum_ref, two_ref, rim_ref, *rest):
+    out_ref, high_ref, low_ref = rest[-3:]
+    columns = slice(2 * two_ref.shape[1], op_ref.shape[2])
+    out_ref[0] = update(sum_ref[0] + product(op_ref, columns, (two_ref, rim_ref), high_ref, low_ref))
+
+
+def finish(operator, held, two, rim, part, total, before, held_first, flops):
+    lo, hi = part
+    count, rows, width = two.shape
     depth = operator.shape[2]
     here = lambda i: (i, 0, 0)
-    in_specs = [
-        pl.BlockSpec((1, operator.shape[1], depth), lambda i: (i + lo, 0, 0)),
-        pl.BlockSpec((1, rows, width), lambda i: (i + own_first, 0, 0)),
-        pl.BlockSpec((1, rows, width), here),
-        pl.BlockSpec((1, rows, width), here),
-        pl.BlockSpec((1, RIM, width), here),
-    ]
-    operands = [operator, own, one, two, rim]
+    firsts = (held_first, 0)
+    in_specs = [pl.BlockSpec((1, operator.shape[1], depth), lambda i: (i + lo, 0, 0))]
+    for first, value in zip(firsts, held):
+        in_specs.append(pl.BlockSpec((1,) + value.shape[1:], lambda i, first=first: (i + first, 0, 0)))
+    in_specs += [pl.BlockSpec((1, rows, width), here), pl.BlockSpec((1, RIM, width), here)]
+    operands = [operator, *held, two, rim]
     aliases = {}
     if before is not None:
+        aliases = {len(operands): 0}
         in_specs.append(pl.BlockSpec(memory_space=pl.ANY))
         operands.append(before)
-        aliases = {5: 0}
-    return pl.pallas_call(
-        finish_kernel,
+    return pl.pallas_call(
+        finish_kernel if len(held) == 2 else complete_kernel,
         grid=(count,),
         in_specs=in_specs,
         out_specs=pl.BlockSpec((1, rows, width), lambda i: (i + lo, 0, 0)),
@@ -195,8 +230,8 @@
     )(*operands)
 
 
-EARLY = (0, 6)
-BACK = (6, 9)
+EARLY = (0, 7)
+BACK = (7, 9)
 LATE = (9, 16)
 FIRST = (0, 9)
 
@@ -228,6 +263,8 @@
     early_one_raw = hop(early)
     back_away_raw = back_first(back)
     edge = side(rim)
+    me = lax.axis_index("len")[None].astype(jnp.int32)
+    edge, me = lax.optimization_barrier((edge, me))
 
     late_own = sweep(density, edge, *wide, LATE, LATE[0], LATE[0], 1)
     late_one = hop(late_own)
@@ -235,16 +272,15 @@
     early_one_raw, back_away_raw, first_own = lax.optimization_barrier((early_one_raw, back_away_raw, first_own))
 
     first_edge = side(jnp.concatenate([early_one_raw[:, :, margin:], back_away_raw[:, :, margin:]], axis=0))
-    me = after(lax.axis_index("len")[None].astype(jnp.int32), first_own)
-    operator = length_operator(me, tile_pairs.T, len_band, len_taps.T, agg_kern)
-    first_edge = after(first_edge, operator)
-    early_one = sweep(early_one_raw, first_edge, *wide, EARLY, 0, 0)
+    early_one = sweep(early_one_raw, first_edge, *wide, EARLY, 0, 0, 1)
     early_two = hop(early_one)
     back_away = sweep(back_away_raw, after(first_edge, early_one), *wide, BACK, 0, EARLY[1])
     back_three_below = back_rest(back_away)
     late_one = after(late_one, back_away)
     late_two = hop(late_one)
-    early_two = after(early_two, late_one)
+    operator = length_operator(me, tile_pairs.T, len_band, after(len_taps.T, late_one), agg_kern)
+    late_sum = prepare(operator, late_own, late_one, LATE)
+    early_two = after(early_two, late_sum)
     early_rim = hop(early_two[:, tile_len - RIM :])
     back_three_below = after(back_three_below, early_two)
     back_two = unhop(back_three_below)
@@ -254,10 +290,10 @@
     back_one = unhop(back_two)
 
     early_rim = after(early_rim, back_two)
-    out = finish(operator, first_own, early_one, early_two, early_rim, EARLY, batches, None, 0, 1000000000)
-    out = finish(operator, late_own, late_one, late_two, late_rim, LATE, batches, out, 0, 1000000000)
+    out = finish(operator, (first_own, early_one), early_two, early_rim, EARLY, batches, None, 0, 1000000000)
+    out = finish(operator, (late_sum,), late_two, late_rim, LATE, batches, out, 0, 1000000000)
     back_rim = back_three_below[:, tile_len - RIM :]
-    return finish(operator, first_own, back_one, back_two, back_rim, BACK, batches, out, EARLY[1], 1)
+    return finish(operator, (first_own, back_one), back_two, back_rim, BACK, batches, out, EARLY[1], 1)
 
 
 def solution(mesh):

time: 125 us -> 121 us (0.968)
  the two profiles are of different devices: /device:TPU:2 before, /device:TPU:1 now
where the time goes in v6:
time: 121 us; the launch traced here: 120 us
  starting transfers between devices  47.3 us (39%)
  waiting for transfers between devices  42.3 us (35%)
  Pallas kernels  28 us (23%)
  local copies, waits for them, and re-layouts  2.42 us (2%)
    ppermute x1, waiting for transfers between devices, shards(): late_two = hop(late_one)  10.5 us
    pallas_call x4, Pallas kernels, sweep(): pl.pallas_call(functools.partial(sweep_kernel, lo), grid_spec=pltpu.Prefe...  10.2 us
    ppermute x1, starting transfers between devices, shards(): back_away_raw = back_first(back)  9.76 us
    pallas_call x3, Pallas kernels, finish(): pl.pallas_call(finish_kernel if len(held) == 2 else complete_kernel, grid...  8.62 us
    ppermute x1, waiting for transfers between devices, shards(): early_two = hop(early_one)  7.83 us
    ppermute x1, starting transfers between devices, shards(): back_one = unhop(back_two)  6.68 us
    ppermute x1, waiting for transfers between devices, shards(): late_one = hop(late_own)  6.41 us
    pallas_call x1, Pallas kernels, length_operator(): pl.pallas_call(operator_kernel, grid_spec=pltpu.PrefetchScalarGridSpec(nu...  6.12 us
  transfers between devices with their start and end apart: 12, of which 9 were waited for; matrix products, arithmetic and copies ran while one was open for 0% of the time, Pallas kernels for 21%

profile of v6, /device:TPU:1, one launch (start us, length us, event | category | flops | bytes accessed | tf_op | source)
XLA Modules:
  0.0 120.4 jit_solution(2519911634300189665)
XLA Ops:
  3.5 4.5 %collective-permute-start = (f32[16,64,128]{2,1,0:T(8,128)}, f32[16,64,128]{2,1,0:T(8,128)S(1)}, u32[]{:S(2)}, u32[]{:S(2)}) collective-permute-start(f32[16,64,128]{2,1,0:T(8,128)} %get-tuple-element.22), channel_id=1, source_target_pairs={{0,1},{1,2},{2,3},{3,4},{4,5},{5,6},{6,7},{8,9},{9,10},{10,11},{11... | collective-permute-start | bytes 1572872 | tf_op jit(solution)/shard_map/ppermute | solution.py:265
  8.0 4.0 %collective-permute-start.2 = (f32[7,64,512]{2,1,0:T(8,128)}, f32[7,64,512]{2,1,0:T(8,128)S(1)}, u32[]{:S(2)}, u32[]{:S(2)}) collective-permute-start(f32[7,64,512]{2,1,0:T(8,128)} %get-tuple-element.25), channel_id=1, source_target_pairs={{0,8},{8,16},{16,24},{24,32},{32,40},{40,48},{48,56},{56,64},{64,7... | collective-permute-start | bytes 2752520 | tf_op jit(solution)/shard_map/ppermute | solution.py:263
  12.0 2.4 %collective-permute-done.edge_ref = f32[16,64,128]{2,1,0:T(8,128)S(1)} collective-permute-done((f32[16,64,128]{2,1,0:T(8,128)}, f32[16,64,128]{2,1,0:T(8,128)S(1)}, u32[]{:S(2)}, u32[]{:S(2)}) %collective-permute-start) | collective-permute-done | bytes 524320 | tf_op jit(solution)/shard_map/ppermute | solution.py:265
  14.5 2.8 %sweep.4.own_ref = f32[7,64,512]{2,1,0:T(8,128)S(1)} custom-call(s32[2,16]{1,0:T(2,128)S(1)} %copy-done.4, f32[8,16]{1,0:T(8,128)S(1)} %bitcast.4, f32[16,64,512]{2,1,0:T(8,128)S(1)} %copy-done.1, f32[16,64,128]{2,1,0:T(8,128)S(1)} %collective-permute-done.edge_ref), custom_call_target="tpu_custom_call" | custom-call | flops 1 | bytes 1 | tf_op jit(solution)/shard_map/sweep/pallas_call | solution.py:61
  17.2 4.0 %collective-permute-start.1 = (f32[7,64,512]{2,1,0:T(8,128)S(1)}, f32[7,64,512]{2,1,0:T(8,128)S(1)}, u32[]{:S(2)}, u32[]{:S(2)}) collective-permute-start(f32[7,64,512]{2,1,0:T(8,128)S(1)} %sweep.4.own_ref), channel_id=1, source_target_pairs={{0,8},{8,16},{16,24},{24,32},{32,40},{40,48},{48,56},{56,64},{64,7... | collective-permute-start | bytes 2752520 | tf_op jit(solution)/shard_map/ppermute | solution.py:270
  21.3 9.8 %collective-permute-start.3 = (f32[2,64,512]{2,1,0:T(8,128)S(1)}, f32[2,64,512]{2,1,0:T(8,128)S(1)}, u32[]{:S(2)}, u32[]{:S(2)}) collective-permute-start(f32[2,64,512]{2,1,0:T(8,128)S(1)} %copy-done.9), channel_id=1, source_target_pairs={{0,48},{8,56},{16,0},{24,8},{32,16},{40,24},{48,32},{56,40},{64,11... | collective-permute-start | bytes 786440 | tf_op jit(solution)/shard_map/ppermute | solution.py:264
  31.0 3.4 %sweep.5.own_ref = f32[9,64,512]{2,1,0:T(8,128)S(1)} custom-call(s32[2,16]{1,0:T(2,128)S(1)} %copy-done.4, f32[8,16]{1,0:T(8,128)S(1)} %bitcast.5, f32[16,64,512]{2,1,0:T(8,128)S(1)} %copy-done.1, f32[16,64,128]{2,1,0:T(8,128)S(1)} %collective-permute-done.edge_ref), custom_call_target="tpu_custom_call" | custom-call | flops 1 | bytes 1 | tf_op jit(solution)/shard_map/sweep/pallas_call | solution.py:61
  34.5 3.5 %collective-permute-done.3.field_ref = f32[2,64,512]{2,1,0:T(8,128)S(1)} collective-permute-done((f32[2,64,512]{2,1,0:T(8,128)S(1)}, f32[2,64,512]{2,1,0:T(8,128)S(1)}, u32[]{:S(2)}, u32[]{:S(2)}) %collective-permute-start.3) | collective-permute-done | bytes 262176 | tf_op jit(solution)/shard_map/ppermute | solution.py:264
  38.0 4.8 %collective-permute-done.2.field_ref = f32[7,64,512]{2,1,0:T(8,128)S(1)} collective-permute-done((f32[7,64,512]{2,1,0:T(8,128)}, f32[7,64,512]{2,1,0:T(8,128)S(1)}, u32[]{:S(2)}, u32[]{:S(2)}) %collective-permute-start.2) | collective-permute-done | bytes 917536 | tf_op jit(solution)/shard_map/ppermute | solution.py:263
  42.8 3.2 %collective-permute-start.4 = (f32[9,64,128]{2,1,0:T(8,128)S(1)}, f32[9,64,128]{2,1,0:T(8,128)S(1)}, u32[]{:S(2)}, u32[]{:S(2)}) collective-permute-start(f32[9,64,128]{2,1,0:T(8,128)S(1)} %pad_maximum_fusion), channel_id=1, source_target_pairs={{0,1},{1,2},{2,3},{3,4},{4,5},{5,6},{6,7},{8,9},{9,10},{10,11},{11... | collective-permute-start | bytes 884744 | tf_op jit(solution)/shard_map/ppermute | solution.py:274
  46.0 3.6 %collective-permute-done.4.edge_ref = f32[9,64,128]{2,1,0:T(8,128)S(1)} collective-permute-done((f32[9,64,128]{2,1,0:T(8,128)S(1)}, f32[9,64,128]{2,1,0:T(8,128)S(1)}, u32[]{:S(2)}, u32[]{:S(2)}) %collective-permute-start.4) | collective-permute-done | bytes 294944 | tf_op jit(solution)/shard_map/ppermute | solution.py:274
  49.7 2.8 %sweep.6.one_ref = f32[7,64,512]{2,1,0:T(8,128)S(1)} custom-call(s32[2,16]{1,0:T(2,128)S(1)} %copy-done.4, f32[8,16]{1,0:T(8,128)S(1)} %bitcast.6, f32[7,64,512]{2,1,0:T(8,128)S(1)} %collective-permute-done.2.field_ref, f32[9,64,128]{2,1,0:T(8,128)S(1)} %collective-permute-done.4.edge_ref), custom_call_target="tpu_custom_call" | custom-call | flops 1 | bytes 1 | tf_op jit(solution)/shard_map/sweep/pallas_call | solution.py:61
  52.5 2.2 %collective-permute-start.6 = (f32[7,64,512]{2,1,0:T(8,128)S(1)}, f32[7,64,512]{2,1,0:T(8,128)S(1)}, u32[]{:S(2)}, u32[]{:S(2)}) collective-permute-start(f32[7,64,512]{2,1,0:T(8,128)S(1)} %sweep.6.one_ref), channel_id=1, source_target_pairs={{0,8},{8,16},{16,24},{24,32},{32,40},{40,48},{48,56},{56,64},{64,7... | collective-permute-start | bytes 2752520 | tf_op jit(solution)/shard_map/ppermute | solution.py:276
  56.0 6.4 %collective-permute-done.1.one_ref = f32[7,64,512]{2,1,0:T(8,128)S(1)} collective-permute-done((f32[7,64,512]{2,1,0:T(8,128)S(1)}, f32[7,64,512]{2,1,0:T(8,128)S(1)}, u32[]{:S(2)}, u32[]{:S(2)}) %collective-permute-start.1) | collective-permute-done | bytes 917536 | tf_op jit(solution)/shard_map/ppermute | solution.py:270
  64.3 1.9 %collective-permute-start.5 = (f32[2,64,512]{2,1,0:T(8,128)S(1)}, f32[2,64,512]{2,1,0:T(8,128)S(1)}, u32[]{:S(2)}, u32[]{:S(2)}) collective-permute-start(f32[2,64,512]{2,1,0:T(8,128)S(1)} %sweep.7), channel_id=1, source_target_pairs={{48,24},{56,32},{0,40},{8,48},{16,56},{24,64},{32,72},{40,80},{112... | collective-permute-start | bytes 786440 | tf_op jit(solution)/shard_map/ppermute | solution.py:278
  66.3 6.1 %operator.1.op_ref = bf16[16,256,216]{2,1,0:T(8,128)(2,1)S(1)} custom-call(s32[1]{0:T(128)} %bitcast.me_ref, s32[3,64]{1,0:T(4,128)S(1)} %bitcast.9, s32[2,16]{1,0:T(2,128)S(1)} %copy-done.7, f32[8,16]{1,0:T(8,128)S(1)} %bitcast.8, f32[4,64,64]{2,1,0:T(8,128)S(1)} %copy-done.2, f32[4,64,64]{2,1,0:T(8,128)S(1)} %copy-done.2, f32[4,64,64]{2,1,0:T(8,128)S(1)} %copy-done.2), custom_call_target="tpu_custom_call" | custom-call | flops 1 | bytes 1 | tf_op jit(solution)/shard_map/operator/pallas_call | solution.py:131
  74.2 7.8 %collective-permute-done.6.two_ref = f32[7,64,512]{2,1,0:T(8,128)S(1)} collective-permute-done((f32[7,64,512]{2,1,0:T(8,128)S(1)}, f32[7,64,512]{2,1,0:T(8,128)S(1)}, u32[]{:S(2)}, u32[]{:S(2)}) %collective-permute-start.6) | collective-permute-done | bytes 917536 | tf_op jit(solution)/shard_map/ppermute | solution.py:276
  82.1 1.9 %collective-permute-start.11 = (f32[7,24,512]{2,1,0:T(8,128)S(1)}, f32[7,24,512]{2,1,0:T(8,128)S(1)}, u32[]{:S(2)}, u32[]{:S(2)}) collective-permute-start(f32[7,24,512]{2,1,0:T(8,128)S(1)} %slice.19), channel_id=1, source_target_pairs={{0,8},{8,16},{16,24},{24,32},{32,40},{40,48},{48,56},{56,64},{64,7... | collective-permute-start | bytes 1032200 | tf_op jit(solution)/shard_map/ppermute | solution.py:284
  84.0 2.0 %collective-permute-done.5 = f32[2,64,512]{2,1,0:T(8,128)S(1)} collective-permute-done((f32[2,64,512]{2,1,0:T(8,128)S(1)}, f32[2,64,512]{2,1,0:T(8,128)S(1)}, u32[]{:S(2)}, u32[]{:S(2)}) %collective-permute-start.5) | collective-permute-done | bytes 262176 | tf_op jit(solution)/shard_map/ppermute | solution.py:278
  85.9 5.2 %collective-permute-start.7 = (f32[2,64,512]{2,1,0:T(8,128)S(1)}, f32[2,64,512]{2,1,0:T(8,128)S(1)}, u32[]{:S(2)}, u32[]{:S(2)}) collective-permute-start(f32[2,64,512]{2,1,0:T(8,128)S(1)} %collective-permute-done.5), channel_id=1, source_target_pairs={{0,504},{8,0},{16,8},{24,16},{32,24},{40,32},{48,40},{56,48},{64,5... | collective-permute-start | bytes 786440 | tf_op jit(solution)/shard_map/ppermute | solution.py:286
  91.2 10.5 %collective-permute-done.8.two_ref = f32[7,64,512]{2,1,0:T(8,128)S(1)} collective-permute-done((f32[7,64,512]{2,1,0:T(8,128)S(1)}, f32[7,64,512]{2,1,0:T(8,128)S(1)}, u32[]{:S(2)}, u32[]{:S(2)}) %collective-permute-start.8) | collective-permute-done | bytes 917536 | tf_op jit(solution)/shard_map/ppermute | solution.py:280
  103.7 6.7 %collective-permute-start.9 = (f32[2,64,512]{2,1,0:T(8,128)S(1)}, f32[2,64,512]{2,1,0:T(8,128)S(1)}, u32[]{:S(2)}, u32[]{:S(2)}) collective-permute-start(f32[2,64,512]{2,1,0:T(8,128)S(1)} %collective-permute-done.7.two_ref), channel_id=1, source_target_pairs={{0,504},{8,0},{16,8},{24,16},{32,24},{40,32},{48,40},{56,48},{64,5... | collective-permute-start | bytes 786440 | tf_op jit(solution)/shard_map/ppermute | solution.py:290
  110.4 3.7 %finish.3.rest_0_ = f32[16,64,512]{2,1,0:T(8,128)} custom-call(bf16[16,256,216]{2,1,0:T(8,128)(2,1)S(1)} %operator.1.op_ref, f32[9,64,512]{2,1,0:T(8,128)S(1)} %sweep.5.own_ref, f32[7,64,512]{2,1,0:T(8,128)S(1)} %sweep.6.one_ref, f32[7,64,512]{2,1,0:T(8,128)S(1)} %collective-permute-done.6.two_ref, f32[7,24,512]{2,1,0:T(8,128)S(1)} %collective-permute-done.11.rim_ref), custom_call_target="tpu_custom_call" | custom-call | flops 1000000000 | bytes 1 | tf_op jit(solution)/shard_map/finish/pallas_call | solution.py:219
  115.5 3.7 %finish.4.rest_0_ = f32[16,64,512]{2,1,0:T(8,128)} custom-call(bf16[16,256,216]{2,1,0:T(8,128)(2,1)S(1)} %operator.1.op_ref, f32[7,128,512]{2,1,0:T(8,128)S(1)} %prepare.1.sum_ref, f32[7,64,512]{2,1,0:T(8,128)S(1)} %collective-permute-done.8.two_ref, f32[7,24,512]{2,1,0:T(8,128)S(1)} %collective-permute-done.10.rim_ref, ...), custom_call_target="tpu_custom_call", output_to_operand_aliasing={{}: (4, {})} | custom-call | flops 1000000000 | bytes 1 | tf_op jit(solution)/shard_map/finish/pallas_call | solution.py:219
  (36 shorter events, 13.1 us)
Async XLA Ops:
  0.0 1.6 %copy-start = (f32[16,64,512]{2,1,0:T(8,128)S(1)}, f32[16,64,512]{2,1,0:T(8,128)}, u32[]{:S(2)}) copy-start(f32[16,64,512]{2,1,0:T(8,128)} %field_ref.5) | copy-start | bytes 6291460
  1.6 12.9 %copy-start.1 = (f32[16,64,512]{2,1,0:T(8,128)S(1)}, f32[16,64,512]{2,1,0:T(8,128)}, u32[]{:S(2)}) copy-start(f32[16,64,512]{2,1,0:T(8,128)} %field_ref.5) | copy-start | bytes 6291460
  1.6 12.9 %copy-start.3 = (f32[16,8]{0,1:T(8,128)S(1)}, f32[16,8]{0,1:T(8,128)}, u32[]{:S(2)}) copy-start(f32[16,8]{0,1:T(8,128)} %param.11) | copy-start | bytes 1540
  1.6 12.9 %copy-start.4 = (s32[2,16]{1,0:T(2,128)S(1)}, s32[2,16]{1,0:T(2,128)}, u32[]{:S(2)}) copy-start(s32[2,16]{1,0:T(2,128)} %band_ref.8) | copy-start | bytes 388
  2.8 0.7 copy-start.8
  3.5 10.9 %collective-permute-start = (f32[16,64,128]{2,1,0:T(8,128)}, f32[16,64,128]{2,1,0:T(8,128)S(1)}, u32[]{:S(2)}, u32[]{:S(2)}) collective-permute-start(f32[16,64,128]{2,1,0:T(8,128)} %get-tuple-element.22), channel_id=1, source_target_pairs={{0,1},{1,2},{2,3},{3,4},{4,5},{5,6},{6,7},{8,9},{9,10},{10,11},{11... | collective-permute-start | bytes 1572872 | tf_op jit(solution)/shard_map/ppermute | solution.py:265
  8.0 34.7 %collective-permute-start.2 = (f32[7,64,512]{2,1,0:T(8,128)}, f32[7,64,512]{2,1,0:T(8,128)S(1)}, u32[]{:S(2)}, u32[]{:S(2)}) collective-permute-start(f32[7,64,512]{2,1,0:T(8,128)} %get-tuple-element.25), channel_id=1, source_target_pairs={{0,8},{8,16},{16,24},{24,32},{32,40},{40,48},{48,56},{56,64},{64,7... | collective-permute-start | bytes 2752520 | tf_op jit(solution)/shard_map/ppermute | solution.py:263
  12.0 9.2 %copy-start.9 = (f32[2,64,512]{2,1,0:T(8,128)S(1)}, f32[2,64,512]{2,1,0:T(8,128)}, u32[]{:S(2)}) copy-start(f32[2,64,512]{2,1,0:T(8,128)} %copy-done.8) | copy-start | bytes 786436
  17.2 45.1 %collective-permute-start.1 = (f32[7,64,512]{2,1,0:T(8,128)S(1)}, f32[7,64,512]{2,1,0:T(8,128)S(1)}, u32[]{:S(2)}, u32[]{:S(2)}) collective-permute-start(f32[7,64,512]{2,1,0:T(8,128)S(1)} %sweep.4.own_ref), channel_id=1, source_target_pairs={{0,8},{8,16},{16,24},{24,32},{32,40},{40,48},{48,56},{56,64},{64,7... | collective-permute-start | bytes 2752520 | tf_op jit(solution)/shard_map/ppermute | solution.py:270
  21.3 16.7 %collective-permute-start.3 = (f32[2,64,512]{2,1,0:T(8,128)S(1)}, f32[2,64,512]{2,1,0:T(8,128)S(1)}, u32[]{:S(2)}, u32[]{:S(2)}) collective-permute-start(f32[2,64,512]{2,1,0:T(8,128)S(1)} %copy-done.9), channel_id=1, source_target_pairs={{0,48},{8,56},{16,0},{24,8},{32,16},{40,24},{48,32},{56,40},{64,11... | collective-permute-start | bytes 786440 | tf_op jit(solution)/shard_map/ppermute | solution.py:264
  34.4 31.8 %copy-start.2 = (f32[4,64,64]{2,1,0:T(8,128)S(1)}, f32[4,64,64]{2,1,0:T(8,128)}, u32[]{:S(2)}) copy-start(f32[4,64,64]{2,1,0:T(8,128)} %two_ref.1) | copy-start | bytes 196612
  34.4 31.8 %copy-start.5 = (f32[16,8]{0,1:T(8,128)S(1)}, f32[16,8]{0,1:T(8,128)}, u32[]{:S(2)}) copy-start(f32[16,8]{0,1:T(8,128)} %param.10) | copy-start | bytes 1540
  34.5 31.8 %copy-start.6 = (s32[64,3]{0,1:T(4,128)S(1)}, s32[64,3]{0,1:T(4,128)}, u32[]{:S(2)}) copy-start(s32[64,3]{0,1:T(4,128)} %param.12) | copy-start | bytes 2308
  34.5 31.8 %copy-start.7 = (s32[2,16]{1,0:T(2,128)S(1)}, s32[2,16]{1,0:T(2,128)}, u32[]{:S(2)}) copy-start(s32[2,16]{1,0:T(2,128)} %band_ref.9) | copy-start | bytes 388
  42.8 6.9 %collective-permute-start.4 = (f32[9,64,128]{2,1,0:T(8,128)S(1)}, f32[9,64,128]{2,1,0:T(8,128)S(1)}, u32[]{:S(2)}, u32[]{:S(2)}) collective-permute-start(f32[9,64,128]{2,1,0:T(8,128)S(1)} %pad_maximum_fusion), channel_id=1, source_target_pairs={{0,1},{1,2},{2,3},{3,4},{4,5},{5,6},{6,7},{8,9},{9,10},{10,11},{11... | collective-permute-start | bytes 884744 | tf_op jit(solution)/shard_map/ppermute | solution.py:274
  52.5 29.6 %collective-permute-start.6 = (f32[7,64,512]{2,1,0:T(8,128)S(1)}, f32[7,64,512]{2,1,0:T(8,128)S(1)}, u32[]{:S(2)}, u32[]{:S(2)}) collective-permute-start(f32[7,64,512]{2,1,0:T(8,128)S(1)} %sweep.6.one_ref), channel_id=1, source_target_pairs={{0,8},{8,16},{16,24},{24,32},{32,40},{40,48},{48,56},{56,64},{64,7... | collective-permute-start | bytes 2752520 | tf_op jit(solution)/shard_map/ppermute | solution.py:276
  62.4 39.3 %collective-permute-start.8 = (f32[7,64,512]{2,1,0:T(8,128)S(1)}, f32[7,64,512]{2,1,0:T(8,128)S(1)}, u32[]{:S(2)}, u32[]{:S(2)}) collective-permute-start(f32[7,64,512]{2,1,0:T(8,128)S(1)} %collective-permute-done.1.one_ref), channel_id=1, source_target_pairs={{0,8},{8,16},{16,24},{24,32},{32,40},{40,48},{48,56},{56,64},{64,7... | collective-permute-start | bytes 2752520 | tf_op jit(solution)/shard_map/ppermute | solution.py:280
  64.3 21.7 %collective-permute-start.5 = (f32[2,64,512]{2,1,0:T(8,128)S(1)}, f32[2,64,512]{2,1,0:T(8,128)S(1)}, u32[]{:S(2)}, u32[]{:S(2)}) collective-permute-start(f32[2,64,512]{2,1,0:T(8,128)S(1)} %sweep.7), channel_id=1, source_target_pairs={{48,24},{56,32},{0,40},{8,48},{16,56},{24,64},{32,72},{40,80},{112... | collective-permute-start | bytes 786440 | tf_op jit(solution)/shard_map/ppermute | solution.py:278
  82.1 28.3 %collective-permute-start.11 = (f32[7,24,512]{2,1,0:T(8,128)S(1)}, f32[7,24,512]{2,1,0:T(8,128)S(1)}, u32[]{:S(2)}, u32[]{:S(2)}) collective-permute-start(f32[7,24,512]{2,1,0:T(8,128)S(1)} %slice.19), channel_id=1, source_target_pairs={{0,8},{8,16},{16,24},{24,32},{32,40},{40,48},{48,56},{56,64},{64,7... | collective-permute-start | bytes 1032200 | tf_op jit(solution)/shard_map/ppermute | solution.py:284
  85.9 17.7 %collective-permute-start.7 = (f32[2,64,512]{2,1,0:T(8,128)S(1)}, f32[2,64,512]{2,1,0:T(8,128)S(1)}, u32[]{:S(2)}, u32[]{:S(2)}) collective-permute-start(f32[2,64,512]{2,1,0:T(8,128)S(1)} %collective-permute-done.5), channel_id=1, source_target_pairs={{0,504},{8,0},{16,8},{24,16},{32,24},{40,32},{48,40},{56,48},{64,5... | collective-permute-start | bytes 786440 | tf_op jit(solution)/shard_map/ppermute | solution.py:286
  101.7 13.7 %collective-permute-start.10 = (f32[7,24,512]{2,1,0:T(8,128)S(1)}, f32[7,24,512]{2,1,0:T(8,128)S(1)}, u32[]{:S(2)}, u32[]{:S(2)}) collective-permute-start(f32[7,24,512]{2,1,0:T(8,128)S(1)} %slice.18), channel_id=1, source_target_pairs={{0,8},{8,16},{16,24},{24,32},{32,40},{40,48},{48,56},{56,64},{64,7... | collective-permute-start | bytes 1032200 | tf_op jit(solution)/shard_map/ppermute | solution.py:288
  103.7 15.5 %collective-permute-start.9 = (f32[2,64,512]{2,1,0:T(8,128)S(1)}, f32[2,64,512]{2,1,0:T(8,128)S(1)}, u32[]{:S(2)}, u32[]{:S(2)}) collective-permute-start(f32[2,64,512]{2,1,0:T(8,128)S(1)} %collective-permute-done.7.two_ref), channel_id=1, source_target_pairs={{0,504},{8,0},{16,8},{24,16},{32,24},{40,32},{48,40},{56,48},{64,5... | collective-permute-start | bytes 786440 | tf_op jit(solution)/shard_map/ppermute | solution.py:290

commit v7 on v6

--- a/solution.py
+++ b/solution.py
@@ -230,8 +230,8 @@
     )(*operands)
 
 
-EARLY = (0, 7)
-BACK = (7, 9)
+EARLY = (0, 6)
+BACK = (6, 9)
 LATE = (9, 16)
 FIRST = (0, 9)
 

time: 121 us -> 123 us (1.017)
  the two profiles are of different devices: /device:TPU:1 before, /device:TPU:2 now
where the time goes in v7:
time: 123 us
  starting transfers between devices  46 us (37%)
  waiting for transfers between devices  44.4 us (36%)
  Pallas kernels  29.6 us (24%)
  local copies, waits for them, and re-layouts  2.61 us (2%)
    ppermute x1, waiting for transfers between devices, shards(): back_three_below = back_rest(back_away)  18.4 us
    pallas_call x4, Pallas kernels, sweep(): pl.pallas_call(functools.partial(sweep_kernel, lo), grid_spec=pltpu.Prefe...  11.7 us
    ppermute x1, starting transfers between devices, shards(): back_away_raw = back_first(back)  10 us
    ppermute x1, waiting for transfers between devices, shards(): back_away_raw = back_first(back)  9.42 us
    pallas_call x3, Pallas kernels, finish(): pl.pallas_call(finish_kernel if len(held) == 2 else complete_kernel, grid...  8.63 us
    ppermute x1, starting transfers between devices, shards(): back_one = unhop(back_two)  7.57 us
    pallas_call x1, Pallas kernels, length_operator(): pl.pallas_call(operator_kernel, grid_spec=pltpu.PrefetchScalarGridSpec(nu...  6.12 us
    ppermute x1, starting transfers between devices, shards(): back_three_below = back_rest(back_away)  5.2 us
  transfers between devices with their start and end apart: 12, of which 7 were waited for; matrix products, arithmetic and copies ran while one was open for 1% of the time, Pallas kernels for 21%

profile of v7, /device:TPU:2, one launch (start us, length us, event | category | flops | bytes accessed | tf_op | source)
XLA Modules:
  0.0 122.9 jit_solution(3009080079944014661)
XLA Ops:
  4.8 4.3 %collective-permute-start.2 = (f32[6,64,512]{2,1,0:T(8,128)}, f32[6,64,512]{2,1,0:T(8,128)S(1)}, u32[]{:S(2)}, u32[]{:S(2)}) collective-permute-start(f32[6,64,512]{2,1,0:T(8,128)} %get-tuple-element.25), channel_id=1, source_target_pairs={{0,8},{8,16},{16,24},{24,32},{32,40},{40,48},{48,56},{56,64},{64,7... | collective-permute-start | bytes 2359304 | tf_op jit(solution)/shard_map/ppermute | solution.py:263
  9.1 10.0 %collective-permute-start.3 = (f32[3,64,512]{2,1,0:T(8,128)}, f32[3,64,512]{2,1,0:T(8,128)}, u32[]{:S(2)}, u32[]{:S(2)}) collective-permute-start(f32[3,64,512]{2,1,0:T(8,128)} %get-tuple-element.26), channel_id=1, source_target_pairs={{0,48},{8,56},{16,0},{24,8},{32,16},{40,24},{48,32},{56,40},{64,11... | collective-permute-start | bytes 1179656 | tf_op jit(solution)/shard_map/ppermute | solution.py:264
  19.2 2.8 %sweep.4.own_ref = f32[7,64,512]{2,1,0:T(8,128)S(1)} custom-call(s32[2,16]{1,0:T(2,128)S(1)} %copy-done.4, f32[8,16]{1,0:T(8,128)S(1)} %bitcast.4, f32[16,64,512]{2,1,0:T(8,128)S(1)} %copy-done.1, f32[16,64,128]{2,1,0:T(8,128)S(1)} %collective-permute-done.edge_ref), custom_call_target="tpu_custom_call" | custom-call | flops 1 | bytes 1 | tf_op jit(solution)/shard_map/sweep/pallas_call | solution.py:61
  22.0 1.9 %collective-permute-start.1 = (f32[7,64,512]{2,1,0:T(8,128)S(1)}, f32[7,64,512]{2,1,0:T(8,128)S(1)}, u32[]{:S(2)}, u32[]{:S(2)}) collective-permute-start(f32[7,64,512]{2,1,0:T(8,128)S(1)} %sweep.4.own_ref), channel_id=1, source_target_pairs={{0,8},{8,16},{16,24},{24,32},{32,40},{40,48},{48,56},{56,64},{64,7... | collective-permute-start | bytes 2752520 | tf_op jit(solution)/shard_map/ppermute | solution.py:270
  23.9 3.4 %sweep.5.own_ref = f32[9,64,512]{2,1,0:T(8,128)S(1)} custom-call(s32[2,16]{1,0:T(2,128)S(1)} %copy-done.4, f32[8,16]{1,0:T(8,128)S(1)} %bitcast.5, f32[16,64,512]{2,1,0:T(8,128)S(1)} %copy-done.1, f32[16,64,128]{2,1,0:T(8,128)S(1)} %collective-permute-done.edge_ref), custom_call_target="tpu_custom_call" | custom-call | flops 1 | bytes 1 | tf_op jit(solution)/shard_map/sweep/pallas_call | solution.py:61
  27.4 9.4 %collective-permute-done.3.field_ref = f32[3,64,512]{2,1,0:T(8,128)} collective-permute-done((f32[3,64,512]{2,1,0:T(8,128)}, f32[3,64,512]{2,1,0:T(8,128)}, u32[]{:S(2)}, u32[]{:S(2)}) %collective-permute-start.3) | collective-permute-done | bytes 393248 | tf_op jit(solution)/shard_map/ppermute | solution.py:264
  37.8 3.4 %collective-permute-start.4 = (f32[9,64,128]{2,1,0:T(8,128)S(1)}, f32[9,64,128]{2,1,0:T(8,128)S(1)}, u32[]{:S(2)}, u32[]{:S(2)}) collective-permute-start(f32[9,64,128]{2,1,0:T(8,128)S(1)} %pad_maximum_fusion), channel_id=1, source_target_pairs={{0,1},{1,2},{2,3},{3,4},{4,5},{5,6},{6,7},{8,9},{9,10},{10,11},{11... | collective-permute-start | bytes 884744 | tf_op jit(solution)/shard_map/ppermute | solution.py:274
  41.1 4.7 %collective-permute-done.4.edge_ref = f32[9,64,128]{2,1,0:T(8,128)S(1)} collective-permute-done((f32[9,64,128]{2,1,0:T(8,128)S(1)}, f32[9,64,128]{2,1,0:T(8,128)S(1)}, u32[]{:S(2)}, u32[]{:S(2)}) %collective-permute-start.4) | collective-permute-done | bytes 294944 | tf_op jit(solution)/shard_map/ppermute | solution.py:274
  45.8 2.5 %sweep.6.one_ref = f32[6,64,512]{2,1,0:T(8,128)S(1)} custom-call(s32[2,16]{1,0:T(2,128)S(1)} %copy-done.4, f32[8,16]{1,0:T(8,128)S(1)} %bitcast.6, f32[6,64,512]{2,1,0:T(8,128)S(1)} %collective-permute-done.2.field_ref, f32[9,64,128]{2,1,0:T(8,128)S(1)} %collective-permute-done.4.edge_ref), custom_call_target="tpu_custom_call" | custom-call | flops 1 | bytes 1 | tf_op jit(solution)/shard_map/sweep/pallas_call | solution.py:61
  48.3 2.0 %collective-permute-start.6 = (f32[6,64,512]{2,1,0:T(8,128)S(1)}, f32[6,64,512]{2,1,0:T(8,128)S(1)}, u32[]{:S(2)}, u32[]{:S(2)}) collective-permute-start(f32[6,64,512]{2,1,0:T(8,128)S(1)} %sweep.6.one_ref), channel_id=1, source_target_pairs={{0,8},{8,16},{16,24},{24,32},{32,40},{40,48},{48,56},{56,64},{64,7... | collective-permute-start | bytes 2359304 | tf_op jit(solution)/shard_map/ppermute | solution.py:276
  50.3 3.1 %sweep.7 = f32[3,64,512]{2,1,0:T(8,128)S(1)} custom-call(s32[2,16]{1,0:T(2,128)S(1)} %copy-done.4, f32[8,16]{1,0:T(8,128)S(1)} %bitcast.7, f32[3,64,512]{2,1,0:T(8,128)} %collective-permute-done.3.field_ref, f32[9,64,128]{2,1,0:T(8,128)S(1)} %collective-permute-done.4.edge_ref), custom_call_target="tpu_custom_call" | custom-call | flops 1 | bytes 1 | tf_op jit(solution)/shard_map/sweep/pallas_call | solution.py:61
  53.4 2.7 %collective-permute-done.1.one_ref = f32[7,64,512]{2,1,0:T(8,128)S(1)} collective-permute-done((f32[7,64,512]{2,1,0:T(8,128)S(1)}, f32[7,64,512]{2,1,0:T(8,128)S(1)}, u32[]{:S(2)}, u32[]{:S(2)}) %collective-permute-start.1) | collective-permute-done | bytes 917536 | tf_op jit(solution)/shard_map/ppermute | solution.py:270
  56.0 1.9 %collective-permute-start.8 = (f32[7,64,512]{2,1,0:T(8,128)S(1)}, f32[7,64,512]{2,1,0:T(8,128)S(1)}, u32[]{:S(2)}, u32[]{:S(2)}) collective-permute-start(f32[7,64,512]{2,1,0:T(8,128)S(1)} %collective-permute-done.1.one_ref), channel_id=1, source_target_pairs={{0,8},{8,16},{16,24},{24,32},{32,40},{40,48},{48,56},{56,64},{64,7... | collective-permute-start | bytes 2752520 | tf_op jit(solution)/shard_map/ppermute | solution.py:280
  58.0 5.2 %collective-permute-start.5 = (f32[3,64,512]{2,1,0:T(8,128)S(1)}, f32[3,64,512]{2,1,0:T(8,128)S(1)}, u32[]{:S(2)}, u32[]{:S(2)}) collective-permute-start(f32[3,64,512]{2,1,0:T(8,128)S(1)} %sweep.7), channel_id=1, source_target_pairs={{48,24},{56,32},{0,40},{8,48},{16,56},{24,64},{32,72},{40,80},{112... | collective-permute-start | bytes 1179656 | tf_op jit(solution)/shard_map/ppermute | solution.py:278
  63.2 6.1 %operator.1.op_ref = bf16[16,256,216]{2,1,0:T(8,128)(2,1)S(1)} custom-call(s32[1]{0:T(128)} %bitcast.me_ref, s32[3,64]{1,0:T(4,128)S(1)} %bitcast.9, s32[2,16]{1,0:T(2,128)S(1)} %copy-done.7, f32[8,16]{1,0:T(8,128)S(1)} %bitcast.8, f32[4,64,64]{2,1,0:T(8,128)S(1)} %copy-done.2, f32[4,64,64]{2,1,0:T(8,128)S(1)} %copy-done.2, f32[4,64,64]{2,1,0:T(8,128)S(1)} %copy-done.2), custom_call_target="tpu_custom_call" | custom-call | flops 1 | bytes 1 | tf_op jit(solution)/shard_map/operator/pallas_call | solution.py:131
  71.1 2.8 %collective-permute-done.6.two_ref = f32[6,64,512]{2,1,0:T(8,128)S(1)} collective-permute-done((f32[6,64,512]{2,1,0:T(8,128)S(1)}, f32[6,64,512]{2,1,0:T(8,128)S(1)}, u32[]{:S(2)}, u32[]{:S(2)}) %collective-permute-start.6) | collective-permute-done | bytes 786464 | tf_op jit(solution)/shard_map/ppermute | solution.py:276
  74.0 18.4 %collective-permute-done.5 = f32[3,64,512]{2,1,0:T(8,128)S(1)} collective-permute-done((f32[3,64,512]{2,1,0:T(8,128)S(1)}, f32[3,64,512]{2,1,0:T(8,128)S(1)}, u32[]{:S(2)}, u32[]{:S(2)}) %collective-permute-start.5) | collective-permute-done | bytes 393248 | tf_op jit(solution)/shard_map/ppermute | solution.py:278
  92.4 3.7 %collective-permute-start.7 = (f32[3,64,512]{2,1,0:T(8,128)S(1)}, f32[3,64,512]{2,1,0:T(8,128)S(1)}, u32[]{:S(2)}, u32[]{:S(2)}) collective-permute-start(f32[3,64,512]{2,1,0:T(8,128)S(1)} %collective-permute-done.5), channel_id=1, source_target_pairs={{0,504},{8,0},{16,8},{24,16},{32,24},{40,32},{48,40},{56,48},{64,5... | collective-permute-start | bytes 1179656 | tf_op jit(solution)/shard_map/ppermute | solution.py:286
  96.1 2.2 %collective-permute-start.11 = (f32[6,24,512]{2,1,0:T(8,128)S(1)}, f32[6,24,512]{2,1,0:T(8,128)S(1)}, u32[]{:S(2)}, u32[]{:S(2)}) collective-permute-start(f32[6,24,512]{2,1,0:T(8,128)S(1)} %slice.19), channel_id=1, source_target_pairs={{0,8},{8,16},{16,24},{24,32},{32,40},{40,48},{48,56},{56,64},{64,7... | collective-permute-start | bytes 884744 | tf_op jit(solution)/shard_map/ppermute | solution.py:284
  98.3 1.9 %collective-permute-start.10 = (f32[7,24,512]{2,1,0:T(8,128)S(1)}, f32[7,24,512]{2,1,0:T(8,128)S(1)}, u32[]{:S(2)}, u32[]{:S(2)}) collective-permute-start(f32[7,24,512]{2,1,0:T(8,128)S(1)} %slice.18), channel_id=1, source_target_pairs={{0,8},{8,16},{16,24},{24,32},{32,40},{40,48},{48,56},{56,64},{64,7... | collective-permute-start | bytes 1032200 | tf_op jit(solution)/shard_map/ppermute | solution.py:288
  100.2 4.5 %collective-permute-done.7.two_ref = f32[3,64,512]{2,1,0:T(8,128)S(1)} collective-permute-done((f32[3,64,512]{2,1,0:T(8,128)S(1)}, f32[3,64,512]{2,1,0:T(8,128)S(1)}, u32[]{:S(2)}, u32[]{:S(2)}) %collective-permute-start.7) | collective-permute-done | bytes 393248 | tf_op jit(solution)/shard_map/ppermute | solution.py:286
  104.7 7.6 %collective-permute-start.9 = (f32[3,64,512]{2,1,0:T(8,128)S(1)}, f32[3,64,512]{2,1,0:T(8,128)S(1)}, u32[]{:S(2)}, u32[]{:S(2)}) collective-permute-start(f32[3,64,512]{2,1,0:T(8,128)S(1)} %collective-permute-done.7.two_ref), channel_id=1, source_target_pairs={{0,504},{8,0},{16,8},{24,16},{32,24},{40,32},{48,40},{56,48},{64,5... | collective-permute-start | bytes 1179656 | tf_op jit(solution)/shard_map/ppermute | solution.py:290
  112.3 3.1 %finish.3.rest_0_ = f32[16,64,512]{2,1,0:T(8,128)} custom-call(bf16[16,256,216]{2,1,0:T(8,128)(2,1)S(1)} %operator.1.op_ref, f32[9,64,512]{2,1,0:T(8,128)S(1)} %sweep.5.own_ref, f32[6,64,512]{2,1,0:T(8,128)S(1)} %sweep.6.one_ref, f32[6,64,512]{2,1,0:T(8,128)S(1)} %collective-permute-done.6.two_ref, f32[6,24,512]{2,1,0:T(8,128)S(1)} %collective-permute-done.11.rim_ref), custom_call_target="tpu_custom_call" | custom-call | flops 1000000000 | bytes 1 | tf_op jit(solution)/shard_map/finish/pallas_call | solution.py:219
  117.3 3.7 %finish.4.rest_0_ = f32[16,64,512]{2,1,0:T(8,128)} custom-call(bf16[16,256,216]{2,1,0:T(8,128)(2,1)S(1)} %operator.1.op_ref, f32[7,128,512]{2,1,0:T(8,128)S(1)} %prepare.1.sum_ref, f32[7,64,512]{2,1,0:T(8,128)S(1)} %collective-permute-done.8.two_ref, f32[7,24,512]{2,1,0:T(8,128)S(1)} %collective-permute-done.10.rim_ref, ...), custom_call_target="tpu_custom_call", output_to_operand_aliasing={{}: (4, {})} | custom-call | flops 1000000000 | bytes 1 | tf_op jit(solution)/shard_map/finish/pallas_call | solution.py:219
  (32 shorter events, 11.4 us)
Async XLA Ops:
  0.0 1.6 %copy-start = (f32[16,64,512]{2,1,0:T(8,128)S(1)}, f32[16,64,512]{2,1,0:T(8,128)}, u32[]{:S(2)}) copy-start(f32[16,64,512]{2,1,0:T(8,128)} %field_ref.5) | copy-start | bytes 6291460
  1.6 17.6 %copy-start.1 = (f32[16,64,512]{2,1,0:T(8,128)S(1)}, f32[16,64,512]{2,1,0:T(8,128)}, u32[]{:S(2)}) copy-start(f32[16,64,512]{2,1,0:T(8,128)} %field_ref.5) | copy-start | bytes 6291460
  1.6 17.6 %copy-start.3 = (f32[16,8]{0,1:T(8,128)S(1)}, f32[16,8]{0,1:T(8,128)}, u32[]{:S(2)}) copy-start(f32[16,8]{0,1:T(8,128)} %param.11) | copy-start | bytes 1540
  1.6 17.6 %copy-start.4 = (s32[2,16]{1,0:T(2,128)S(1)}, s32[2,16]{1,0:T(2,128)}, u32[]{:S(2)}) copy-start(s32[2,16]{1,0:T(2,128)} %band_ref.8) | copy-start | bytes 388
  2.9 16.3 %collective-permute-start = (f32[16,64,128]{2,1,0:T(8,128)}, f32[16,64,128]{2,1,0:T(8,128)S(1)}, u32[]{:S(2)}, u32[]{:S(2)}) collective-permute-start(f32[16,64,128]{2,1,0:T(8,128)} %get-tuple-element.22), channel_id=1, source_target_pairs={{0,1},{1,2},{2,3},{3,4},{4,5},{5,6},{6,7},{8,9},{9,10},{10,11},{11... | collective-permute-start | bytes 1572872 | tf_op jit(solution)/shard_map/ppermute | solution.py:265
  4.8 32.0 %collective-permute-start.2 = (f32[6,64,512]{2,1,0:T(8,128)}, f32[6,64,512]{2,1,0:T(8,128)S(1)}, u32[]{:S(2)}, u32[]{:S(2)}) collective-permute-start(f32[6,64,512]{2,1,0:T(8,128)} %get-tuple-element.25), channel_id=1, source_target_pairs={{0,8},{8,16},{16,24},{24,32},{32,40},{40,48},{48,56},{56,64},{64,7... | collective-permute-start | bytes 2359304 | tf_op jit(solution)/shard_map/ppermute | solution.py:263
  9.1 27.7 %collective-permute-start.3 = (f32[3,64,512]{2,1,0:T(8,128)}, f32[3,64,512]{2,1,0:T(8,128)}, u32[]{:S(2)}, u32[]{:S(2)}) collective-permute-start(f32[3,64,512]{2,1,0:T(8,128)} %get-tuple-element.26), channel_id=1, source_target_pairs={{0,48},{8,56},{16,0},{24,8},{32,16},{40,24},{48,32},{56,40},{64,11... | collective-permute-start | bytes 1179656 | tf_op jit(solution)/shard_map/ppermute | solution.py:264
  22.0 34.0 %collective-permute-start.1 = (f32[7,64,512]{2,1,0:T(8,128)S(1)}, f32[7,64,512]{2,1,0:T(8,128)S(1)}, u32[]{:S(2)}, u32[]{:S(2)}) collective-permute-start(f32[7,64,512]{2,1,0:T(8,128)S(1)} %sweep.4.own_ref), channel_id=1, source_target_pairs={{0,8},{8,16},{16,24},{24,32},{32,40},{40,48},{48,56},{56,64},{64,7... | collective-permute-start | bytes 2752520 | tf_op jit(solution)/shard_map/ppermute | solution.py:270
  27.3 35.8 %copy-start.2 = (f32[4,64,64]{2,1,0:T(8,128)S(1)}, f32[4,64,64]{2,1,0:T(8,128)}, u32[]{:S(2)}) copy-start(f32[4,64,64]{2,1,0:T(8,128)} %two_ref.1) | copy-start | bytes 196612
  27.3 35.8 %copy-start.5 = (f32[16,8]{0,1:T(8,128)S(1)}, f32[16,8]{0,1:T(8,128)}, u32[]{:S(2)}) copy-start(f32[16,8]{0,1:T(8,128)} %param.10) | copy-start | bytes 1540
  27.3 35.8 %copy-start.6 = (s32[64,3]{0,1:T(4,128)S(1)}, s32[64,3]{0,1:T(4,128)}, u32[]{:S(2)}) copy-start(s32[64,3]{0,1:T(4,128)} %param.12) | copy-start | bytes 2308
  27.4 35.8 %copy-start.7 = (s32[2,16]{1,0:T(2,128)S(1)}, s32[2,16]{1,0:T(2,128)}, u32[]{:S(2)}) copy-start(s32[2,16]{1,0:T(2,128)} %band_ref.9) | copy-start | bytes 388
  37.8 8.0 %collective-permute-start.4 = (f32[9,64,128]{2,1,0:T(8,128)S(1)}, f32[9,64,128]{2,1,0:T(8,128)S(1)}, u32[]{:S(2)}, u32[]{:S(2)}) collective-permute-start(f32[9,64,128]{2,1,0:T(8,128)S(1)} %pad_maximum_fusion), channel_id=1, source_target_pairs={{0,1},{1,2},{2,3},{3,4},{4,5},{5,6},{6,7},{8,9},{9,10},{10,11},{11... | collective-permute-start | bytes 884744 | tf_op jit(solution)/shard_map/ppermute | solution.py:274
  48.3 25.7 %collective-permute-start.6 = (f32[6,64,512]{2,1,0:T(8,128)S(1)}, f32[6,64,512]{2,1,0:T(8,128)S(1)}, u32[]{:S(2)}, u32[]{:S(2)}) collective-permute-start(f32[6,64,512]{2,1,0:T(8,128)S(1)} %sweep.6.one_ref), channel_id=1, source_target_pairs={{0,8},{8,16},{16,24},{24,32},{32,40},{40,48},{48,56},{56,64},{64,7... | collective-permute-start | bytes 2359304 | tf_op jit(solution)/shard_map/ppermute | solution.py:276
  56.0 42.2 %collective-permute-start.8 = (f32[7,64,512]{2,1,0:T(8,128)S(1)}, f32[7,64,512]{2,1,0:T(8,128)S(1)}, u32[]{:S(2)}, u32[]{:S(2)}) collective-permute-start(f32[7,64,512]{2,1,0:T(8,128)S(1)} %collective-permute-done.1.one_ref), channel_id=1, source_target_pairs={{0,8},{8,16},{16,24},{24,32},{32,40},{40,48},{48,56},{56,64},{64,7... | collective-permute-start | bytes 2752520 | tf_op jit(solution)/shard_map/ppermute | solution.py:280
  58.0 34.4 %collective-permute-start.5 = (f32[3,64,512]{2,1,0:T(8,128)S(1)}, f32[3,64,512]{2,1,0:T(8,128)S(1)}, u32[]{:S(2)}, u32[]{:S(2)}) collective-permute-start(f32[3,64,512]{2,1,0:T(8,128)S(1)} %sweep.7), channel_id=1, source_target_pairs={{48,24},{56,32},{0,40},{8,48},{16,56},{24,64},{32,72},{40,80},{112... | collective-permute-start | bytes 1179656 | tf_op jit(solution)/shard_map/ppermute | solution.py:278
  92.4 12.3 %collective-permute-start.7 = (f32[3,64,512]{2,1,0:T(8,128)S(1)}, f32[3,64,512]{2,1,0:T(8,128)S(1)}, u32[]{:S(2)}, u32[]{:S(2)}) collective-permute-start(f32[3,64,512]{2,1,0:T(8,128)S(1)} %collective-permute-done.5), channel_id=1, source_target_pairs={{0,504},{8,0},{16,8},{24,16},{32,24},{40,32},{48,40},{56,48},{64,5... | collective-permute-start | bytes 1179656 | tf_op jit(solution)/shard_map/ppermute | solution.py:286
  96.1 16.2 %collective-permute-start.11 = (f32[6,24,512]{2,1,0:T(8,128)S(1)}, f32[6,24,512]{2,1,0:T(8,128)S(1)}, u32[]{:S(2)}, u32[]{:S(2)}) collective-permute-start(f32[6,24,512]{2,1,0:T(8,128)S(1)} %slice.19), channel_id=1, source_target_pairs={{0,8},{8,16},{16,24},{24,32},{32,40},{40,48},{48,56},{56,64},{64,7... | collective-permute-start | bytes 884744 | tf_op jit(solution)/shard_map/ppermute | solution.py:284
  98.3 19.0 %collective-permute-start.10 = (f32[7,24,512]{2,1,0:T(8,128)S(1)}, f32[7,24,512]{2,1,0:T(8,128)S(1)}, u32[]{:S(2)}, u32[]{:S(2)}) collective-permute-start(f32[7,24,512]{2,1,0:T(8,128)S(1)} %slice.18), channel_id=1, source_target_pairs={{0,8},{8,16},{16,24},{24,32},{32,40},{40,48},{48,56},{56,64},{64,7... | collective-permute-start | bytes 1032200 | tf_op jit(solution)/shard_map/ppermute | solution.py:288
  104.7 16.3 %collective-permute-start.9 = (f32[3,64,512]{2,1,0:T(8,128)S(1)}, f32[3,64,512]{2,1,0:T(8,128)S(1)}, u32[]{:S(2)}, u32[]{:S(2)}) collective-permute-start(f32[3,64,512]{2,1,0:T(8,128)S(1)} %collective-permute-done.7.two_ref), channel_id=1, source_target_pairs={{0,504},{8,0},{16,8},{24,16},{32,24},{40,32},{48,40},{56,48},{64,5... | collective-permute-start | bytes 1179656 | tf_op jit(solution)/shard_map/ppermute | solution.py:290

commit v8 on v7

--- a/solution.py
+++ b/solution.py
@@ -142,7 +142,7 @@
         ),
         out_shape=jax.ShapeDtypeStruct((batches, 4 * tile_len, depth), jnp.bfloat16),
         compiler_params=pltpu.CompilerParams(vmem_limit_bytes=VMEM),
-        cost_estimate=cost(1),
+        cost_estimate=cost(10000000000),
         name="operator",
     )(me, pairs, band, taps, agg_kern, agg_kern, agg_kern)
 
@@ -272,7 +272,7 @@
     early_one_raw, back_away_raw, first_own = lax.optimization_barrier((early_one_raw, back_away_raw, first_own))
 
     first_edge = side(jnp.concatenate([early_one_raw[:, :, margin:], back_away_raw[:, :, margin:]], axis=0))
-    early_one = sweep(early_one_raw, first_edge, *wide, EARLY, 0, 0, 1)
+    early_one = sweep(early_one_raw, first_edge, *wide, EARLY, 0, 0, 4000000000)
     early_two = hop(early_one)
     back_away = sweep(back_away_raw, after(first_edge, early_one), *wide, BACK, 0, EARLY[1])
     back_three_below = back_rest(back_away)

time: 123 us -> 118 us (0.959)
  waiting for transfers between devices: 44.4 us -> 35.2 us
  starting transfers between devices: 46 us -> 48.9 us
    ppermute x1, waiting for transfers between devices: 18.4 us -> 11.6 us  [shards(): back_three_below = back_rest(back_away)]
    ppermute x1, waiting for transfers between devices: 2.66 us -> 0.01 us  [shards(): late_one = hop(late_own)]
    ppermute x1, starting transfers between devices: 5.2 us -> 7.84 us  [shards(): back_three_below = back_rest(back_away)]
    ppermute x1, waiting for transfers between devices: 4.47 us -> 2.34 us  [shards(): back_two = unhop(back_three_below)]
    ppermute x1, waiting for transfers between devices: 2.82 us -> 4.43 us  [shards(): early_two = hop(early_one)]
  transfers between devices with their start and end apart: 12 -> 12, of which waited for: 7 -> 7; matrix products, arithmetic and copies ran while one was open for 1% -> 1% of each run, Pallas kernels for 21% -> 23%
where the time goes in v8:
time: 118 us; the launch traced here: 117 us
  starting transfers between devices  48.9 us (41%)
  waiting for transfers between devices  35.2 us (30%)
  Pallas kernels  30 us (25%)
  local copies, waits for them, and re-layouts  2.64 us (2%)
    pallas_call x4, Pallas kernels, sweep(): pl.pallas_call(functools.partial(sweep_kernel, lo), grid_spec=pltpu.Prefe...  12.3 us
    ppermute x1, waiting for transfers between devices, shards(): back_three_below = back_rest(back_away)  11.6 us
    ppermute x1, starting transfers between devices, shards(): back_away_raw = back_first(back)  10 us
    pallas_call x3, Pallas kernels, finish(): pl.pallas_call(finish_kernel if len(held) == 2 else complete_kernel, grid...  8.63 us
    ppermute x1, waiting for transfers between devices, shards(): back_away_raw = back_first(back)  8.39 us
    ppermute x1, starting transfers between devices, shards(): back_three_below = back_rest(back_away)  7.84 us
    ppermute x1, starting transfers between devices, shards(): back_one = unhop(back_two)  7.7 us
    pallas_call x1, Pallas kernels, length_operator(): pl.pallas_call(operator_kernel, grid_spec=pltpu.PrefetchScalarGridSpec(nu...  6.12 us
  transfers between devices with their start and end apart: 12, of which 7 were waited for; matrix products, arithmetic and copies ran while one was open for 1% of the time, Pallas kernels for 23%

profile of v8, /device:TPU:2, one launch (start us, length us, event | category | flops | bytes accessed | tf_op | source)
XLA Modules:
  0.0 117.1 jit_solution(7850194975354333624)
XLA Ops:
  2.7 4.3 %collective-permute-start.2 = (f32[6,64,512]{2,1,0:T(8,128)}, f32[6,64,512]{2,1,0:T(8,128)}, u32[]{:S(2)}, u32[]{:S(2)}) collective-permute-start(f32[6,64,512]{2,1,0:T(8,128)} %get-tuple-element.25), channel_id=1, source_target_pairs={{0,8},{8,16},{16,24},{24,32},{32,40},{40,48},{48,56},{56,64},{64,7... | collective-permute-start | bytes 2359304 | tf_op jit(solution)/shard_map/ppermute | solution.py:263
  7.0 1.9 %collective-permute-start = (f32[16,64,128]{2,1,0:T(8,128)S(1)}, f32[16,64,128]{2,1,0:T(8,128)S(1)}, u32[]{:S(2)}, u32[]{:S(2)}) collective-permute-start(f32[16,64,128]{2,1,0:T(8,128)S(1)} %get-tuple-element.22), channel_id=1, source_target_pairs={{0,1},{1,2},{2,3},{3,4},{4,5},{5,6},{6,7},{8,9},{9,10},{10,11},{11... | collective-permute-start | bytes 1572872 | tf_op jit(solution)/shard_map/ppermute | solution.py:265
  8.9 10.0 %collective-permute-start.3 = (f32[3,64,512]{2,1,0:T(8,128)}, f32[3,64,512]{2,1,0:T(8,128)S(1)}, u32[]{:S(2)}, u32[]{:S(2)}) collective-permute-start(f32[3,64,512]{2,1,0:T(8,128)} %get-tuple-element.26), channel_id=1, source_target_pairs={{0,48},{8,56},{16,0},{24,8},{32,16},{40,24},{48,32},{56,40},{64,11... | collective-permute-start | bytes 1179656 | tf_op jit(solution)/shard_map/ppermute | solution.py:264
  19.0 2.8 %sweep.4.own_ref = f32[7,64,512]{2,1,0:T(8,128)S(1)} custom-call(s32[2,16]{1,0:T(2,128)S(1)} %copy-done.3, f32[8,16]{1,0:T(8,128)S(1)} %bitcast.4, f32[16,64,512]{2,1,0:T(8,128)S(1)} %copy-done.1, f32[16,64,128]{2,1,0:T(8,128)S(1)} %collective-permute-done.edge_ref), custom_call_target="tpu_custom_call" | custom-call | flops 1 | bytes 1 | tf_op jit(solution)/shard_map/sweep/pallas_call | solution.py:61
  21.8 2.8 %collective-permute-start.1 = (f32[7,64,512]{2,1,0:T(8,128)S(1)}, f32[7,64,512]{2,1,0:T(8,128)S(1)}, u32[]{:S(2)}, u32[]{:S(2)}) collective-permute-start(f32[7,64,512]{2,1,0:T(8,128)S(1)} %sweep.4.own_ref), channel_id=1, source_target_pairs={{0,8},{8,16},{16,24},{24,32},{32,40},{40,48},{48,56},{56,64},{64,7... | collective-permute-start | bytes 2752520 | tf_op jit(solution)/shard_map/ppermute | solution.py:270
  24.6 3.4 %sweep.5.own_ref = f32[9,64,512]{2,1,0:T(8,128)S(1)} custom-call(s32[2,16]{1,0:T(2,128)S(1)} %copy-done.3, f32[8,16]{1,0:T(8,128)S(1)} %bitcast.5, f32[16,64,512]{2,1,0:T(8,128)S(1)} %copy-done.1, f32[16,64,128]{2,1,0:T(8,128)S(1)} %collective-permute-done.edge_ref), custom_call_target="tpu_custom_call" | custom-call | flops 1 | bytes 1 | tf_op jit(solution)/shard_map/sweep/pallas_call | solution.py:61
  28.0 8.4 %collective-permute-done.3.field_ref = f32[3,64,512]{2,1,0:T(8,128)S(1)} collective-permute-done((f32[3,64,512]{2,1,0:T(8,128)}, f32[3,64,512]{2,1,0:T(8,128)S(1)}, u32[]{:S(2)}, u32[]{:S(2)}) %collective-permute-start.3) | collective-permute-done | bytes 393248 | tf_op jit(solution)/shard_map/ppermute | solution.py:264
  37.5 2.7 %collective-permute-start.4 = (f32[9,64,128]{2,1,0:T(8,128)S(1)}, f32[9,64,128]{2,1,0:T(8,128)S(1)}, u32[]{:S(2)}, u32[]{:S(2)}) collective-permute-start(f32[9,64,128]{2,1,0:T(8,128)S(1)} %pad_maximum_fusion), channel_id=1, source_target_pairs={{0,1},{1,2},{2,3},{3,4},{4,5},{5,6},{6,7},{8,9},{9,10},{10,11},{11... | collective-permute-start | bytes 884744 | tf_op jit(solution)/shard_map/ppermute | solution.py:274
  40.2 5.4 %collective-permute-done.4.edge_ref = f32[9,64,128]{2,1,0:T(8,128)S(1)} collective-permute-done((f32[9,64,128]{2,1,0:T(8,128)S(1)}, f32[9,64,128]{2,1,0:T(8,128)S(1)}, u32[]{:S(2)}, u32[]{:S(2)}) %collective-permute-start.4) | collective-permute-done | bytes 294944 | tf_op jit(solution)/shard_map/ppermute | solution.py:274
  45.6 4.6 %sweep.6.one_ref = f32[6,64,512]{2,1,0:T(8,128)S(1)} custom-call(s32[2,16]{1,0:T(2,128)S(1)} %copy-done.3, f32[8,16]{1,0:T(8,128)S(1)} %bitcast.6, f32[6,64,512]{2,1,0:T(8,128)} %collective-permute-done.2.field_ref, f32[9,64,128]{2,1,0:T(8,128)S(1)} %collective-permute-done.4.edge_ref), custom_call_target="tpu_custom_call" | custom-call | flops 4000000000 | bytes 1 | tf_op jit(solution)/shard_map/sweep/pallas_call | solution.py:61
  50.2 1.9 %collective-permute-start.6 = (f32[6,64,512]{2,1,0:T(8,128)S(1)}, f32[6,64,512]{2,1,0:T(8,128)S(1)}, u32[]{:S(2)}, u32[]{:S(2)}) collective-permute-start(f32[6,64,512]{2,1,0:T(8,128)S(1)} %sweep.6.one_ref), channel_id=1, source_target_pairs={{0,8},{8,16},{16,24},{24,32},{32,40},{40,48},{48,56},{56,64},{64,7... | collective-permute-start | bytes 2359304 | tf_op jit(solution)/shard_map/ppermute | solution.py:276
  53.7 7.8 %collective-permute-start.5 = (f32[3,64,512]{2,1,0:T(8,128)S(1)}, f32[3,64,512]{2,1,0:T(8,128)S(1)}, u32[]{:S(2)}, u32[]{:S(2)}) collective-permute-start(f32[3,64,512]{2,1,0:T(8,128)S(1)} %sweep.7), channel_id=1, source_target_pairs={{48,24},{56,32},{0,40},{8,48},{16,56},{24,64},{32,72},{40,80},{112... | collective-permute-start | bytes 1179656 | tf_op jit(solution)/shard_map/ppermute | solution.py:278
  61.6 1.9 %collective-permute-start.8 = (f32[7,64,512]{2,1,0:T(8,128)S(1)}, f32[7,64,512]{2,1,0:T(8,128)S(1)}, u32[]{:S(2)}, u32[]{:S(2)}) collective-permute-start(f32[7,64,512]{2,1,0:T(8,128)S(1)} %collective-permute-done.1.one_ref), channel_id=1, source_target_pairs={{0,8},{8,16},{16,24},{24,32},{32,40},{40,48},{48,56},{56,64},{64,7... | collective-permute-start | bytes 2752520 | tf_op jit(solution)/shard_map/ppermute | solution.py:280
  63.6 6.1 %operator.1.op_ref = bf16[16,256,216]{2,1,0:T(8,128)(2,1)S(1)} custom-call(s32[1]{0:T(128)} %bitcast.me_ref, s32[3,64]{1,0:T(4,128)S(1)} %bitcast.9, s32[2,16]{1,0:T(2,128)S(1)} %copy-done.7, f32[8,16]{1,0:T(8,128)S(1)} %bitcast.8, f32[4,64,64]{2,1,0:T(8,128)S(1)} %copy-done.4, f32[4,64,64]{2,1,0:T(8,128)S(1)} %copy-done.4, f32[4,64,64]{2,1,0:T(8,128)S(1)} %copy-done.4), custom_call_target="tpu_custom_call" | custom-call | flops 10000000000 | bytes 1 | tf_op jit(solution)/shard_map/operator/pallas_call | solution.py:131
  71.5 4.4 %collective-permute-done.6.two_ref = f32[6,64,512]{2,1,0:T(8,128)S(1)} collective-permute-done((f32[6,64,512]{2,1,0:T(8,128)S(1)}, f32[6,64,512]{2,1,0:T(8,128)S(1)}, u32[]{:S(2)}, u32[]{:S(2)}) %collective-permute-start.6) | collective-permute-done | bytes 786464 | tf_op jit(solution)/shard_map/ppermute | solution.py:276
  75.9 11.6 %collective-permute-done.5 = f32[3,64,512]{2,1,0:T(8,128)S(1)} collective-permute-done((f32[3,64,512]{2,1,0:T(8,128)S(1)}, f32[3,64,512]{2,1,0:T(8,128)S(1)}, u32[]{:S(2)}, u32[]{:S(2)}) %collective-permute-start.5) | collective-permute-done | bytes 393248 | tf_op jit(solution)/shard_map/ppermute | solution.py:278
  87.6 2.9 %collective-permute-start.7 = (f32[3,64,512]{2,1,0:T(8,128)S(1)}, f32[3,64,512]{2,1,0:T(8,128)S(1)}, u32[]{:S(2)}, u32[]{:S(2)}) collective-permute-start(f32[3,64,512]{2,1,0:T(8,128)S(1)} %collective-permute-done.5), channel_id=1, source_target_pairs={{0,504},{8,0},{16,8},{24,16},{32,24},{40,32},{48,40},{56,48},{64,5... | collective-permute-start | bytes 1179656 | tf_op jit(solution)/shard_map/ppermute | solution.py:286
  90.5 2.9 %collective-permute-start.11 = (f32[6,24,512]{2,1,0:T(8,128)S(1)}, f32[6,24,512]{2,1,0:T(8,128)S(1)}, u32[]{:S(2)}, u32[]{:S(2)}) collective-permute-start(f32[6,24,512]{2,1,0:T(8,128)S(1)} %slice.19), channel_id=1, source_target_pairs={{0,8},{8,16},{16,24},{24,32},{32,40},{40,48},{48,56},{56,64},{64,7... | collective-permute-start | bytes 884744 | tf_op jit(solution)/shard_map/ppermute | solution.py:284
  94.0 1.9 %collective-permute-start.10 = (f32[7,24,512]{2,1,0:T(8,128)S(1)}, f32[7,24,512]{2,1,0:T(8,128)S(1)}, u32[]{:S(2)}, u32[]{:S(2)}) collective-permute-start(f32[7,24,512]{2,1,0:T(8,128)S(1)} %slice.18), channel_id=1, source_target_pairs={{0,8},{8,16},{16,24},{24,32},{32,40},{40,48},{48,56},{56,64},{64,7... | collective-permute-start | bytes 1032200 | tf_op jit(solution)/shard_map/ppermute | solution.py:288
  95.9 2.3 %collective-permute-done.7.two_ref = f32[3,64,512]{2,1,0:T(8,128)S(1)} collective-permute-done((f32[3,64,512]{2,1,0:T(8,128)S(1)}, f32[3,64,512]{2,1,0:T(8,128)S(1)}, u32[]{:S(2)}, u32[]{:S(2)}) %collective-permute-start.7) | collective-permute-done | bytes 393248 | tf_op jit(solution)/shard_map/ppermute | solution.py:286
  98.2 7.7 %collective-permute-start.9 = (f32[3,64,512]{2,1,0:T(8,128)S(1)}, f32[3,64,512]{2,1,0:T(8,128)S(1)}, u32[]{:S(2)}, u32[]{:S(2)}) collective-permute-start(f32[3,64,512]{2,1,0:T(8,128)S(1)} %collective-permute-done.7.two_ref), channel_id=1, source_target_pairs={{0,504},{8,0},{16,8},{24,16},{32,24},{40,32},{48,40},{56,48},{64,5... | collective-permute-start | bytes 1179656 | tf_op jit(solution)/shard_map/ppermute | solution.py:290
  106.0 3.1 %finish.3.rest_0_ = f32[16,64,512]{2,1,0:T(8,128)} custom-call(bf16[16,256,216]{2,1,0:T(8,128)(2,1)S(1)} %operator.1.op_ref, f32[9,64,512]{2,1,0:T(8,128)S(1)} %sweep.5.own_ref, f32[6,64,512]{2,1,0:T(8,128)S(1)} %sweep.6.one_ref, f32[6,64,512]{2,1,0:T(8,128)S(1)} %collective-permute-done.6.two_ref, f32[6,24,512]{2,1,0:T(8,128)S(1)} %collective-permute-done.11.rim_ref), custom_call_target="tpu_custom_call" | custom-call | flops 1000000000 | bytes 1 | tf_op jit(solution)/shard_map/finish/pallas_call | solution.py:219
  109.1 2.5 %collective-permute-done.10.rim_ref = f32[7,24,512]{2,1,0:T(8,128)S(1)} collective-permute-done((f32[7,24,512]{2,1,0:T(8,128)S(1)}, f32[7,24,512]{2,1,0:T(8,128)S(1)}, u32[]{:S(2)}, u32[]{:S(2)}) %collective-permute-start.10) | collective-permute-done | bytes 344096 | tf_op jit(solution)/shard_map/ppermute | solution.py:288
  111.6 3.7 %finish.4.rest_0_ = f32[16,64,512]{2,1,0:T(8,128)} custom-call(bf16[16,256,216]{2,1,0:T(8,128)(2,1)S(1)} %operator.1.op_ref, f32[7,128,512]{2,1,0:T(8,128)S(1)} %prepare.1.sum_ref, f32[7,64,512]{2,1,0:T(8,128)S(1)} %collective-permute-done.8.two_ref, f32[7,24,512]{2,1,0:T(8,128)S(1)} %collective-permute-done.10.rim_ref, ...), custom_call_target="tpu_custom_call", output_to_operand_aliasing={{}: (4, {})} | custom-call | flops 1000000000 | bytes 1 | tf_op jit(solution)/shard_map/finish/pallas_call | solution.py:219
  (32 shorter events, 9.5 us)
Async XLA Ops:
  0.0 1.6 %copy-start = (f32[16,64,512]{2,1,0:T(8,128)S(1)}, f32[16,64,512]{2,1,0:T(8,128)}, u32[]{:S(2)}) copy-start(f32[16,64,512]{2,1,0:T(8,128)} %field_ref.5) | copy-start | bytes 6291460
  1.6 17.4 %copy-start.1 = (f32[16,64,512]{2,1,0:T(8,128)S(1)}, f32[16,64,512]{2,1,0:T(8,128)}, u32[]{:S(2)}) copy-start(f32[16,64,512]{2,1,0:T(8,128)} %field_ref.5) | copy-start | bytes 6291460
  1.6 17.4 %copy-start.2 = (f32[16,8]{0,1:T(8,128)S(1)}, f32[16,8]{0,1:T(8,128)}, u32[]{:S(2)}) copy-start(f32[16,8]{0,1:T(8,128)} %param.11) | copy-start | bytes 1540
  1.6 17.4 %copy-start.3 = (s32[2,16]{1,0:T(2,128)S(1)}, s32[2,16]{1,0:T(2,128)}, u32[]{:S(2)}) copy-start(s32[2,16]{1,0:T(2,128)} %band_ref.8) | copy-start | bytes 388
  2.7 33.7 %collective-permute-start.2 = (f32[6,64,512]{2,1,0:T(8,128)}, f32[6,64,512]{2,1,0:T(8,128)}, u32[]{:S(2)}, u32[]{:S(2)}) collective-permute-start(f32[6,64,512]{2,1,0:T(8,128)} %get-tuple-element.25), channel_id=1, source_target_pairs={{0,8},{8,16},{16,24},{24,32},{32,40},{40,48},{48,56},{56,64},{64,7... | collective-permute-start | bytes 2359304 | tf_op jit(solution)/shard_map/ppermute | solution.py:263
  7.0 12.0 %collective-permute-start = (f32[16,64,128]{2,1,0:T(8,128)S(1)}, f32[16,64,128]{2,1,0:T(8,128)S(1)}, u32[]{:S(2)}, u32[]{:S(2)}) collective-permute-start(f32[16,64,128]{2,1,0:T(8,128)S(1)} %get-tuple-element.22), channel_id=1, source_target_pairs={{0,1},{1,2},{2,3},{3,4},{4,5},{5,6},{6,7},{8,9},{9,10},{10,11},{11... | collective-permute-start | bytes 1572872 | tf_op jit(solution)/shard_map/ppermute | solution.py:265
  8.9 27.5 %collective-permute-start.3 = (f32[3,64,512]{2,1,0:T(8,128)}, f32[3,64,512]{2,1,0:T(8,128)S(1)}, u32[]{:S(2)}, u32[]{:S(2)}) collective-permute-start(f32[3,64,512]{2,1,0:T(8,128)} %get-tuple-element.26), channel_id=1, source_target_pairs={{0,48},{8,56},{16,0},{24,8},{32,16},{40,24},{48,32},{56,40},{64,11... | collective-permute-start | bytes 1179656 | tf_op jit(solution)/shard_map/ppermute | solution.py:264
  21.8 39.8 %collective-permute-start.1 = (f32[7,64,512]{2,1,0:T(8,128)S(1)}, f32[7,64,512]{2,1,0:T(8,128)S(1)}, u32[]{:S(2)}, u32[]{:S(2)}) collective-permute-start(f32[7,64,512]{2,1,0:T(8,128)S(1)} %sweep.4.own_ref), channel_id=1, source_target_pairs={{0,8},{8,16},{16,24},{24,32},{32,40},{40,48},{48,56},{56,64},{64,7... | collective-permute-start | bytes 2752520 | tf_op jit(solution)/shard_map/ppermute | solution.py:270
  37.4 26.1 %copy-start.4 = (f32[4,64,64]{2,1,0:T(8,128)S(1)}, f32[4,64,64]{2,1,0:T(8,128)}, u32[]{:S(2)}) copy-start(f32[4,64,64]{2,1,0:T(8,128)} %two_ref.1) | copy-start | bytes 196612
  37.4 26.1 %copy-start.5 = (f32[16,8]{0,1:T(8,128)S(1)}, f32[16,8]{0,1:T(8,128)}, u32[]{:S(2)}) copy-start(f32[16,8]{0,1:T(8,128)} %param.10) | copy-start | bytes 1540
  37.4 26.1 %copy-start.6 = (s32[64,3]{0,1:T(4,128)S(1)}, s32[64,3]{0,1:T(4,128)}, u32[]{:S(2)}) copy-start(s32[64,3]{0,1:T(4,128)} %param.12) | copy-start | bytes 2308
  37.4 26.1 %copy-start.7 = (s32[2,16]{1,0:T(2,128)S(1)}, s32[2,16]{1,0:T(2,128)}, u32[]{:S(2)}) copy-start(s32[2,16]{1,0:T(2,128)} %band_ref.9) | copy-start | bytes 388
  37.5 8.2 %collective-permute-start.4 = (f32[9,64,128]{2,1,0:T(8,128)S(1)}, f32[9,64,128]{2,1,0:T(8,128)S(1)}, u32[]{:S(2)}, u32[]{:S(2)}) collective-permute-start(f32[9,64,128]{2,1,0:T(8,128)S(1)} %pad_maximum_fusion), channel_id=1, source_target_pairs={{0,1},{1,2},{2,3},{3,4},{4,5},{5,6},{6,7},{8,9},{9,10},{10,11},{11... | collective-permute-start | bytes 884744 | tf_op jit(solution)/shard_map/ppermute | solution.py:274
  50.2 25.7 %collective-permute-start.6 = (f32[6,64,512]{2,1,0:T(8,128)S(1)}, f32[6,64,512]{2,1,0:T(8,128)S(1)}, u32[]{:S(2)}, u32[]{:S(2)}) collective-permute-start(f32[6,64,512]{2,1,0:T(8,128)S(1)} %sweep.6.one_ref), channel_id=1, source_target_pairs={{0,8},{8,16},{16,24},{24,32},{32,40},{40,48},{48,56},{56,64},{64,7... | collective-permute-start | bytes 2359304 | tf_op jit(solution)/shard_map/ppermute | solution.py:276
  53.7 33.8 %collective-permute-start.5 = (f32[3,64,512]{2,1,0:T(8,128)S(1)}, f32[3,64,512]{2,1,0:T(8,128)S(1)}, u32[]{:S(2)}, u32[]{:S(2)}) collective-permute-start(f32[3,64,512]{2,1,0:T(8,128)S(1)} %sweep.7), channel_id=1, source_target_pairs={{48,24},{56,32},{0,40},{8,48},{16,56},{24,64},{32,72},{40,80},{112... | collective-permute-start | bytes 1179656 | tf_op jit(solution)/shard_map/ppermute | solution.py:278
  61.6 32.3 %collective-permute-start.8 = (f32[7,64,512]{2,1,0:T(8,128)S(1)}, f32[7,64,512]{2,1,0:T(8,128)S(1)}, u32[]{:S(2)}, u32[]{:S(2)}) collective-permute-start(f32[7,64,512]{2,1,0:T(8,128)S(1)} %collective-permute-done.1.one_ref), channel_id=1, source_target_pairs={{0,8},{8,16},{16,24},{24,32},{32,40},{40,48},{48,56},{56,64},{64,7... | collective-permute-start | bytes 2752520 | tf_op jit(solution)/shard_map/ppermute | solution.py:280
  87.6 10.6 %collective-permute-start.7 = (f32[3,64,512]{2,1,0:T(8,128)S(1)}, f32[3,64,512]{2,1,0:T(8,128)S(1)}, u32[]{:S(2)}, u32[]{:S(2)}) collective-permute-start(f32[3,64,512]{2,1,0:T(8,128)S(1)} %collective-permute-done.5), channel_id=1, source_target_pairs={{0,504},{8,0},{16,8},{24,16},{32,24},{40,32},{48,40},{56,48},{64,5... | collective-permute-start | bytes 1179656 | tf_op jit(solution)/shard_map/ppermute | solution.py:286
  90.5 15.4 %collective-permute-start.11 = (f32[6,24,512]{2,1,0:T(8,128)S(1)}, f32[6,24,512]{2,1,0:T(8,128)S(1)}, u32[]{:S(2)}, u32[]{:S(2)}) collective-permute-start(f32[6,24,512]{2,1,0:T(8,128)S(1)} %slice.19), channel_id=1, source_target_pairs={{0,8},{8,16},{16,24},{24,32},{32,40},{40,48},{48,56},{56,64},{64,7... | collective-permute-start | bytes 884744 | tf_op jit(solution)/shard_map/ppermute | solution.py:284
  94.0 17.6 %collective-permute-start.10 = (f32[7,24,512]{2,1,0:T(8,128)S(1)}, f32[7,24,512]{2,1,0:T(8,128)S(1)}, u32[]{:S(2)}, u32[]{:S(2)}) collective-permute-start(f32[7,24,512]{2,1,0:T(8,128)S(1)} %slice.18), channel_id=1, source_target_pairs={{0,8},{8,16},{16,24},{24,32},{32,40},{40,48},{48,56},{56,64},{64,7... | collective-permute-start | bytes 1032200 | tf_op jit(solution)/shard_map/ppermute | solution.py:288
  98.2 17.0 %collective-permute-start.9 = (f32[3,64,512]{2,1,0:T(8,128)S(1)}, f32[3,64,512]{2,1,0:T(8,128)S(1)}, u32[]{:S(2)}, u32[]{:S(2)}) collective-permute-start(f32[3,64,512]{2,1,0:T(8,128)S(1)} %collective-permute-done.7.two_ref), channel_id=1, source_target_pairs={{0,504},{8,0},{16,8},{24,16},{32,24},{40,32},{48,40},{56,48},{64,5... | collective-permute-start | bytes 1179656 | tf_op jit(solution)/shard_map/ppermute | solution.py:290

commit v9 on v8

--- a/solution.py
+++ b/solution.py
@@ -76,22 +76,29 @@
     )(band, taps, field, edge)
 
 
-def carve_kernel(early, back, margin, field_ref, early_ref, back_ref, edge_ref):
+def carve_kernel(early, back, margin, me_ref, field_ref, early_ref, back_ref, edge_ref):
     early_ref[...] = field_ref[early[0] : early[1]]
     back_ref[...] = field_ref[back[0] : back[1]]
     edge_ref[...] = field_ref[:, :, margin:]
 
 
-def carve(field, early, back, margin):
+def carve(me, field, early, back, margin):
     batches, rows, width = field.shape
     shapes = ((early[1] - early[0], rows, width), (back[1] - back[0], rows, width), (batches, rows, width - margin))
+    whole = lambda i, m: (0, 0, 0)
     return pl.pallas_call(
         functools.partial(carve_kernel, early, back, margin),
+        grid_spec=pltpu.PrefetchScalarGridSpec(
+            num_scalar_prefetch=1,
+            grid=(1,),
+            in_specs=[pl.BlockSpec(field.shape, whole)],
+            out_specs=[pl.BlockSpec(shape, whole) for shape in shapes],
+        ),
         out_shape=[jax.ShapeDtypeStruct(shape, jnp.float32) for shape in shapes],
         compiler_params=pltpu.CompilerParams(vmem_limit_bytes=VMEM),
         cost_estimate=cost(1),
         name="carve",
-    )(field)
+    )(me, field)
 
 
 def operator_kernel(me_ref, pair_ref, band_ref, taps_ref, own_ref, one_ref, two_ref, out_ref, turn_ref, base_ref):
@@ -259,12 +266,11 @@
     side = functools.partial(lax.ppermute, axis_name="wid", perm=[(s, s + 1) for s in range(groups - 1)])
     wide = (wid_band, wid_taps.T)
 
-    early, back, rim = carve(density, EARLY, BACK, margin)
+    me = lax.axis_index("len")[None].astype(jnp.int32)
+    early, back, rim = carve(me, density, EARLY, BACK, margin)
     early_one_raw = hop(early)
     back_away_raw = back_first(back)
     edge = side(rim)
-    me = lax.axis_index("len")[None].astype(jnp.int32)
-    edge, me = lax.optimization_barrier((edge, me))
 
     late_own = sweep(density, edge, *wide, LATE, LATE[0], LATE[0], 1)
     late_one = hop(late_own)
@@ -272,11 +278,11 @@
     early_one_raw, back_away_raw, first_own = lax.optimization_barrier((early_one_raw, back_away_raw, first_own))
 
     first_edge = side(jnp.concatenate([early_one_raw[:, :, margin:], back_away_raw[:, :, margin:]], axis=0))
-    early_one = sweep(early_one_raw, first_edge, *wide, EARLY, 0, 0, 4000000000)
+    back_away = sweep(back_away_raw, first_edge, *wide, BACK, 0, EARLY[1], 1)
+    back_three_below = back_rest(back_away)
+    early_one = sweep(early_one_raw, after(first_edge, back_away), *wide, EARLY, 0, 0, 4000000000)
     early_two = hop(early_one)
-    back_away = sweep(back_away_raw, after(first_edge, early_one), *wide, BACK, 0, EARLY[1])
-    back_three_below = back_rest(back_away)
-    late_one = after(late_one, back_away)
+    late_one = after(late_one, early_one)
     late_two = hop(late_one)
     operator = length_operator(me, tile_pairs.T, len_band, after(len_taps.T, late_one), agg_kern)
     late_sum = prepare(operator, late_own, late_one, LATE)

time: 118 us -> 115 us (0.975)
  the two profiles are of different devices: /device:TPU:2 before, /device:TPU:4 now
where the time goes in v9:
time: 115 us
  starting transfers between devices  48.4 us (42%)
  waiting for transfers between devices  37.6 us (33%)
  Pallas kernels  26.9 us (23%)
  local copies, waits for them, and re-layouts  1.75 us (2%)
    ppermute x1, waiting for transfers between devices, shards(): late_two = hop(late_one)  13.8 us
    pallas_call x4, Pallas kernels, sweep(): pl.pallas_call(functools.partial(sweep_kernel, lo), grid_spec=pltpu.Prefe...  10.2 us
    ppermute x1, starting transfers between devices, shards(): back_away_raw = back_first(back)  10 us
    ppermute x1, waiting for transfers between devices, shards(): early_two = hop(early_one)  9.62 us
    pallas_call x3, Pallas kernels, finish(): pl.pallas_call(finish_kernel if len(held) == 2 else complete_kernel, grid...  8.63 us
    ppermute x1, waiting for transfers between devices, shards(): back_away_raw = back_first(back)  8.31 us
    ppermute x1, starting transfers between devices, shards(): early_two = hop(early_one)  7.45 us
    ppermute x1, starting transfers between devices, shards(): back_one = unhop(back_two)  6.34 us
  transfers between devices with their start and end apart: 12, of which 5 were waited for; matrix products, arithmetic and copies ran while one was open for 0% of the time, Pallas kernels for 22%

profile of v9, /device:TPU:4, one launch (start us, length us, event | category | flops | bytes accessed | tf_op | source)
XLA Modules:
  0.0 115.0 jit_solution(18269204079176480845)
XLA Ops:
  1.7 4.4 %collective-permute-start.2 = (f32[6,64,512]{2,1,0:T(8,128)S(1)}, f32[6,64,512]{2,1,0:T(8,128)S(1)}, u32[]{:S(2)}, u32[]{:S(2)}) collective-permute-start(f32[6,64,512]{2,1,0:T(8,128)S(1)} %get-tuple-element.21), channel_id=1, source_target_pairs={{0,8},{8,16},{16,24},{24,32},{32,40},{40,48},{48,56},{56,64},{64,7... | collective-permute-start | bytes 2359304 | tf_op jit(solution)/shard_map/ppermute | solution.py:271
  6.2 1.9 %collective-permute-start = (f32[16,64,128]{2,1,0:T(8,128)S(1)}, f32[16,64,128]{2,1,0:T(8,128)S(1)}, u32[]{:S(2)}, u32[]{:S(2)}) collective-permute-start(f32[16,64,128]{2,1,0:T(8,128)S(1)} %get-tuple-element.20), channel_id=1, source_target_pairs={{0,1},{1,2},{2,3},{3,4},{4,5},{5,6},{6,7},{8,9},{9,10},{10,11},{11... | collective-permute-start | bytes 1572872 | tf_op jit(solution)/shard_map/ppermute | solution.py:273
  8.1 10.0 %collective-permute-start.3 = (f32[3,64,512]{2,1,0:T(8,128)S(1)}, f32[3,64,512]{2,1,0:T(8,128)S(1)}, u32[]{:S(2)}, u32[]{:S(2)}) collective-permute-start(f32[3,64,512]{2,1,0:T(8,128)S(1)} %get-tuple-element.22), channel_id=1, source_target_pairs={{0,48},{8,56},{16,0},{24,8},{32,16},{40,24},{48,32},{56,40},{64,11... | collective-permute-start | bytes 1179656 | tf_op jit(solution)/shard_map/ppermute | solution.py:272
  18.2 2.8 %sweep.4.own_ref = f32[7,64,512]{2,1,0:T(8,128)S(1)} custom-call(s32[2,16]{1,0:T(2,128)S(1)} %copy-done.3, f32[8,16]{1,0:T(8,128)S(1)} %bitcast.4, f32[16,64,512]{2,1,0:T(8,128)S(1)} %copy-done.1, f32[16,64,128]{2,1,0:T(8,128)S(1)} %collective-permute-done.edge_ref), custom_call_target="tpu_custom_call" | custom-call | flops 1 | bytes 1 | tf_op jit(solution)/shard_map/sweep/pallas_call | solution.py:61
  21.0 2.8 %collective-permute-start.1 = (f32[7,64,512]{2,1,0:T(8,128)S(1)}, f32[7,64,512]{2,1,0:T(8,128)S(1)}, u32[]{:S(2)}, u32[]{:S(2)}) collective-permute-start(f32[7,64,512]{2,1,0:T(8,128)S(1)} %sweep.4.own_ref), channel_id=1, source_target_pairs={{0,8},{8,16},{16,24},{24,32},{32,40},{40,48},{48,56},{56,64},{64,7... | collective-permute-start | bytes 2752520 | tf_op jit(solution)/shard_map/ppermute | solution.py:276
  23.8 3.4 %sweep.5.own_ref = f32[9,64,512]{2,1,0:T(8,128)S(1)} custom-call(s32[2,16]{1,0:T(2,128)S(1)} %copy-done.3, f32[8,16]{1,0:T(8,128)S(1)} %bitcast.5, f32[16,64,512]{2,1,0:T(8,128)S(1)} %copy-done.1, f32[16,64,128]{2,1,0:T(8,128)S(1)} %collective-permute-done.edge_ref), custom_call_target="tpu_custom_call" | custom-call | flops 1 | bytes 1 | tf_op jit(solution)/shard_map/sweep/pallas_call | solution.py:61
  27.2 8.3 %collective-permute-done.3.field_ref = f32[3,64,512]{2,1,0:T(8,128)S(1)} collective-permute-done((f32[3,64,512]{2,1,0:T(8,128)S(1)}, f32[3,64,512]{2,1,0:T(8,128)S(1)}, u32[]{:S(2)}, u32[]{:S(2)}) %collective-permute-start.3) | collective-permute-done | bytes 393248 | tf_op jit(solution)/shard_map/ppermute | solution.py:272
  35.6 2.4 %collective-permute-start.4 = (f32[9,64,128]{2,1,0:T(8,128)S(1)}, f32[9,64,128]{2,1,0:T(8,128)S(1)}, u32[]{:S(2)}, u32[]{:S(2)}) collective-permute-start(f32[9,64,128]{2,1,0:T(8,128)S(1)} %pad_maximum_fusion), channel_id=1, source_target_pairs={{0,1},{1,2},{2,3},{3,4},{4,5},{5,6},{6,7},{8,9},{9,10},{10,11},{11... | collective-permute-start | bytes 884744 | tf_op jit(solution)/shard_map/ppermute | solution.py:280
  37.9 5.7 %collective-permute-done.4.edge_ref = f32[9,64,128]{2,1,0:T(8,128)S(1)} collective-permute-done((f32[9,64,128]{2,1,0:T(8,128)S(1)}, f32[9,64,128]{2,1,0:T(8,128)S(1)}, u32[]{:S(2)}, u32[]{:S(2)}) %collective-permute-start.4) | collective-permute-done | bytes 294944 | tf_op jit(solution)/shard_map/ppermute | solution.py:280
  45.2 2.6 %collective-permute-start.5 = (f32[3,64,512]{2,1,0:T(8,128)S(1)}, f32[3,64,512]{2,1,0:T(8,128)S(1)}, u32[]{:S(2)}, u32[]{:S(2)}) collective-permute-start(f32[3,64,512]{2,1,0:T(8,128)S(1)} %sweep.6), channel_id=1, source_target_pairs={{48,24},{56,32},{0,40},{8,48},{16,56},{24,64},{32,72},{40,80},{112... | collective-permute-start | bytes 1179656 | tf_op jit(solution)/shard_map/ppermute | solution.py:282
  47.8 2.5 %sweep.7.one_ref = f32[6,64,512]{2,1,0:T(8,128)S(1)} custom-call(s32[2,16]{1,0:T(2,128)S(1)} %copy-done.3, f32[8,16]{1,0:T(8,128)S(1)} %bitcast.7, f32[6,64,512]{2,1,0:T(8,128)S(1)} %collective-permute-done.2.field_ref, f32[9,64,128]{2,1,0:T(8,128)S(1)} %collective-permute-done.4.edge_ref), custom_call_target="tpu_custom_call" | custom-call | flops 4000000000 | bytes 1 | tf_op jit(solution)/shard_map/sweep/pallas_call | solution.py:61
  50.3 7.5 %collective-permute-start.6 = (f32[6,64,512]{2,1,0:T(8,128)S(1)}, f32[6,64,512]{2,1,0:T(8,128)S(1)}, u32[]{:S(2)}, u32[]{:S(2)}) collective-permute-start(f32[6,64,512]{2,1,0:T(8,128)S(1)} %sweep.7.one_ref), channel_id=1, source_target_pairs={{0,8},{8,16},{16,24},{24,32},{32,40},{40,48},{48,56},{56,64},{64,7... | collective-permute-start | bytes 2359304 | tf_op jit(solution)/shard_map/ppermute | solution.py:284
  57.7 1.9 %collective-permute-start.8 = (f32[7,64,512]{2,1,0:T(8,128)S(1)}, f32[7,64,512]{2,1,0:T(8,128)S(1)}, u32[]{:S(2)}, u32[]{:S(2)}) collective-permute-start(f32[7,64,512]{2,1,0:T(8,128)S(1)} %collective-permute-done.1.one_ref), channel_id=1, source_target_pairs={{0,8},{8,16},{16,24},{24,32},{32,40},{40,48},{48,56},{56,64},{64,7... | collective-permute-start | bytes 2752520 | tf_op jit(solution)/shard_map/ppermute | solution.py:286
  59.7 6.1 %operator.1.op_ref = bf16[16,256,216]{2,1,0:T(8,128)(2,1)S(1)} custom-call(s32[1]{0:T(128)} %bitcast.me_ref, s32[3,64]{1,0:T(4,128)S(1)} %bitcast.9, s32[2,16]{1,0:T(2,128)S(1)} %copy-done.7, f32[8,16]{1,0:T(8,128)S(1)} %bitcast.8, f32[4,64,64]{2,1,0:T(8,128)S(1)} %copy-done.4, f32[4,64,64]{2,1,0:T(8,128)S(1)} %copy-done.4, f32[4,64,64]{2,1,0:T(8,128)S(1)} %copy-done.4), custom_call_target="tpu_custom_call" | custom-call | flops 10000000000 | bytes 1 | tf_op jit(solution)/shard_map/operator/pallas_call | solution.py:138
  65.8 1.8 %prepare.1.sum_ref = f32[7,128,512]{2,1,0:T(8,128)S(1)} custom-call(bf16[16,256,216]{2,1,0:T(8,128)(2,1)S(1)} %operator.1.op_ref, f32[7,64,512]{2,1,0:T(8,128)S(1)} %sweep.4.own_ref, f32[7,64,512]{2,1,0:T(8,128)S(1)} %collective-permute-done.1.one_ref), custom_call_target="tpu_custom_call" | custom-call | flops 1 | bytes 1 | tf_op jit(solution)/shard_map/prepare/pallas_call | solution.py:179
  67.6 9.6 %collective-permute-done.6.two_ref = f32[6,64,512]{2,1,0:T(8,128)S(1)} collective-permute-done((f32[6,64,512]{2,1,0:T(8,128)S(1)}, f32[6,64,512]{2,1,0:T(8,128)S(1)}, u32[]{:S(2)}, u32[]{:S(2)}) %collective-permute-start.6) | collective-permute-done | bytes 786464 | tf_op jit(solution)/shard_map/ppermute | solution.py:284
  77.3 3.9 %collective-permute-start.7 = (f32[3,64,512]{2,1,0:T(8,128)S(1)}, f32[3,64,512]{2,1,0:T(8,128)S(1)}, u32[]{:S(2)}, u32[]{:S(2)}) collective-permute-start(f32[3,64,512]{2,1,0:T(8,128)S(1)} %collective-permute-done.5), channel_id=1, source_target_pairs={{0,504},{8,0},{16,8},{24,16},{32,24},{40,32},{48,40},{56,48},{64,5... | collective-permute-start | bytes 1179656 | tf_op jit(solution)/shard_map/ppermute | solution.py:292
  81.2 1.9 %collective-permute-start.11 = (f32[6,24,512]{2,1,0:T(8,128)S(1)}, f32[6,24,512]{2,1,0:T(8,128)S(1)}, u32[]{:S(2)}, u32[]{:S(2)}) collective-permute-start(f32[6,24,512]{2,1,0:T(8,128)S(1)} %slice.19), channel_id=1, source_target_pairs={{0,8},{8,16},{16,24},{24,32},{32,40},{40,48},{48,56},{56,64},{64,7... | collective-permute-start | bytes 884744 | tf_op jit(solution)/shard_map/ppermute | solution.py:290
  83.1 13.8 %collective-permute-done.8.two_ref = f32[7,64,512]{2,1,0:T(8,128)S(1)} collective-permute-done((f32[7,64,512]{2,1,0:T(8,128)S(1)}, f32[7,64,512]{2,1,0:T(8,128)S(1)}, u32[]{:S(2)}, u32[]{:S(2)}) %collective-permute-start.8) | collective-permute-done | bytes 917536 | tf_op jit(solution)/shard_map/ppermute | solution.py:286
  97.0 2.8 %collective-permute-start.10 = (f32[7,24,512]{2,1,0:T(8,128)S(1)}, f32[7,24,512]{2,1,0:T(8,128)S(1)}, u32[]{:S(2)}, u32[]{:S(2)}) collective-permute-start(f32[7,24,512]{2,1,0:T(8,128)S(1)} %slice.18), channel_id=1, source_target_pairs={{0,8},{8,16},{16,24},{24,32},{32,40},{40,48},{48,56},{56,64},{64,7... | collective-permute-start | bytes 1032200 | tf_op jit(solution)/shard_map/ppermute | solution.py:294
  99.8 6.3 %collective-permute-start.9 = (f32[3,64,512]{2,1,0:T(8,128)S(1)}, f32[3,64,512]{2,1,0:T(8,128)S(1)}, u32[]{:S(2)}, u32[]{:S(2)}) collective-permute-start(f32[3,64,512]{2,1,0:T(8,128)S(1)} %collective-permute-done.7.two_ref), channel_id=1, source_target_pairs={{0,504},{8,0},{16,8},{24,16},{32,24},{40,32},{48,40},{56,48},{64,5... | collective-permute-start | bytes 1179656 | tf_op jit(solution)/shard_map/ppermute | solution.py:296
  106.2 3.1 %finish.3.rest_0_ = f32[16,64,512]{2,1,0:T(8,128)} custom-call(bf16[16,256,216]{2,1,0:T(8,128)(2,1)S(1)} %operator.1.op_ref, f32[9,64,512]{2,1,0:T(8,128)S(1)} %sweep.5.own_ref, f32[6,64,512]{2,1,0:T(8,128)S(1)} %sweep.7.one_ref, f32[6,64,512]{2,1,0:T(8,128)S(1)} %collective-permute-done.6.two_ref, f32[6,24,512]{2,1,0:T(8,128)S(1)} %collective-permute-done.11.rim_ref), custom_call_target="tpu_custom_call" | custom-call | flops 1000000000 | bytes 1 | tf_op jit(solution)/shard_map/finish/pallas_call | solution.py:226
  109.4 3.7 %finish.4.rest_0_ = f32[16,64,512]{2,1,0:T(8,128)} custom-call(bf16[16,256,216]{2,1,0:T(8,128)(2,1)S(1)} %operator.1.op_ref, f32[7,128,512]{2,1,0:T(8,128)S(1)} %prepare.1.sum_ref, f32[7,64,512]{2,1,0:T(8,128)S(1)} %collective-permute-done.8.two_ref, f32[7,24,512]{2,1,0:T(8,128)S(1)} %collective-permute-done.10.rim_ref, ...), custom_call_target="tpu_custom_call", output_to_operand_aliasing={{}: (4, {})} | custom-call | flops 1000000000 | bytes 1 | tf_op jit(solution)/shard_map/finish/pallas_call | solution.py:226
  113.1 1.9 %finish.5 = f32[16,64,512]{2,1,0:T(8,128)} custom-call(bf16[16,256,216]{2,1,0:T(8,128)(2,1)S(1)} %operator.1.op_ref, f32[9,64,512]{2,1,0:T(8,128)S(1)} %sweep.5.own_ref, f32[3,64,512]{2,1,0:T(8,128)S(1)} %collective-permute-done.9.one_ref, f32[3,64,512]{2,1,0:T(8,128)S(1)} %collective-permute-done.7.two_ref, ...), custom_call_target="tpu_custom_call", output_to_operand_aliasing={{}: (5, {})} | custom-call | flops 1 | bytes 1 | tf_op jit(solution)/shard_map/finish/pallas_call | solution.py:226
  (32 shorter events, 3.6 us)
Async XLA Ops:
  0.0 18.1 %copy-start.3 = (s32[2,16]{1,0:T(2,128)S(1)}, s32[2,16]{1,0:T(2,128)}, u32[]{:S(2)}) copy-start(s32[2,16]{1,0:T(2,128)} %band_ref.8) | copy-start | bytes 388
  0.0 18.2 %copy-start.2 = (f32[16,8]{0,1:T(8,128)S(1)}, f32[16,8]{0,1:T(8,128)}, u32[]{:S(2)}) copy-start(f32[16,8]{0,1:T(8,128)} %param.11) | copy-start | bytes 1540
  0.0 1.6 %copy-start = (f32[16,64,512]{2,1,0:T(8,128)S(1)}, f32[16,64,512]{2,1,0:T(8,128)}, u32[]{:S(2)}) copy-start(f32[16,64,512]{2,1,0:T(8,128)} %field_ref.5) | copy-start | bytes 6291460
  1.6 16.5 %copy-start.1 = (f32[16,64,512]{2,1,0:T(8,128)S(1)}, f32[16,64,512]{2,1,0:T(8,128)}, u32[]{:S(2)}) copy-start(f32[16,64,512]{2,1,0:T(8,128)} %field_ref.5) | copy-start | bytes 6291460
  1.7 33.7 %collective-permute-start.2 = (f32[6,64,512]{2,1,0:T(8,128)S(1)}, f32[6,64,512]{2,1,0:T(8,128)S(1)}, u32[]{:S(2)}, u32[]{:S(2)}) collective-permute-start(f32[6,64,512]{2,1,0:T(8,128)S(1)} %get-tuple-element.21), channel_id=1, source_target_pairs={{0,8},{8,16},{16,24},{24,32},{32,40},{40,48},{48,56},{56,64},{64,7... | collective-permute-start | bytes 2359304 | tf_op jit(solution)/shard_map/ppermute | solution.py:271
  6.2 12.0 %collective-permute-start = (f32[16,64,128]{2,1,0:T(8,128)S(1)}, f32[16,64,128]{2,1,0:T(8,128)S(1)}, u32[]{:S(2)}, u32[]{:S(2)}) collective-permute-start(f32[16,64,128]{2,1,0:T(8,128)S(1)} %get-tuple-element.20), channel_id=1, source_target_pairs={{0,1},{1,2},{2,3},{3,4},{4,5},{5,6},{6,7},{8,9},{9,10},{10,11},{11... | collective-permute-start | bytes 1572872 | tf_op jit(solution)/shard_map/ppermute | solution.py:273
  8.1 27.4 %collective-permute-start.3 = (f32[3,64,512]{2,1,0:T(8,128)S(1)}, f32[3,64,512]{2,1,0:T(8,128)S(1)}, u32[]{:S(2)}, u32[]{:S(2)}) collective-permute-start(f32[3,64,512]{2,1,0:T(8,128)S(1)} %get-tuple-element.22), channel_id=1, source_target_pairs={{0,48},{8,56},{16,0},{24,8},{32,16},{40,24},{48,32},{56,40},{64,11... | collective-permute-start | bytes 1179656 | tf_op jit(solution)/shard_map/ppermute | solution.py:272
  21.0 36.8 %collective-permute-start.1 = (f32[7,64,512]{2,1,0:T(8,128)S(1)}, f32[7,64,512]{2,1,0:T(8,128)S(1)}, u32[]{:S(2)}, u32[]{:S(2)}) collective-permute-start(f32[7,64,512]{2,1,0:T(8,128)S(1)} %sweep.4.own_ref), channel_id=1, source_target_pairs={{0,8},{8,16},{16,24},{24,32},{32,40},{40,48},{48,56},{56,64},{64,7... | collective-permute-start | bytes 2752520 | tf_op jit(solution)/shard_map/ppermute | solution.py:276
  35.6 8.0 %collective-permute-start.4 = (f32[9,64,128]{2,1,0:T(8,128)S(1)}, f32[9,64,128]{2,1,0:T(8,128)S(1)}, u32[]{:S(2)}, u32[]{:S(2)}) collective-permute-start(f32[9,64,128]{2,1,0:T(8,128)S(1)} %pad_maximum_fusion), channel_id=1, source_target_pairs={{0,1},{1,2},{2,3},{3,4},{4,5},{5,6},{6,7},{8,9},{9,10},{10,11},{11... | collective-permute-start | bytes 884744 | tf_op jit(solution)/shard_map/ppermute | solution.py:280
  45.2 14.5 %copy-start.4 = (f32[4,64,64]{2,1,0:T(8,128)S(1)}, f32[4,64,64]{2,1,0:T(8,128)}, u32[]{:S(2)}) copy-start(f32[4,64,64]{2,1,0:T(8,128)} %two_ref.1) | copy-start | bytes 196612
  45.2 14.5 %copy-start.5 = (f32[16,8]{0,1:T(8,128)S(1)}, f32[16,8]{0,1:T(8,128)}, u32[]{:S(2)}) copy-start(f32[16,8]{0,1:T(8,128)} %param.10) | copy-start | bytes 1540
  45.2 14.5 %copy-start.6 = (s32[64,3]{0,1:T(4,128)S(1)}, s32[64,3]{0,1:T(4,128)}, u32[]{:S(2)}) copy-start(s32[64,3]{0,1:T(4,128)} %param.12) | copy-start | bytes 2308
  45.2 14.5 %copy-start.7 = (s32[2,16]{1,0:T(2,128)S(1)}, s32[2,16]{1,0:T(2,128)}, u32[]{:S(2)}) copy-start(s32[2,16]{1,0:T(2,128)} %band_ref.9) | copy-start | bytes 388
  45.2 32.1 %collective-permute-start.5 = (f32[3,64,512]{2,1,0:T(8,128)S(1)}, f32[3,64,512]{2,1,0:T(8,128)S(1)}, u32[]{:S(2)}, u32[]{:S(2)}) collective-permute-start(f32[3,64,512]{2,1,0:T(8,128)S(1)} %sweep.6), channel_id=1, source_target_pairs={{48,24},{56,32},{0,40},{8,48},{16,56},{24,64},{32,72},{40,80},{112... | collective-permute-start | bytes 1179656 | tf_op jit(solution)/shard_map/ppermute | solution.py:282
  50.3 27.0 %collective-permute-start.6 = (f32[6,64,512]{2,1,0:T(8,128)S(1)}, f32[6,64,512]{2,1,0:T(8,128)S(1)}, u32[]{:S(2)}, u32[]{:S(2)}) collective-permute-start(f32[6,64,512]{2,1,0:T(8,128)S(1)} %sweep.7.one_ref), channel_id=1, source_target_pairs={{0,8},{8,16},{16,24},{24,32},{32,40},{40,48},{48,56},{56,64},{64,7... | collective-permute-start | bytes 2359304 | tf_op jit(solution)/shard_map/ppermute | solution.py:284
  57.7 39.2 %collective-permute-start.8 = (f32[7,64,512]{2,1,0:T(8,128)S(1)}, f32[7,64,512]{2,1,0:T(8,128)S(1)}, u32[]{:S(2)}, u32[]{:S(2)}) collective-permute-start(f32[7,64,512]{2,1,0:T(8,128)S(1)} %collective-permute-done.1.one_ref), channel_id=1, source_target_pairs={{0,8},{8,16},{16,24},{24,32},{32,40},{40,48},{48,56},{56,64},{64,7... | collective-permute-start | bytes 2752520 | tf_op jit(solution)/shard_map/ppermute | solution.py:286
  77.3 22.5 %collective-permute-start.7 = (f32[3,64,512]{2,1,0:T(8,128)S(1)}, f32[3,64,512]{2,1,0:T(8,128)S(1)}, u32[]{:S(2)}, u32[]{:S(2)}) collective-permute-start(f32[3,64,512]{2,1,0:T(8,128)S(1)} %collective-permute-done.5), channel_id=1, source_target_pairs={{0,504},{8,0},{16,8},{24,16},{32,24},{40,32},{48,40},{56,48},{64,5... | collective-permute-start | bytes 1179656 | tf_op jit(solution)/shard_map/ppermute | solution.py:292
  81.2 25.0 %collective-permute-start.11 = (f32[6,24,512]{2,1,0:T(8,128)S(1)}, f32[6,24,512]{2,1,0:T(8,128)S(1)}, u32[]{:S(2)}, u32[]{:S(2)}) collective-permute-start(f32[6,24,512]{2,1,0:T(8,128)S(1)} %slice.19), channel_id=1, source_target_pairs={{0,8},{8,16},{16,24},{24,32},{32,40},{40,48},{48,56},{56,64},{64,7... | collective-permute-start | bytes 884744 | tf_op jit(solution)/shard_map/ppermute | solution.py:290
  97.0 12.5 %collective-permute-start.10 = (f32[7,24,512]{2,1,0:T(8,128)S(1)}, f32[7,24,512]{2,1,0:T(8,128)S(1)}, u32[]{:S(2)}, u32[]{:S(2)}) collective-permute-start(f32[7,24,512]{2,1,0:T(8,128)S(1)} %slice.18), channel_id=1, source_target_pairs={{0,8},{8,16},{16,24},{24,32},{32,40},{40,48},{48,56},{56,64},{64,7... | collective-permute-start | bytes 1032200 | tf_op jit(solution)/shard_map/ppermute | solution.py:294
  99.8 13.3 %collective-permute-start.9 = (f32[3,64,512]{2,1,0:T(8,128)S(1)}, f32[3,64,512]{2,1,0:T(8,128)S(1)}, u32[]{:S(2)}, u32[]{:S(2)}) collective-permute-start(f32[3,64,512]{2,1,0:T(8,128)S(1)} %collective-permute-done.7.two_ref), channel_id=1, source_target_pairs={{0,504},{8,0},{16,8},{24,16},{32,24},{40,32},{48,40},{56,48},{64,5... | collective-permute-start | bytes 1179656 | tf_op jit(solution)/shard_map/ppermute | solution.py:296

commit v10 on v9

--- a/solution.py
+++ b/solution.py
@@ -290,16 +290,15 @@
     early_rim = hop(early_two[:, tile_len - RIM :])
     back_three_below = after(back_three_below, early_two)
     back_two = unhop(back_three_below)
-    late_two = after(late_two, back_three_below)
+    back_one = unhop(back_two)
+    late_two = after(late_two, back_two)
     late_rim = hop(late_two[:, tile_len - RIM :])
-    back_two = after(back_two, late_two)
-    back_one = unhop(back_two)
-
-    early_rim = after(early_rim, back_two)
-    out = finish(operator, (first_own, early_one), early_two, early_rim, EARLY, batches, None, 0, 1000000000)
-    out = finish(operator, (late_sum,), late_two, late_rim, LATE, batches, out, 0, 1000000000)
+
+    early_rim = after(early_rim, late_two)
+    out = finish(operator, (first_own, early_one), early_two, early_rim, EARLY, batches, None, 0, 2000000000)
     back_rim = back_three_below[:, tile_len - RIM :]
-    return finish(operator, (first_own, back_one), back_two, back_rim, BACK, batches, out, EARLY[1], 1)
+    out = finish(operator, (first_own, back_one), back_two, back_rim, BACK, batches, out, EARLY[1], 1)
+    return finish(operator, (late_sum,), late_two, late_rim, LATE, batches, out, 0, 1)
 
 
 def solution(mesh):

time: 115 us -> 114 us (level)
  the two profiles are of different devices: /device:TPU:4 before, /device:TPU:2 now
where the time goes in v10:
time: 114 us; the launch traced here: 113 us
  starting transfers between devices  51.6 us (45%)
  waiting for transfers between devices  32.3 us (28%)
  Pallas kernels  26.9 us (24%)
  local copies, waits for them, and re-layouts  1.75 us (2%)
    pallas_call x4, Pallas kernels, sweep(): pl.pallas_call(functools.partial(sweep_kernel, lo), grid_spec=pltpu.Prefe...  10.2 us
    ppermute x1, starting transfers between devices, shards(): back_away_raw = back_first(back)  10 us
    ppermute x1, waiting for transfers between devices, shards(): early_two = hop(early_one)  9.62 us
    pallas_call x3, Pallas kernels, finish(): pl.pallas_call(finish_kernel if len(held) == 2 else complete_kernel, grid...  8.6 us
    ppermute x1, waiting for transfers between devices, shards(): back_away_raw = back_first(back)  8.07 us
    ppermute x1, starting transfers between devices, shards(): back_one = unhop(back_two)  7.7 us
    ppermute x1, starting transfers between devices, shards(): early_two = hop(early_one)  7.45 us
    pallas_call x1, Pallas kernels, length_operator(): pl.pallas_call(operator_kernel, grid_spec=pltpu.PrefetchScalarGridSpec(nu...  6.12 us
  transfers between devices with their start and end apart: 12, of which 7 were waited for; matrix products, arithmetic and copies ran while one was open for 0% of the time, Pallas kernels for 20%

profile of v10, /device:TPU:2, one launch (start us, length us, event | category | flops | bytes accessed | tf_op | source)
XLA Modules:
  0.0 112.9 jit_solution(13479566719038976066)
XLA Ops:
  1.7 4.4 %collective-permute-start.2 = (f32[6,64,512]{2,1,0:T(8,128)S(1)}, f32[6,64,512]{2,1,0:T(8,128)S(1)}, u32[]{:S(2)}, u32[]{:S(2)}) collective-permute-start(f32[6,64,512]{2,1,0:T(8,128)S(1)} %get-tuple-element.20), channel_id=1, source_target_pairs={{0,8},{8,16},{16,24},{24,32},{32,40},{40,48},{48,56},{56,64},{64,7... | collective-permute-start | bytes 2359304 | tf_op jit(solution)/shard_map/ppermute | solution.py:271
  6.2 1.9 %collective-permute-start = (f32[16,64,128]{2,1,0:T(8,128)S(1)}, f32[16,64,128]{2,1,0:T(8,128)S(1)}, u32[]{:S(2)}, u32[]{:S(2)}) collective-permute-start(f32[16,64,128]{2,1,0:T(8,128)S(1)} %get-tuple-element.19), channel_id=1, source_target_pairs={{0,1},{1,2},{2,3},{3,4},{4,5},{5,6},{6,7},{8,9},{9,10},{10,11},{11... | collective-permute-start | bytes 1572872 | tf_op jit(solution)/shard_map/ppermute | solution.py:273
  8.1 10.0 %collective-permute-start.3 = (f32[3,64,512]{2,1,0:T(8,128)S(1)}, f32[3,64,512]{2,1,0:T(8,128)S(1)}, u32[]{:S(2)}, u32[]{:S(2)}) collective-permute-start(f32[3,64,512]{2,1,0:T(8,128)S(1)} %get-tuple-element.21), channel_id=1, source_target_pairs={{0,48},{8,56},{16,0},{24,8},{32,16},{40,24},{48,32},{56,40},{64,11... | collective-permute-start | bytes 1179656 | tf_op jit(solution)/shard_map/ppermute | solution.py:272
  18.2 2.8 %sweep.4.own_ref = f32[7,64,512]{2,1,0:T(8,128)S(1)} custom-call(s32[2,16]{1,0:T(2,128)S(1)} %copy-done.3, f32[8,16]{1,0:T(8,128)S(1)} %bitcast.4, f32[16,64,512]{2,1,0:T(8,128)S(1)} %copy-done.1, f32[16,64,128]{2,1,0:T(8,128)S(1)} %collective-permute-done.edge_ref), custom_call_target="tpu_custom_call" | custom-call | flops 1 | bytes 1 | tf_op jit(solution)/shard_map/sweep/pallas_call | solution.py:61
  21.0 2.8 %collective-permute-start.1 = (f32[7,64,512]{2,1,0:T(8,128)S(1)}, f32[7,64,512]{2,1,0:T(8,128)S(1)}, u32[]{:S(2)}, u32[]{:S(2)}) collective-permute-start(f32[7,64,512]{2,1,0:T(8,128)S(1)} %sweep.4.own_ref), channel_id=1, source_target_pairs={{0,8},{8,16},{16,24},{24,32},{32,40},{40,48},{48,56},{56,64},{64,7... | collective-permute-start | bytes 2752520 | tf_op jit(solution)/shard_map/ppermute | solution.py:276
  23.8 3.4 %sweep.5.own_ref = f32[9,64,512]{2,1,0:T(8,128)S(1)} custom-call(s32[2,16]{1,0:T(2,128)S(1)} %copy-done.3, f32[8,16]{1,0:T(8,128)S(1)} %bitcast.5, f32[16,64,512]{2,1,0:T(8,128)S(1)} %copy-done.1, f32[16,64,128]{2,1,0:T(8,128)S(1)} %collective-permute-done.edge_ref), custom_call_target="tpu_custom_call" | custom-call | flops 1 | bytes 1 | tf_op jit(solution)/shard_map/sweep/pallas_call | solution.py:61
  27.2 8.1 %collective-permute-done.3.field_ref = f32[3,64,512]{2,1,0:T(8,128)S(1)} collective-permute-done((f32[3,64,512]{2,1,0:T(8,128)S(1)}, f32[3,64,512]{2,1,0:T(8,128)S(1)}, u32[]{:S(2)}, u32[]{:S(2)}) %collective-permute-start.3) | collective-permute-done | bytes 393248 | tf_op jit(solution)/shard_map/ppermute | solution.py:272
  35.3 2.6 %collective-permute-start.4 = (f32[9,64,128]{2,1,0:T(8,128)S(1)}, f32[9,64,128]{2,1,0:T(8,128)S(1)}, u32[]{:S(2)}, u32[]{:S(2)}) collective-permute-start(f32[9,64,128]{2,1,0:T(8,128)S(1)} %pad_maximum_fusion), channel_id=1, source_target_pairs={{0,1},{1,2},{2,3},{3,4},{4,5},{5,6},{6,7},{8,9},{9,10},{10,11},{11... | collective-permute-start | bytes 884744 | tf_op jit(solution)/shard_map/ppermute | solution.py:280
  37.9 5.4 %collective-permute-done.4.edge_ref = f32[9,64,128]{2,1,0:T(8,128)S(1)} collective-permute-done((f32[9,64,128]{2,1,0:T(8,128)S(1)}, f32[9,64,128]{2,1,0:T(8,128)S(1)}, u32[]{:S(2)}, u32[]{:S(2)}) %collective-permute-start.4) | collective-permute-done | bytes 294944 | tf_op jit(solution)/shard_map/ppermute | solution.py:280
  45.0 2.6 %collective-permute-start.6 = (f32[3,64,512]{2,1,0:T(8,128)S(1)}, f32[3,64,512]{2,1,0:T(8,128)S(1)}, u32[]{:S(2)}, u32[]{:S(2)}) collective-permute-start(f32[3,64,512]{2,1,0:T(8,128)S(1)} %sweep.6), channel_id=1, source_target_pairs={{48,24},{56,32},{0,40},{8,48},{16,56},{24,64},{32,72},{40,80},{112... | collective-permute-start | bytes 1179656 | tf_op jit(solution)/shard_map/ppermute | solution.py:282
  47.5 2.5 %sweep.7.one_ref = f32[6,64,512]{2,1,0:T(8,128)S(1)} custom-call(s32[2,16]{1,0:T(2,128)S(1)} %copy-done.3, f32[8,16]{1,0:T(8,128)S(1)} %bitcast.7, f32[6,64,512]{2,1,0:T(8,128)S(1)} %collective-permute-done.2.field_ref, f32[9,64,128]{2,1,0:T(8,128)S(1)} %collective-permute-done.4.edge_ref), custom_call_target="tpu_custom_call" | custom-call | flops 4000000000 | bytes 1 | tf_op jit(solution)/shard_map/sweep/pallas_call | solution.py:61
  50.0 7.4 %collective-permute-start.7 = (f32[6,64,512]{2,1,0:T(8,128)S(1)}, f32[6,64,512]{2,1,0:T(8,128)S(1)}, u32[]{:S(2)}, u32[]{:S(2)}) collective-permute-start(f32[6,64,512]{2,1,0:T(8,128)S(1)} %sweep.7.one_ref), channel_id=1, source_target_pairs={{0,8},{8,16},{16,24},{24,32},{32,40},{40,48},{48,56},{56,64},{64,7... | collective-permute-start | bytes 2359304 | tf_op jit(solution)/shard_map/ppermute | solution.py:284
  57.5 1.9 %collective-permute-start.5 = (f32[7,64,512]{2,1,0:T(8,128)S(1)}, f32[7,64,512]{2,1,0:T(8,128)S(1)}, u32[]{:S(2)}, u32[]{:S(2)}) collective-permute-start(f32[7,64,512]{2,1,0:T(8,128)S(1)} %collective-permute-done.1.one_ref), channel_id=1, source_target_pairs={{0,8},{8,16},{16,24},{24,32},{32,40},{40,48},{48,56},{56,64},{64,7... | collective-permute-start | bytes 2752520 | tf_op jit(solution)/shard_map/ppermute | solution.py:286
  59.5 6.1 %operator.1.op_ref = bf16[16,256,216]{2,1,0:T(8,128)(2,1)S(1)} custom-call(s32[1]{0:T(128)} %bitcast.me_ref, s32[3,64]{1,0:T(4,128)S(1)} %bitcast.9, s32[2,16]{1,0:T(2,128)S(1)} %copy-done.7, f32[8,16]{1,0:T(8,128)S(1)} %bitcast.8, f32[4,64,64]{2,1,0:T(8,128)S(1)} %copy-done.4, f32[4,64,64]{2,1,0:T(8,128)S(1)} %copy-done.4, f32[4,64,64]{2,1,0:T(8,128)S(1)} %copy-done.4), custom_call_target="tpu_custom_call" | custom-call | flops 10000000000 | bytes 1 | tf_op jit(solution)/shard_map/operator/pallas_call | solution.py:138
  67.4 9.6 %collective-permute-done.7.two_ref = f32[6,64,512]{2,1,0:T(8,128)S(1)} collective-permute-done((f32[6,64,512]{2,1,0:T(8,128)S(1)}, f32[6,64,512]{2,1,0:T(8,128)S(1)}, u32[]{:S(2)}, u32[]{:S(2)}) %collective-permute-start.7) | collective-permute-done | bytes 786464 | tf_op jit(solution)/shard_map/ppermute | solution.py:284
  77.0 5.5 %collective-permute-start.8 = (f32[3,64,512]{2,1,0:T(8,128)S(1)}, f32[3,64,512]{2,1,0:T(8,128)S(1)}, u32[]{:S(2)}, u32[]{:S(2)}) collective-permute-start(f32[3,64,512]{2,1,0:T(8,128)S(1)} %collective-permute-done.6), channel_id=1, source_target_pairs={{0,504},{8,0},{16,8},{24,16},{32,24},{40,32},{48,40},{56,48},{64,5... | collective-permute-start | bytes 1179656 | tf_op jit(solution)/shard_map/ppermute | solution.py:292
  82.5 1.9 %collective-permute-start.11 = (f32[6,24,512]{2,1,0:T(8,128)S(1)}, f32[6,24,512]{2,1,0:T(8,128)S(1)}, u32[]{:S(2)}, u32[]{:S(2)}) collective-permute-start(f32[6,24,512]{2,1,0:T(8,128)S(1)} %slice.19), channel_id=1, source_target_pairs={{0,8},{8,16},{16,24},{24,32},{32,40},{40,48},{48,56},{56,64},{64,7... | collective-permute-start | bytes 884744 | tf_op jit(solution)/shard_map/ppermute | solution.py:290
  84.5 3.3 %collective-permute-done.8.two_ref = f32[3,64,512]{2,1,0:T(8,128)S(1)} collective-permute-done((f32[3,64,512]{2,1,0:T(8,128)S(1)}, f32[3,64,512]{2,1,0:T(8,128)S(1)}, u32[]{:S(2)}, u32[]{:S(2)}) %collective-permute-start.8) | collective-permute-done | bytes 393248 | tf_op jit(solution)/shard_map/ppermute | solution.py:292
  87.8 7.7 %collective-permute-start.10 = (f32[3,64,512]{2,1,0:T(8,128)S(1)}, f32[3,64,512]{2,1,0:T(8,128)S(1)}, u32[]{:S(2)}, u32[]{:S(2)}) collective-permute-start(f32[3,64,512]{2,1,0:T(8,128)S(1)} %collective-permute-done.8.two_ref), channel_id=1, source_target_pairs={{0,504},{8,0},{16,8},{24,16},{32,24},{40,32},{48,40},{56,48},{64,5... | collective-permute-start | bytes 1179656 | tf_op jit(solution)/shard_map/ppermute | solution.py:293
  96.7 2.8 %collective-permute-start.9 = (f32[7,24,512]{2,1,0:T(8,128)S(1)}, f32[7,24,512]{2,1,0:T(8,128)S(1)}, u32[]{:S(2)}, u32[]{:S(2)}) collective-permute-start(f32[7,24,512]{2,1,0:T(8,128)S(1)} %slice.17), channel_id=1, source_target_pairs={{0,8},{8,16},{16,24},{24,32},{32,40},{40,48},{48,56},{56,64},{64,7... | collective-permute-start | bytes 1032200 | tf_op jit(solution)/shard_map/ppermute | solution.py:295
  99.6 1.9 %collective-permute-done.11.rim_ref = f32[6,24,512]{2,1,0:T(8,128)S(1)} collective-permute-done((f32[6,24,512]{2,1,0:T(8,128)S(1)}, f32[6,24,512]{2,1,0:T(8,128)S(1)}, u32[]{:S(2)}, u32[]{:S(2)}) %collective-permute-start.11) | collective-permute-done | bytes 294944 | tf_op jit(solution)/shard_map/ppermute | solution.py:290
  101.4 3.1 %finish.3.rest_0_ = f32[16,64,512]{2,1,0:T(8,128)} custom-call(bf16[16,256,216]{2,1,0:T(8,128)(2,1)S(1)} %operator.1.op_ref, f32[9,64,512]{2,1,0:T(8,128)S(1)} %sweep.5.own_ref, f32[6,64,512]{2,1,0:T(8,128)S(1)} %sweep.7.one_ref, f32[6,64,512]{2,1,0:T(8,128)S(1)} %collective-permute-done.7.two_ref, f32[6,24,512]{2,1,0:T(8,128)S(1)} %collective-permute-done.11.rim_ref), custom_call_target="tpu_custom_call" | custom-call | flops 2000000000 | bytes 1 | tf_op jit(solution)/shard_map/finish/pallas_call | solution.py:226
  106.4 2.8 %collective-permute-done.9.rim_ref = f32[7,24,512]{2,1,0:T(8,128)S(1)} collective-permute-done((f32[7,24,512]{2,1,0:T(8,128)S(1)}, f32[7,24,512]{2,1,0:T(8,128)S(1)}, u32[]{:S(2)}, u32[]{:S(2)}) %collective-permute-start.9) | collective-permute-done | bytes 344096 | tf_op jit(solution)/shard_map/ppermute | solution.py:295
  109.2 3.7 %finish.5 = f32[16,64,512]{2,1,0:T(8,128)} custom-call(bf16[16,256,216]{2,1,0:T(8,128)(2,1)S(1)} %operator.1.op_ref, f32[7,128,512]{2,1,0:T(8,128)S(1)} %prepare.1.sum_ref, f32[7,64,512]{2,1,0:T(8,128)S(1)} %collective-permute-done.5.two_ref, f32[7,24,512]{2,1,0:T(8,128)S(1)} %collective-permute-done.9.rim_ref, ...), custom_call_target="tpu_custom_call", output_to_operand_aliasing={{}: (4, {})} | custom-call | flops 1 | bytes 1 | tf_op jit(solution)/shard_map/finish/pallas_call | solution.py:226
  (32 shorter events, 8.3 us)
Async XLA Ops:
  0.0 18.1 %copy-start.2 = (f32[16,8]{0,1:T(8,128)S(1)}, f32[16,8]{0,1:T(8,128)}, u32[]{:S(2)}) copy-start(f32[16,8]{0,1:T(8,128)} %param.11) | copy-start | bytes 1540
  0.0 18.2 %copy-start.3 = (s32[2,16]{1,0:T(2,128)S(1)}, s32[2,16]{1,0:T(2,128)}, u32[]{:S(2)}) copy-start(s32[2,16]{1,0:T(2,128)} %band_ref.8) | copy-start | bytes 388
  0.0 1.6 %copy-start = (f32[16,64,512]{2,1,0:T(8,128)S(1)}, f32[16,64,512]{2,1,0:T(8,128)}, u32[]{:S(2)}) copy-start(f32[16,64,512]{2,1,0:T(8,128)} %field_ref.5) | copy-start | bytes 6291460
  1.6 16.5 %copy-start.1 = (f32[16,64,512]{2,1,0:T(8,128)S(1)}, f32[16,64,512]{2,1,0:T(8,128)}, u32[]{:S(2)}) copy-start(f32[16,64,512]{2,1,0:T(8,128)} %field_ref.5) | copy-start | bytes 6291460
  1.7 33.5 %collective-permute-start.2 = (f32[6,64,512]{2,1,0:T(8,128)S(1)}, f32[6,64,512]{2,1,0:T(8,128)S(1)}, u32[]{:S(2)}, u32[]{:S(2)}) collective-permute-start(f32[6,64,512]{2,1,0:T(8,128)S(1)} %get-tuple-element.20), channel_id=1, source_target_pairs={{0,8},{8,16},{16,24},{24,32},{32,40},{40,48},{48,56},{56,64},{64,7... | collective-permute-start | bytes 2359304 | tf_op jit(solution)/shard_map/ppermute | solution.py:271
  6.2 12.0 %collective-permute-start = (f32[16,64,128]{2,1,0:T(8,128)S(1)}, f32[16,64,128]{2,1,0:T(8,128)S(1)}, u32[]{:S(2)}, u32[]{:S(2)}) collective-permute-start(f32[16,64,128]{2,1,0:T(8,128)S(1)} %get-tuple-element.19), channel_id=1, source_target_pairs={{0,1},{1,2},{2,3},{3,4},{4,5},{5,6},{6,7},{8,9},{9,10},{10,11},{11... | collective-permute-start | bytes 1572872 | tf_op jit(solution)/shard_map/ppermute | solution.py:273
  8.1 27.1 %collective-permute-start.3 = (f32[3,64,512]{2,1,0:T(8,128)S(1)}, f32[3,64,512]{2,1,0:T(8,128)S(1)}, u32[]{:S(2)}, u32[]{:S(2)}) collective-permute-start(f32[3,64,512]{2,1,0:T(8,128)S(1)} %get-tuple-element.21), channel_id=1, source_target_pairs={{0,48},{8,56},{16,0},{24,8},{32,16},{40,24},{48,32},{56,40},{64,11... | collective-permute-start | bytes 1179656 | tf_op jit(solution)/shard_map/ppermute | solution.py:272
  21.0 36.5 %collective-permute-start.1 = (f32[7,64,512]{2,1,0:T(8,128)S(1)}, f32[7,64,512]{2,1,0:T(8,128)S(1)}, u32[]{:S(2)}, u32[]{:S(2)}) collective-permute-start(f32[7,64,512]{2,1,0:T(8,128)S(1)} %sweep.4.own_ref), channel_id=1, source_target_pairs={{0,8},{8,16},{16,24},{24,32},{32,40},{40,48},{48,56},{56,64},{64,7... | collective-permute-start | bytes 2752520 | tf_op jit(solution)/shard_map/ppermute | solution.py:276
  35.3 8.0 %collective-permute-start.4 = (f32[9,64,128]{2,1,0:T(8,128)S(1)}, f32[9,64,128]{2,1,0:T(8,128)S(1)}, u32[]{:S(2)}, u32[]{:S(2)}) collective-permute-start(f32[9,64,128]{2,1,0:T(8,128)S(1)} %pad_maximum_fusion), channel_id=1, source_target_pairs={{0,1},{1,2},{2,3},{3,4},{4,5},{5,6},{6,7},{8,9},{9,10},{10,11},{11... | collective-permute-start | bytes 884744 | tf_op jit(solution)/shard_map/ppermute | solution.py:280
  44.9 14.5 %copy-start.4 = (f32[4,64,64]{2,1,0:T(8,128)S(1)}, f32[4,64,64]{2,1,0:T(8,128)}, u32[]{:S(2)}) copy-start(f32[4,64,64]{2,1,0:T(8,128)} %two_ref.1) | copy-start | bytes 196612
  44.9 14.5 %copy-start.5 = (f32[16,8]{0,1:T(8,128)S(1)}, f32[16,8]{0,1:T(8,128)}, u32[]{:S(2)}) copy-start(f32[16,8]{0,1:T(8,128)} %param.10) | copy-start | bytes 1540
  45.0 14.5 %copy-start.6 = (s32[64,3]{0,1:T(4,128)S(1)}, s32[64,3]{0,1:T(4,128)}, u32[]{:S(2)}) copy-start(s32[64,3]{0,1:T(4,128)} %param.12) | copy-start | bytes 2308
  45.0 14.5 %copy-start.7 = (s32[2,16]{1,0:T(2,128)S(1)}, s32[2,16]{1,0:T(2,128)}, u32[]{:S(2)}) copy-start(s32[2,16]{1,0:T(2,128)} %band_ref.9) | copy-start | bytes 388
  45.0 32.1 %collective-permute-start.6 = (f32[3,64,512]{2,1,0:T(8,128)S(1)}, f32[3,64,512]{2,1,0:T(8,128)S(1)}, u32[]{:S(2)}, u32[]{:S(2)}) collective-permute-start(f32[3,64,512]{2,1,0:T(8,128)S(1)} %sweep.6), channel_id=1, source_target_pairs={{48,24},{56,32},{0,40},{8,48},{16,56},{24,64},{32,72},{40,80},{112... | collective-permute-start | bytes 1179656 | tf_op jit(solution)/shard_map/ppermute | solution.py:282
  50.0 27.0 %collective-permute-start.7 = (f32[6,64,512]{2,1,0:T(8,128)S(1)}, f32[6,64,512]{2,1,0:T(8,128)S(1)}, u32[]{:S(2)}, u32[]{:S(2)}) collective-permute-start(f32[6,64,512]{2,1,0:T(8,128)S(1)} %sweep.7.one_ref), channel_id=1, source_target_pairs={{0,8},{8,16},{16,24},{24,32},{32,40},{40,48},{48,56},{56,64},{64,7... | collective-permute-start | bytes 2359304 | tf_op jit(solution)/shard_map/ppermute | solution.py:284
  57.5 39.2 %collective-permute-start.5 = (f32[7,64,512]{2,1,0:T(8,128)S(1)}, f32[7,64,512]{2,1,0:T(8,128)S(1)}, u32[]{:S(2)}, u32[]{:S(2)}) collective-permute-start(f32[7,64,512]{2,1,0:T(8,128)S(1)} %collective-permute-done.1.one_ref), channel_id=1, source_target_pairs={{0,8},{8,16},{16,24},{24,32},{32,40},{40,48},{48,56},{56,64},{64,7... | collective-permute-start | bytes 2752520 | tf_op jit(solution)/shard_map/ppermute | solution.py:286
  77.0 10.8 %collective-permute-start.8 = (f32[3,64,512]{2,1,0:T(8,128)S(1)}, f32[3,64,512]{2,1,0:T(8,128)S(1)}, u32[]{:S(2)}, u32[]{:S(2)}) collective-permute-start(f32[3,64,512]{2,1,0:T(8,128)S(1)} %collective-permute-done.6), channel_id=1, source_target_pairs={{0,504},{8,0},{16,8},{24,16},{32,24},{40,32},{48,40},{56,48},{64,5... | collective-permute-start | bytes 1179656 | tf_op jit(solution)/shard_map/ppermute | solution.py:292
  82.5 18.9 %collective-permute-start.11 = (f32[6,24,512]{2,1,0:T(8,128)S(1)}, f32[6,24,512]{2,1,0:T(8,128)S(1)}, u32[]{:S(2)}, u32[]{:S(2)}) collective-permute-start(f32[6,24,512]{2,1,0:T(8,128)S(1)} %slice.19), channel_id=1, source_target_pairs={{0,8},{8,16},{16,24},{24,32},{32,40},{40,48},{48,56},{56,64},{64,7... | collective-permute-start | bytes 884744 | tf_op jit(solution)/shard_map/ppermute | solution.py:290
  87.8 16.7 %collective-permute-start.10 = (f32[3,64,512]{2,1,0:T(8,128)S(1)}, f32[3,64,512]{2,1,0:T(8,128)S(1)}, u32[]{:S(2)}, u32[]{:S(2)}) collective-permute-start(f32[3,64,512]{2,1,0:T(8,128)S(1)} %collective-permute-done.8.two_ref), channel_id=1, source_target_pairs={{0,504},{8,0},{16,8},{24,16},{32,24},{40,32},{48,40},{56,48},{64,5... | collective-permute-start | bytes 1179656 | tf_op jit(solution)/shard_map/ppermute | solution.py:293
  96.7 12.5 %collective-permute-start.9 = (f32[7,24,512]{2,1,0:T(8,128)S(1)}, f32[7,24,512]{2,1,0:T(8,128)S(1)}, u32[]{:S(2)}, u32[]{:S(2)}) collective-permute-start(f32[7,24,512]{2,1,0:T(8,128)S(1)} %slice.17), channel_id=1, source_target_pairs={{0,8},{8,16},{16,24},{24,32},{32,40},{40,48},{48,56},{56,64},{64,7... | collective-permute-start | bytes 1032200 | tf_op jit(solution)/shard_map/ppermute | solution.py:295

commit v11 on v10

--- a/solution.py
+++ b/solution.py
@@ -203,8 +203,19 @@
 
 def complete_kernel(op_ref, sum_ref, two_ref, rim_ref, *rest):
     out_ref, high_ref, low_ref = rest[-3:]
-    columns = slice(2 * two_ref.shape[1], op_ref.shape[2])
-    out_ref[0] = update(sum_ref[0] + product(op_ref, columns, (two_ref, rim_ref), high_ref, low_ref))
+    rows = two_ref.shape[1]
+    columns = slice(2 * rows, op_ref.shape[2])
+    at = 0
+    for ref in (two_ref, rim_ref):
+        high, low = split(ref[0])
+        high_ref[at : at + ref.shape[1]] = high
+        low_ref[at : at + ref.shape[1]] = low
+        at += ref.shape[1]
+    dot = functools.partial(jnp.dot, preferred_element_type=jnp.float32)
+    op_high, op_low = op_ref[0, :rows, columns], op_ref[0, 2 * rows : 3 * rows, columns]
+    late = dot(op_high, high_ref[:at]) + dot(op_low, high_ref[:at]) + dot(op_high, low_ref[:at])
+    rate, spread = sum_ref[0, :rows] + late, sum_ref[0, rows:]
+    out_ref[0] = spread + BETA * (rate * rate / (1.0 + rate) - spread * rate)
 
 
 def finish(operator, held, two, rim, part, total, before, held_first, flops):

time: 114 us -> 113 us (level)
  no operation moved by 1% of the time
where the time goes in v11:
time: 113 us
  starting transfers between devices  51.6 us (46%)
  waiting for transfers between devices  32.3 us (29%)
  Pallas kernels  26.7 us (24%)
  local copies, waits for them, and re-layouts  1.75 us (2%)
    pallas_call x4, Pallas kernels, sweep(): pl.pallas_call(functools.partial(sweep_kernel, lo), grid_spec=pltpu.Prefe...  10.2 us
    ppermute x1, starting transfers between devices, shards(): back_away_raw = back_first(back)  10 us
    ppermute x1, waiting for transfers between devices, shards(): early_two = hop(early_one)  9.62 us
    pallas_call x3, Pallas kernels, finish(): pl.pallas_call(finish_kernel if len(held) == 2 else complete_kernel, grid...  8.45 us
    ppermute x1, waiting for transfers between devices, shards(): back_away_raw = back_first(back)  8.07 us
    ppermute x1, starting transfers between devices, shards(): back_one = unhop(back_two)  7.7 us
    ppermute x1, starting transfers between devices, shards(): early_two = hop(early_one)  7.45 us
    pallas_call x1, Pallas kernels, length_operator(): pl.pallas_call(operator_kernel, grid_spec=pltpu.PrefetchScalarGridSpec(nu...  6.12 us
  transfers between devices with their start and end apart: 12, of which 7 were waited for; matrix products, arithmetic and copies ran while one was open for 0% of the time, Pallas kernels for 20%

profile of v11, /device:TPU:2, one launch (start us, length us, event | category | flops | bytes accessed | tf_op | source)
XLA Modules:
  0.0 112.7 jit_solution(6729855542211835550)
XLA Ops:
  1.7 4.4 %collective-permute-start.2 = (f32[6,64,512]{2,1,0:T(8,128)S(1)}, f32[6,64,512]{2,1,0:T(8,128)S(1)}, u32[]{:S(2)}, u32[]{:S(2)}) collective-permute-start(f32[6,64,512]{2,1,0:T(8,128)S(1)} %get-tuple-element.20), channel_id=1, source_target_pairs={{0,8},{8,16},{16,24},{24,32},{32,40},{40,48},{48,56},{56,64},{64,7... | collective-permute-start | bytes 2359304 | tf_op jit(solution)/shard_map/ppermute | solution.py:282
  6.2 1.9 %collective-permute-start = (f32[16,64,128]{2,1,0:T(8,128)S(1)}, f32[16,64,128]{2,1,0:T(8,128)S(1)}, u32[]{:S(2)}, u32[]{:S(2)}) collective-permute-start(f32[16,64,128]{2,1,0:T(8,128)S(1)} %get-tuple-element.19), channel_id=1, source_target_pairs={{0,1},{1,2},{2,3},{3,4},{4,5},{5,6},{6,7},{8,9},{9,10},{10,11},{11... | collective-permute-start | bytes 1572872 | tf_op jit(solution)/shard_map/ppermute | solution.py:284
  8.1 10.0 %collective-permute-start.3 = (f32[3,64,512]{2,1,0:T(8,128)S(1)}, f32[3,64,512]{2,1,0:T(8,128)S(1)}, u32[]{:S(2)}, u32[]{:S(2)}) collective-permute-start(f32[3,64,512]{2,1,0:T(8,128)S(1)} %get-tuple-element.21), channel_id=1, source_target_pairs={{0,48},{8,56},{16,0},{24,8},{32,16},{40,24},{48,32},{56,40},{64,11... | collective-permute-start | bytes 1179656 | tf_op jit(solution)/shard_map/ppermute | solution.py:283
  18.2 2.8 %sweep.4.own_ref = f32[7,64,512]{2,1,0:T(8,128)S(1)} custom-call(s32[2,16]{1,0:T(2,128)S(1)} %copy-done.3, f32[8,16]{1,0:T(8,128)S(1)} %bitcast.4, f32[16,64,512]{2,1,0:T(8,128)S(1)} %copy-done.1, f32[16,64,128]{2,1,0:T(8,128)S(1)} %collective-permute-done.edge_ref), custom_call_target="tpu_custom_call" | custom-call | flops 1 | bytes 1 | tf_op jit(solution)/shard_map/sweep/pallas_call | solution.py:61
  21.0 2.8 %collective-permute-start.1 = (f32[7,64,512]{2,1,0:T(8,128)S(1)}, f32[7,64,512]{2,1,0:T(8,128)S(1)}, u32[]{:S(2)}, u32[]{:S(2)}) collective-permute-start(f32[7,64,512]{2,1,0:T(8,128)S(1)} %sweep.4.own_ref), channel_id=1, source_target_pairs={{0,8},{8,16},{16,24},{24,32},{32,40},{40,48},{48,56},{56,64},{64,7... | collective-permute-start | bytes 2752520 | tf_op jit(solution)/shard_map/ppermute | solution.py:287
  23.8 3.4 %sweep.5.own_ref = f32[9,64,512]{2,1,0:T(8,128)S(1)} custom-call(s32[2,16]{1,0:T(2,128)S(1)} %copy-done.3, f32[8,16]{1,0:T(8,128)S(1)} %bitcast.5, f32[16,64,512]{2,1,0:T(8,128)S(1)} %copy-done.1, f32[16,64,128]{2,1,0:T(8,128)S(1)} %collective-permute-done.edge_ref), custom_call_target="tpu_custom_call" | custom-call | flops 1 | bytes 1 | tf_op jit(solution)/shard_map/sweep/pallas_call | solution.py:61
  27.2 8.1 %collective-permute-done.3.field_ref = f32[3,64,512]{2,1,0:T(8,128)S(1)} collective-permute-done((f32[3,64,512]{2,1,0:T(8,128)S(1)}, f32[3,64,512]{2,1,0:T(8,128)S(1)}, u32[]{:S(2)}, u32[]{:S(2)}) %collective-permute-start.3) | collective-permute-done | bytes 393248 | tf_op jit(solution)/shard_map/ppermute | solution.py:283
  35.3 2.6 %collective-permute-start.4 = (f32[9,64,128]{2,1,0:T(8,128)S(1)}, f32[9,64,128]{2,1,0:T(8,128)S(1)}, u32[]{:S(2)}, u32[]{:S(2)}) collective-permute-start(f32[9,64,128]{2,1,0:T(8,128)S(1)} %pad_maximum_fusion), channel_id=1, source_target_pairs={{0,1},{1,2},{2,3},{3,4},{4,5},{5,6},{6,7},{8,9},{9,10},{10,11},{11... | collective-permute-start | bytes 884744 | tf_op jit(solution)/shard_map/ppermute | solution.py:291
  37.9 5.4 %collective-permute-done.4.edge_ref = f32[9,64,128]{2,1,0:T(8,128)S(1)} collective-permute-done((f32[9,64,128]{2,1,0:T(8,128)S(1)}, f32[9,64,128]{2,1,0:T(8,128)S(1)}, u32[]{:S(2)}, u32[]{:S(2)}) %collective-permute-start.4) | collective-permute-done | bytes 294944 | tf_op jit(solution)/shard_map/ppermute | solution.py:291
  45.0 2.6 %collective-permute-start.6 = (f32[3,64,512]{2,1,0:T(8,128)S(1)}, f32[3,64,512]{2,1,0:T(8,128)S(1)}, u32[]{:S(2)}, u32[]{:S(2)}) collective-permute-start(f32[3,64,512]{2,1,0:T(8,128)S(1)} %sweep.6), channel_id=1, source_target_pairs={{48,24},{56,32},{0,40},{8,48},{16,56},{24,64},{32,72},{40,80},{112... | collective-permute-start | bytes 1179656 | tf_op jit(solution)/shard_map/ppermute | solution.py:293
  47.5 2.5 %sweep.7.one_ref = f32[6,64,512]{2,1,0:T(8,128)S(1)} custom-call(s32[2,16]{1,0:T(2,128)S(1)} %copy-done.3, f32[8,16]{1,0:T(8,128)S(1)} %bitcast.7, f32[6,64,512]{2,1,0:T(8,128)S(1)} %collective-permute-done.2.field_ref, f32[9,64,128]{2,1,0:T(8,128)S(1)} %collective-permute-done.4.edge_ref), custom_call_target="tpu_custom_call" | custom-call | flops 4000000000 | bytes 1 | tf_op jit(solution)/shard_map/sweep/pallas_call | solution.py:61
  50.0 7.4 %collective-permute-start.7 = (f32[6,64,512]{2,1,0:T(8,128)S(1)}, f32[6,64,512]{2,1,0:T(8,128)S(1)}, u32[]{:S(2)}, u32[]{:S(2)}) collective-permute-start(f32[6,64,512]{2,1,0:T(8,128)S(1)} %sweep.7.one_ref), channel_id=1, source_target_pairs={{0,8},{8,16},{16,24},{24,32},{32,40},{40,48},{48,56},{56,64},{64,7... | collective-permute-start | bytes 2359304 | tf_op jit(solution)/shard_map/ppermute | solution.py:295
  57.5 1.9 %collective-permute-start.5 = (f32[7,64,512]{2,1,0:T(8,128)S(1)}, f32[7,64,512]{2,1,0:T(8,128)S(1)}, u32[]{:S(2)}, u32[]{:S(2)}) collective-permute-start(f32[7,64,512]{2,1,0:T(8,128)S(1)} %collective-permute-done.1.one_ref), channel_id=1, source_target_pairs={{0,8},{8,16},{16,24},{24,32},{32,40},{40,48},{48,56},{56,64},{64,7... | collective-permute-start | bytes 2752520 | tf_op jit(solution)/shard_map/ppermute | solution.py:297
  59.5 6.1 %operator.1.op_ref = bf16[16,256,216]{2,1,0:T(8,128)(2,1)S(1)} custom-call(s32[1]{0:T(128)} %bitcast.me_ref, s32[3,64]{1,0:T(4,128)S(1)} %bitcast.9, s32[2,16]{1,0:T(2,128)S(1)} %copy-done.7, f32[8,16]{1,0:T(8,128)S(1)} %bitcast.8, f32[4,64,64]{2,1,0:T(8,128)S(1)} %copy-done.4, f32[4,64,64]{2,1,0:T(8,128)S(1)} %copy-done.4, f32[4,64,64]{2,1,0:T(8,128)S(1)} %copy-done.4), custom_call_target="tpu_custom_call" | custom-call | flops 10000000000 | bytes 1 | tf_op jit(solution)/shard_map/operator/pallas_call | solution.py:138
  67.4 9.6 %collective-permute-done.7.two_ref = f32[6,64,512]{2,1,0:T(8,128)S(1)} collective-permute-done((f32[6,64,512]{2,1,0:T(8,128)S(1)}, f32[6,64,512]{2,1,0:T(8,128)S(1)}, u32[]{:S(2)}, u32[]{:S(2)}) %collective-permute-start.7) | collective-permute-done | bytes 786464 | tf_op jit(solution)/shard_map/ppermute | solution.py:295
  77.0 5.5 %collective-permute-start.8 = (f32[3,64,512]{2,1,0:T(8,128)S(1)}, f32[3,64,512]{2,1,0:T(8,128)S(1)}, u32[]{:S(2)}, u32[]{:S(2)}) collective-permute-start(f32[3,64,512]{2,1,0:T(8,128)S(1)} %collective-permute-done.6), channel_id=1, source_target_pairs={{0,504},{8,0},{16,8},{24,16},{32,24},{40,32},{48,40},{56,48},{64,5... | collective-permute-start | bytes 1179656 | tf_op jit(solution)/shard_map/ppermute | solution.py:303
  82.5 1.9 %collective-permute-start.11 = (f32[6,24,512]{2,1,0:T(8,128)S(1)}, f32[6,24,512]{2,1,0:T(8,128)S(1)}, u32[]{:S(2)}, u32[]{:S(2)}) collective-permute-start(f32[6,24,512]{2,1,0:T(8,128)S(1)} %slice.19), channel_id=1, source_target_pairs={{0,8},{8,16},{16,24},{24,32},{32,40},{40,48},{48,56},{56,64},{64,7... | collective-permute-start | bytes 884744 | tf_op jit(solution)/shard_map/ppermute | solution.py:301
  84.5 3.3 %collective-permute-done.8.two_ref = f32[3,64,512]{2,1,0:T(8,128)S(1)} collective-permute-done((f32[3,64,512]{2,1,0:T(8,128)S(1)}, f32[3,64,512]{2,1,0:T(8,128)S(1)}, u32[]{:S(2)}, u32[]{:S(2)}) %collective-permute-start.8) | collective-permute-done | bytes 393248 | tf_op jit(solution)/shard_map/ppermute | solution.py:303
  87.8 7.7 %collective-permute-start.10 = (f32[3,64,512]{2,1,0:T(8,128)S(1)}, f32[3,64,512]{2,1,0:T(8,128)S(1)}, u32[]{:S(2)}, u32[]{:S(2)}) collective-permute-start(f32[3,64,512]{2,1,0:T(8,128)S(1)} %collective-permute-done.8.two_ref), channel_id=1, source_target_pairs={{0,504},{8,0},{16,8},{24,16},{32,24},{40,32},{48,40},{56,48},{64,5... | collective-permute-start | bytes 1179656 | tf_op jit(solution)/shard_map/ppermute | solution.py:304
  96.7 2.8 %collective-permute-start.9 = (f32[7,24,512]{2,1,0:T(8,128)S(1)}, f32[7,24,512]{2,1,0:T(8,128)S(1)}, u32[]{:S(2)}, u32[]{:S(2)}) collective-permute-start(f32[7,24,512]{2,1,0:T(8,128)S(1)} %slice.17), channel_id=1, source_target_pairs={{0,8},{8,16},{16,24},{24,32},{32,40},{40,48},{48,56},{56,64},{64,7... | collective-permute-start | bytes 1032200 | tf_op jit(solution)/shard_map/ppermute | solution.py:306
  99.6 1.9 %collective-permute-done.11.rim_ref = f32[6,24,512]{2,1,0:T(8,128)S(1)} collective-permute-done((f32[6,24,512]{2,1,0:T(8,128)S(1)}, f32[6,24,512]{2,1,0:T(8,128)S(1)}, u32[]{:S(2)}, u32[]{:S(2)}) %collective-permute-start.11) | collective-permute-done | bytes 294944 | tf_op jit(solution)/shard_map/ppermute | solution.py:301
  101.4 3.1 %finish.3.rest_0_ = f32[16,64,512]{2,1,0:T(8,128)} custom-call(bf16[16,256,216]{2,1,0:T(8,128)(2,1)S(1)} %operator.1.op_ref, f32[9,64,512]{2,1,0:T(8,128)S(1)} %sweep.5.own_ref, f32[6,64,512]{2,1,0:T(8,128)S(1)} %sweep.7.one_ref, f32[6,64,512]{2,1,0:T(8,128)S(1)} %collective-permute-done.7.two_ref, f32[6,24,512]{2,1,0:T(8,128)S(1)} %collective-permute-done.11.rim_ref), custom_call_target="tpu_custom_call" | custom-call | flops 2000000000 | bytes 1 | tf_op jit(solution)/shard_map/finish/pallas_call | solution.py:237
  106.4 2.8 %collective-permute-done.9.rim_ref = f32[7,24,512]{2,1,0:T(8,128)S(1)} collective-permute-done((f32[7,24,512]{2,1,0:T(8,128)S(1)}, f32[7,24,512]{2,1,0:T(8,128)S(1)}, u32[]{:S(2)}, u32[]{:S(2)}) %collective-permute-start.9) | collective-permute-done | bytes 344096 | tf_op jit(solution)/shard_map/ppermute | solution.py:306
  109.2 3.5 %finish.5 = f32[16,64,512]{2,1,0:T(8,128)} custom-call(bf16[16,256,216]{2,1,0:T(8,128)(2,1)S(1)} %operator.1.op_ref, f32[7,128,512]{2,1,0:T(8,128)S(1)} %prepare.1.sum_ref, f32[7,64,512]{2,1,0:T(8,128)S(1)} %collective-permute-done.5.two_ref, f32[7,24,512]{2,1,0:T(8,128)S(1)} %collective-permute-done.9.rim_ref, ...), custom_call_target="tpu_custom_call", output_to_operand_aliasing={{}: (4, {})} | custom-call | flops 1 | bytes 1 | tf_op jit(solution)/shard_map/finish/pallas_call | solution.py:237
  (32 shorter events, 8.3 us)
Async XLA Ops:
  0.0 18.1 %copy-start.2 = (f32[16,8]{0,1:T(8,128)S(1)}, f32[16,8]{0,1:T(8,128)}, u32[]{:S(2)}) copy-start(f32[16,8]{0,1:T(8,128)} %param.11) | copy-start | bytes 1540
  0.0 18.2 %copy-start.3 = (s32[2,16]{1,0:T(2,128)S(1)}, s32[2,16]{1,0:T(2,128)}, u32[]{:S(2)}) copy-start(s32[2,16]{1,0:T(2,128)} %band_ref.8) | copy-start | bytes 388
  0.0 1.6 %copy-start = (f32[16,64,512]{2,1,0:T(8,128)S(1)}, f32[16,64,512]{2,1,0:T(8,128)}, u32[]{:S(2)}) copy-start(f32[16,64,512]{2,1,0:T(8,128)} %field_ref.5) | copy-start | bytes 6291460
  1.6 16.5 %copy-start.1 = (f32[16,64,512]{2,1,0:T(8,128)S(1)}, f32[16,64,512]{2,1,0:T(8,128)}, u32[]{:S(2)}) copy-start(f32[16,64,512]{2,1,0:T(8,128)} %field_ref.5) | copy-start | bytes 6291460
  1.7 33.5 %collective-permute-start.2 = (f32[6,64,512]{2,1,0:T(8,128)S(1)}, f32[6,64,512]{2,1,0:T(8,128)S(1)}, u32[]{:S(2)}, u32[]{:S(2)}) collective-permute-start(f32[6,64,512]{2,1,0:T(8,128)S(1)} %get-tuple-element.20), channel_id=1, source_target_pairs={{0,8},{8,16},{16,24},{24,32},{32,40},{40,48},{48,56},{56,64},{64,7... | collective-permute-start | bytes 2359304 | tf_op jit(solution)/shard_map/ppermute | solution.py:282
  6.2 12.0 %collective-permute-start = (f32[16,64,128]{2,1,0:T(8,128)S(1)}, f32[16,64,128]{2,1,0:T(8,128)S(1)}, u32[]{:S(2)}, u32[]{:S(2)}) collective-permute-start(f32[16,64,128]{2,1,0:T(8,128)S(1)} %get-tuple-element.19), channel_id=1, source_target_pairs={{0,1},{1,2},{2,3},{3,4},{4,5},{5,6},{6,7},{8,9},{9,10},{10,11},{11... | collective-permute-start | bytes 1572872 | tf_op jit(solution)/shard_map/ppermute | solution.py:284
  8.1 27.1 %collective-permute-start.3 = (f32[3,64,512]{2,1,0:T(8,128)S(1)}, f32[3,64,512]{2,1,0:T(8,128)S(1)}, u32[]{:S(2)}, u32[]{:S(2)}) collective-permute-start(f32[3,64,512]{2,1,0:T(8,128)S(1)} %get-tuple-element.21), channel_id=1, source_target_pairs={{0,48},{8,56},{16,0},{24,8},{32,16},{40,24},{48,32},{56,40},{64,11... | collective-permute-start | bytes 1179656 | tf_op jit(solution)/shard_map/ppermute | solution.py:283
  21.0 36.5 %collective-permute-start.1 = (f32[7,64,512]{2,1,0:T(8,128)S(1)}, f32[7,64,512]{2,1,0:T(8,128)S(1)}, u32[]{:S(2)}, u32[]{:S(2)}) collective-permute-start(f32[7,64,512]{2,1,0:T(8,128)S(1)} %sweep.4.own_ref), channel_id=1, source_target_pairs={{0,8},{8,16},{16,24},{24,32},{32,40},{40,48},{48,56},{56,64},{64,7... | collective-permute-start | bytes 2752520 | tf_op jit(solution)/shard_map/ppermute | solution.py:287
  35.3 8.0 %collective-permute-start.4 = (f32[9,64,128]{2,1,0:T(8,128)S(1)}, f32[9,64,128]{2,1,0:T(8,128)S(1)}, u32[]{:S(2)}, u32[]{:S(2)}) collective-permute-start(f32[9,64,128]{2,1,0:T(8,128)S(1)} %pad_maximum_fusion), channel_id=1, source_target_pairs={{0,1},{1,2},{2,3},{3,4},{4,5},{5,6},{6,7},{8,9},{9,10},{10,11},{11... | collective-permute-start | bytes 884744 | tf_op jit(solution)/shard_map/ppermute | solution.py:291
  44.9 14.5 %copy-start.4 = (f32[4,64,64]{2,1,0:T(8,128)S(1)}, f32[4,64,64]{2,1,0:T(8,128)}, u32[]{:S(2)}) copy-start(f32[4,64,64]{2,1,0:T(8,128)} %two_ref.1) | copy-start | bytes 196612
  44.9 14.5 %copy-start.5 = (f32[16,8]{0,1:T(8,128)S(1)}, f32[16,8]{0,1:T(8,128)}, u32[]{:S(2)}) copy-start(f32[16,8]{0,1:T(8,128)} %param.10) | copy-start | bytes 1540
  45.0 14.5 %copy-start.6 = (s32[64,3]{0,1:T(4,128)S(1)}, s32[64,3]{0,1:T(4,128)}, u32[]{:S(2)}) copy-start(s32[64,3]{0,1:T(4,128)} %param.12) | copy-start | bytes 2308
  45.0 14.5 %copy-start.7 = (s32[2,16]{1,0:T(2,128)S(1)}, s32[2,16]{1,0:T(2,128)}, u32[]{:S(2)}) copy-start(s32[2,16]{1,0:T(2,128)} %band_ref.9) | copy-start | bytes 388
  45.0 32.1 %collective-permute-start.6 = (f32[3,64,512]{2,1,0:T(8,128)S(1)}, f32[3,64,512]{2,1,0:T(8,128)S(1)}, u32[]{:S(2)}, u32[]{:S(2)}) collective-permute-start(f32[3,64,512]{2,1,0:T(8,128)S(1)} %sweep.6), channel_id=1, source_target_pairs={{48,24},{56,32},{0,40},{8,48},{16,56},{24,64},{32,72},{40,80},{112... | collective-permute-start | bytes 1179656 | tf_op jit(solution)/shard_map/ppermute | solution.py:293
  50.0 27.0 %collective-permute-start.7 = (f32[6,64,512]{2,1,0:T(8,128)S(1)}, f32[6,64,512]{2,1,0:T(8,128)S(1)}, u32[]{:S(2)}, u32[]{:S(2)}) collective-permute-start(f32[6,64,512]{2,1,0:T(8,128)S(1)} %sweep.7.one_ref), channel_id=1, source_target_pairs={{0,8},{8,16},{16,24},{24,32},{32,40},{40,48},{48,56},{56,64},{64,7... | collective-permute-start | bytes 2359304 | tf_op jit(solution)/shard_map/ppermute | solution.py:295
  57.5 39.2 %collective-permute-start.5 = (f32[7,64,512]{2,1,0:T(8,128)S(1)}, f32[7,64,512]{2,1,0:T(8,128)S(1)}, u32[]{:S(2)}, u32[]{:S(2)}) collective-permute-start(f32[7,64,512]{2,1,0:T(8,128)S(1)} %collective-permute-done.1.one_ref), channel_id=1, source_target_pairs={{0,8},{8,16},{16,24},{24,32},{32,40},{40,48},{48,56},{56,64},{64,7... | collective-permute-start | bytes 2752520 | tf_op jit(solution)/shard_map/ppermute | solution.py:297
  77.0 10.8 %collective-permute-start.8 = (f32[3,64,512]{2,1,0:T(8,128)S(1)}, f32[3,64,512]{2,1,0:T(8,128)S(1)}, u32[]{:S(2)}, u32[]{:S(2)}) collective-permute-start(f32[3,64,512]{2,1,0:T(8,128)S(1)} %collective-permute-done.6), channel_id=1, source_target_pairs={{0,504},{8,0},{16,8},{24,16},{32,24},{40,32},{48,40},{56,48},{64,5... | collective-permute-start | bytes 1179656 | tf_op jit(solution)/shard_map/ppermute | solution.py:303
  82.5 18.9 %collective-permute-start.11 = (f32[6,24,512]{2,1,0:T(8,128)S(1)}, f32[6,24,512]{2,1,0:T(8,128)S(1)}, u32[]{:S(2)}, u32[]{:S(2)}) collective-permute-start(f32[6,24,512]{2,1,0:T(8,128)S(1)} %slice.19), channel_id=1, source_target_pairs={{0,8},{8,16},{16,24},{24,32},{32,40},{40,48},{48,56},{56,64},{64,7... | collective-permute-start | bytes 884744 | tf_op jit(solution)/shard_map/ppermute | solution.py:301
  87.8 16.7 %collective-permute-start.10 = (f32[3,64,512]{2,1,0:T(8,128)S(1)}, f32[3,64,512]{2,1,0:T(8,128)S(1)}, u32[]{:S(2)}, u32[]{:S(2)}) collective-permute-start(f32[3,64,512]{2,1,0:T(8,128)S(1)} %collective-permute-done.8.two_ref), channel_id=1, source_target_pairs={{0,504},{8,0},{16,8},{24,16},{32,24},{40,32},{48,40},{56,48},{64,5... | collective-permute-start | bytes 1179656 | tf_op jit(solution)/shard_map/ppermute | solution.py:304
  96.7 12.5 %collective-permute-start.9 = (f32[7,24,512]{2,1,0:T(8,128)S(1)}, f32[7,24,512]{2,1,0:T(8,128)S(1)}, u32[]{:S(2)}, u32[]{:S(2)}) collective-permute-start(f32[7,24,512]{2,1,0:T(8,128)S(1)} %slice.17), channel_id=1, source_target_pairs={{0,8},{8,16},{16,24},{24,32},{32,40},{40,48},{48,56},{56,64},{64,7... | collective-permute-start | bytes 1032200 | tf_op jit(solution)/shard_map/ppermute | solution.py:306
